TPU v7x, 256 devices: a whole 4x4x8 slice. The times are simulated.
256 devices in a mesh: ens: 8 (over y, z_hi), lat: 8 (over z_lo, core), lon: 4 (over x).
Axes of the slice: x: 4, y: 4, z: 8 (z_hi: 2, z_lo: 4; z = z_hi * 4 + z_lo), core: 2. Of those that a mesh axis runs over, the one named last changes fastest.
Arguments:
- perturbation: float32 [8, 16, 128, 1024], P('ens', None, 'lat', 'lon'), may hold values from -6 to 6
- seed_ids: int32 [8], P('ens'), may hold values from 0 to 15
- amp_table: float32 [16, 16], replicated, may hold values from 0.5 to 2
- start_state: float32 [16, 128, 1024], P('ens', 'lat', 'lon'), may hold values from -2.5 to 2.5
- speeds: bfloat16 [4, 2, 16, 128, 1024], P(None, None, None, 'lat', 'lon'), may hold values from 0.039794922 to 0.29882812
- upwind: int32 [4, 16, 128, 1024], P(None, None, 'lat', 'lon'), may hold values from 0 to 3
- viscosity: float32 [16], replicated, may hold values from 0.02 to 0.08
- reaction: float32 [16], replicated, may hold values from 0.02 to 0.1
Outputs:
- final_perturbation: float32 [8, 16, 128, 1024], P('ens', None, 'lat', 'lon')
- final_state: float32 [16, 128, 1024], P('ens', 'lat', 'lon')
Inputs may be any that keep to these rules, and one draw needn't show every extreme that they name: `upwind`: value mod 2 is 1 where the zonal wind blows eastward, floor of value / 2 is 1 where the meridional wind blows toward higher rows. `seed_ids`: A row index of amp_table.
All inputs are finite; a program needn't handle non-finite values.
Results may differ from a plain program's by a relative error of at most 0.0003.
Values sent between devices are 32-bit elements; how exact they have to be, the bound alone decides.
No kernel may reach another device: no remote copies, remote signals or barrier semaphores. Data moves between devices by JAX's collectives and lax.ppermute only.
A program may use at most 64 MiB of HBM per device.

v0:
```python
import jax
import jax.numpy as jnp
from jax import lax
from jax.sharding import PartitionSpec as P

STEPS = 4


def extended(block, sides, width, periodic):
    for axis, dim in sides:
        count = lax.axis_size(axis)
        forward = [(i, i + 1) for i in range(count - 1)]
        if periodic:
            forward.append((count - 1, 0))
        backward = [(target, source) for source, target in forward]
        low = lax.ppermute(
            lax.slice_in_dim(block, block.shape[dim] - width, None, axis=dim), axis, forward
        )
        high = lax.ppermute(lax.slice_in_dim(block, 0, width, axis=dim), axis, backward)
        block = jnp.concatenate([low, block, high], axis=dim)
    return block


def stencil(current, below, above, western, eastern, speed_lon, speed_lat, direction, viscous):
    lon_side = jnp.where(direction % 2 == 1, western, eastern)
    lat_side = jnp.where(direction // 2 == 1, below, above)
    spread = western + eastern + below + above - 4.0 * current
    return (
        current
        - speed_lon * (current - lon_side)
        - speed_lat * (current - lat_side)
        + viscous * spread
    )


def state_step(current, speed_part, direction, viscous, rates):
    rows = extended(current, (("lat", 1),), 1, False)
    columns = extended(current, (("lon", 2),), 1, True)
    moved = stencil(
        current,
        rows[:, :-2, :],
        rows[:, 2:, :],
        columns[:, :, :-2],
        columns[:, :, 2:],
        speed_part[0].astype(jnp.float32),
        speed_part[1].astype(jnp.float32),
        direction,
        viscous,
    )
    return moved - rates * current * current * current


def member_step(delta, past, speed_part, direction, viscous, rates):
    rows = extended(delta, (("lat", 2),), 1, False)
    columns = extended(delta, (("lon", 3),), 1, True)
    moved = stencil(
        delta,
        rows[:, :, :-2, :],
        rows[:, :, 2:, :],
        columns[:, :, :, :-2],
        columns[:, :, :, 2:],
        speed_part[0].astype(jnp.float32),
        speed_part[1].astype(jnp.float32),
        direction,
        viscous,
    )
    return moved - 3.0 * rates * past * past * delta


def per_device(perturbation, seed_ids, amp_table, start_state, speeds, upwind, viscosity, reaction):
    bank_rows = amp_table.shape[0]
    onehot = (seed_ids[:, None] == jnp.arange(bank_rows, dtype=jnp.int32)[None, :]).astype(
        jnp.float32
    )
    amplitudes = jnp.dot(onehot, amp_table, precision=lax.Precision.HIGHEST)
    delta = perturbation * amplitudes[:, :, None, None]
    viscous_all = viscosity[:, None, None]
    rates_all = reaction[:, None, None]
    own_levels = start_state.shape[0]
    first_level = lax.axis_index("ens") * own_levels
    speeds_own = lax.dynamic_slice_in_dim(speeds, first_level, own_levels, 2)
    upwind_own = lax.dynamic_slice_in_dim(upwind, first_level, own_levels, 1)
    viscous_own = lax.dynamic_slice_in_dim(viscosity, first_level, own_levels, 0)[:, None, None]
    rates_own = lax.dynamic_slice_in_dim(reaction, first_level, own_levels, 0)[:, None, None]
    current = start_state
    for step_index in range(STEPS):
        past = lax.all_gather(current, "ens", axis=0, tiled=True)
        delta = member_step(
            delta, past, speeds[step_index], upwind[step_index], viscous_all, rates_all
        )
        current = state_step(
            current, speeds_own[step_index], upwind_own[step_index], viscous_own, rates_own
        )
    return (delta, current)


def solution(mesh):
    return jax.shard_map(
        per_device,
        mesh=mesh,
        in_specs=(
            P("ens", None, "lat", "lon"),
            P("ens"),
            P(),
            P("ens", "lat", "lon"),
            P(None, None, None, "lat", "lon"),
            P(None, None, "lat", "lon"),
            P(),
            P(),
        ),
        out_specs=(P("ens", None, "lat", "lon"), P("ens", "lat", "lon")),
        check_vma=False,
    )
```

profile of v0, /device:TPU:1, one launch (start us, length us, event | category | flops | bytes accessed | tf_op | source)
XLA Modules:
  0.0 271.5 jit_solution(9284665718085572266)
XLA Ops:
  1.4 0.1 convolution_bitcast_fusion
  1.5 1.1 broadcast_multiply_fusion
  2.6 5.1 %collective-permute-start.2 = (f32[1,16,1,256]{3,2,1,0:T(1,128)S(1)}, f32[1,16,1,256]{3,2,1,0:T(1,128)S(1)}, u32[]{:S(2)}, u32[]{:S(2)}) collective-permute-start(f32[1,16,1,256]{3,2,1,0:T(1,128)S(1)} %get-tuple-element.17), channel_id=1, source_target_pairs={{0,4},{4,8},{8,12},{12,16},{16,20},{20,24},{24,28},{1,5},{5,9},{9,... | collective-permute-start | bytes 49160 | tf_op jit(solution)/shard_map/ppermute | solution.py:16
  7.7 0.7 fusion.91
  8.4 1.9 collective-permute-start.10
  10.4 2.4 collective-permute-start.11
  12.8 0.8 fusion.90
  13.6 1.2 collective-permute-start.8
  14.8 1.5 collective-permute-start.9
  16.4 39.8 %all_gather.12 = f32[16,16,256]{2,1,0:T(8,128)S(1)} all-gather(f32[2,16,256]{2,1,0:T(8,128)S(1)} %copy-done.3), channel_id=1, replica_groups=mesh['ens'=8,'lat'=8,'lon'=4] {'ens'}, dimensions={0}, use_global_device_ids=true | all-gather | bytes 294912 | tf_op jit(solution)/shard_map/all_gather | solution.py:87
  56.4 0.8 fusion.42
  57.3 9.1 %collective-permute-start.18 = (f32[2,1,256]{2,1,0:T(1,128)S(1)}, f32[2,1,256]{2,1,0:T(1,128)S(1)}, u32[]{:S(2)}, u32[]{:S(2)}) collective-permute-start(f32[2,1,256]{2,1,0:T(1,128)S(1)} %get-tuple-element.29), channel_id=1, source_target_pairs={{0,4},{4,8},{8,12},{12,16},{16,20},{20,24},{24,28},{1,5},{5,9},{9,... | collective-permute-start | bytes 6152 | tf_op jit(solution)/shard_map/ppermute | solution.py:16
  66.4 1.9 collective-permute-start.19
  68.4 2.7 collective-permute-start.17
  71.1 40.2 %all_gather.13 = f32[16,16,256]{2,1,0:T(8,128)S(1)} all-gather(f32[2,16,256]{2,1,0:T(8,128)S(1)} %fusion.42), channel_id=1, replica_groups=mesh['ens'=8,'lat'=8,'lon'=4] {'ens'}, dimensions={0}, use_global_device_ids=true | all-gather | bytes 294912 | tf_op jit(solution)/shard_map/all_gather | solution.py:87
  111.3 0.8 fusion.45
  112.3 8.8 %collective-permute-start.26 = (f32[2,1,256]{2,1,0:T(1,128)S(1)}, f32[2,1,256]{2,1,0:T(1,128)S(1)}, u32[]{:S(2)}, u32[]{:S(2)}) collective-permute-start(f32[2,1,256]{2,1,0:T(1,128)S(1)} %get-tuple-element.25), channel_id=1, source_target_pairs={{0,4},{4,8},{8,12},{12,16},{16,20},{20,24},{24,28},{1,5},{5,9},{9,... | collective-permute-start | bytes 6152 | tf_op jit(solution)/shard_map/ppermute | solution.py:16
  121.1 1.9 collective-permute-start.27
  123.0 39.0 %all_gather.14 = f32[16,16,256]{2,1,0:T(8,128)S(1)} all-gather(f32[2,16,256]{2,1,0:T(8,128)S(1)} %fusion.45), channel_id=1, replica_groups=mesh['ens'=8,'lat'=8,'lon'=4] {'ens'}, dimensions={0}, use_global_device_ids=true | all-gather | bytes 294912 | tf_op jit(solution)/shard_map/all_gather | solution.py:87
  162.1 2.7 collective-permute-start.25
  164.7 1.5 collective-permute-done.24
  166.2 2.4 collective-permute-start.3
  168.7 2.7 collective-permute-start.1
  171.4 0.1 fusion.48
  171.6 3.5 %collective-permute-done = f32[1,16,16,1]{3,2,1,0:T(8,128)S(1)} collective-permute-done((f32[1,16,16,1]{3,2,1,0:T(8,128)S(1)}, f32[1,16,16,1]{3,2,1,0:T(8,128)S(1)}, u32[]{:S(2)}, u32[]{:S(2)}) %collective-permute-start) | collective-permute-done | bytes 1056 | tf_op jit(solution)/shard_map/ppermute | solution.py:16
  175.1 3.1 %collective-permute-done.3 = f32[1,16,1,256]{3,2,1,0:T(1,128)S(1)} collective-permute-done((f32[1,16,1,256]{3,2,1,0:T(1,128)S(1)}, f32[1,16,1,256]{3,2,1,0:T(1,128)S(1)}, u32[]{:S(2)}, u32[]{:S(2)}) %collective-permute-start.3) | collective-permute-done | bytes 16416 | tf_op jit(solution)/shard_map/ppermute | solution.py:19
  178.2 0.6 fusion.4
  178.8 0.1 fusion.80
  178.9 7.7 %collective-permute-start.6 = (f32[1,16,1,256]{3,2,1,0:T(1,128)S(1)}, f32[1,16,1,256]{3,2,1,0:T(1,128)S(1)}, u32[]{:S(2)}, u32[]{:S(2)}) collective-permute-start(f32[1,16,1,256]{3,2,1,0:T(1,128)S(1)} %get-tuple-element.13), channel_id=1, source_target_pairs={{0,4},{4,8},{8,12},{12,16},{16,20},{20,24},{24,28},{1,5},{5,9},{9,... | collective-permute-start | bytes 49160 | tf_op jit(solution)/shard_map/ppermute | solution.py:16
  186.6 1.9 collective-permute-start.7
  188.7 2.8 %collective-permute-start.5 = (f32[1,16,16,1]{3,2,1,0:T(8,128)S(1)}, f32[1,16,16,1]{3,2,1,0:T(8,128)S(1)}, u32[]{:S(2)}, u32[]{:S(2)}) collective-permute-start(f32[1,16,16,1]{3,2,1,0:T(8,128)S(1)} %get-tuple-element.10), channel_id=1, source_target_pairs={{1,0},{2,1},{3,2},{0,3},{5,4},{6,5},{7,6},{4,7},{9,8},{10,9},{11,1... | collective-permute-start | bytes 3080 | tf_op jit(solution)/shard_map/ppermute | solution.py:19
  191.4 2.3 collective-permute-done.4
  193.7 0.6 fusion.9
  194.4 4.8 %collective-permute-start.14 = (f32[1,16,1,256]{3,2,1,0:T(1,128)S(1)}, f32[1,16,1,256]{3,2,1,0:T(1,128)S(1)}, u32[]{:S(2)}, u32[]{:S(2)}) collective-permute-start(f32[1,16,1,256]{3,2,1,0:T(1,128)S(1)} %get-tuple-element.9), channel_id=1, source_target_pairs={{0,4},{4,8},{8,12},{12,16},{16,20},{20,24},{24,28},{1,5},{5,9},{9,... | collective-permute-start | bytes 49160 | tf_op jit(solution)/shard_map/ppermute | solution.py:16
  199.2 1.9 collective-permute-start.15
  201.1 0.9 collective-permute-start.12
  202.0 2.4 collective-permute-start.13
  204.4 40.0 %all_gather.15 = f32[16,16,256]{2,1,0:T(8,128)S(1)} all-gather(f32[2,16,256]{2,1,0:T(8,128)S(1)} %fusion.48), channel_id=1, replica_groups=mesh['ens'=8,'lat'=8,'lon'=4] {'ens'}, dimensions={0}, use_global_device_ids=true | all-gather | bytes 294912 | tf_op jit(solution)/shard_map/all_gather | solution.py:87
  244.4 9.1 %collective-permute-start.30 = (f32[2,1,256]{2,1,0:T(1,128)S(1)}, f32[2,1,256]{2,1,0:T(1,128)S(1)}, u32[]{:S(2)}, u32[]{:S(2)}) collective-permute-start(f32[2,1,256]{2,1,0:T(1,128)S(1)} %get-tuple-element.21), channel_id=1, source_target_pairs={{0,4},{4,8},{8,12},{12,16},{16,20},{20,24},{24,28},{1,5},{5,9},{9,... | collective-permute-start | bytes 6152 | tf_op jit(solution)/shard_map/ppermute | solution.py:16
  253.5 1.9 collective-permute-start.31
  255.6 2.7 collective-permute-start.29
  258.2 0.6 fusion.14
  258.9 4.2 %collective-permute-start.22 = (f32[1,16,1,256]{3,2,1,0:T(1,128)S(1)}, f32[1,16,1,256]{3,2,1,0:T(1,128)S(1)}, u32[]{:S(2)}, u32[]{:S(2)}) collective-permute-start(f32[1,16,1,256]{3,2,1,0:T(1,128)S(1)} %get-tuple-element.5), channel_id=1, source_target_pairs={{0,4},{4,8},{8,12},{12,16},{16,20},{20,24},{24,28},{1,5},{5,9},{9,... | collective-permute-start | bytes 49160 | tf_op jit(solution)/shard_map/ppermute | solution.py:16
  263.1 1.9 collective-permute-start.23
  265.2 2.7 collective-permute-start.21
  267.8 0.7 fusion.51
  268.5 1.6 collective-permute-done.20
  270.2 1.3 fusion.19
  (61 shorter events, 1.3 us)
Async XLA Ops:
  0.6 0.8 copy-start
  0.6 55.7 %copy-start.1 = (s32[4,16,16,256]{3,2,1,0:T(8,128)S(1)}, s32[4,16,16,256]{3,2,1,0:T(8,128)}, u32[]{:S(2)}) copy-start(s32[4,16,16,256]{3,2,1,0:T(8,128)} %param.13) | copy-start | bytes 3145732
  1.5 14.8 %copy-start.5 = (f32[16]{0:T(128)S(1)}, f32[16]{0:T(128)}, u32[]{:S(2)}) copy-start(f32[16]{0:T(128)} %param.15) | copy-start | bytes 196
  1.5 14.9 %copy-start.3 = (f32[2,16,256]{2,1,0:T(8,128)S(1)}, f32[2,16,256]{2,1,0:T(8,128)}, u32[]{:S(2)}) copy-start(f32[2,16,256]{2,1,0:T(8,128)} %param.11) | copy-start | bytes 98308
  1.5 54.7 %copy-start.4 = (f32[16]{0:T(128)S(1)}, f32[16]{0:T(128)}, u32[]{:S(2)}) copy-start(f32[16]{0:T(128)} %param.14) | copy-start | bytes 196
  2.6 168.8 %copy-start.2 = (bf16[4,2,16,16,256]{4,3,2,1,0:T(8,128)(2,1)S(1)}, bf16[4,2,16,16,256]{4,3,2,1,0:T(8,128)(2,1)}, u32[]{:S(2)}) copy-start(bf16[4,2,16,16,256]{4,3,2,1,0:T(8,128)(2,1)} %param.12) | copy-start | bytes 3145732
  2.6 172.5 %collective-permute-start.2 = (f32[1,16,1,256]{3,2,1,0:T(1,128)S(1)}, f32[1,16,1,256]{3,2,1,0:T(1,128)S(1)}, u32[]{:S(2)}, u32[]{:S(2)}) collective-permute-start(f32[1,16,1,256]{3,2,1,0:T(1,128)S(1)} %get-tuple-element.17), channel_id=1, source_target_pairs={{0,4},{4,8},{8,12},{12,16},{16,20},{20,24},{24,28},{1,5},{5,9},{9,... | collective-permute-start | bytes 49160 | tf_op jit(solution)/shard_map/ppermute | solution.py:16
  8.4 47.9 %collective-permute-start.10 = (f32[2,1,256]{2,1,0:T(1,128)S(1)}, f32[2,1,256]{2,1,0:T(1,128)S(1)}, u32[]{:S(2)}, u32[]{:S(2)}) collective-permute-start(f32[2,1,256]{2,1,0:T(1,128)S(1)} %get-tuple-element.33), channel_id=1, source_target_pairs={{0,4},{4,8},{8,12},{12,16},{16,20},{20,24},{24,28},{1,5},{5,9},{9,... | collective-permute-start | bytes 6152 | tf_op jit(solution)/shard_map/ppermute | solution.py:16
  10.4 46.0 %collective-permute-start.11 = (f32[2,1,256]{2,1,0:T(1,128)S(1)}, f32[2,1,256]{2,1,0:T(1,128)S(1)}, u32[]{:S(2)}, u32[]{:S(2)}) collective-permute-start(f32[2,1,256]{2,1,0:T(1,128)S(1)} %get-tuple-element.32), channel_id=1, source_target_pairs={{4,0},{8,4},{12,8},{16,12},{20,16},{24,20},{28,24},{5,1},{9,5},{13... | collective-permute-start | bytes 6152 | tf_op jit(solution)/shard_map/ppermute | solution.py:19
  13.6 42.8 %collective-permute-start.8 = (f32[2,16,1]{2,1,0:T(8,128)S(1)}, f32[2,16,1]{2,1,0:T(8,128)S(1)}, u32[]{:S(2)}, u32[]{:S(2)}) collective-permute-start(f32[2,16,1]{2,1,0:T(8,128)S(1)} %get-tuple-element.31), channel_id=1, source_target_pairs={{0,1},{1,2},{2,3},{3,0},{4,5},{5,6},{6,7},{7,4},{8,9},{9,10},{10,1... | collective-permute-start | bytes 392 | tf_op jit(solution)/shard_map/ppermute | solution.py:16
  14.8 41.5 %collective-permute-start.9 = (f32[2,16,1]{2,1,0:T(8,128)S(1)}, f32[2,16,1]{2,1,0:T(8,128)S(1)}, u32[]{:S(2)}, u32[]{:S(2)}) collective-permute-start(f32[2,16,1]{2,1,0:T(8,128)S(1)} %get-tuple-element.30), channel_id=1, source_target_pairs={{1,0},{2,1},{3,2},{0,3},{5,4},{6,5},{7,6},{4,7},{9,8},{10,9},{11,1... | collective-permute-start | bytes 392 | tf_op jit(solution)/shard_map/ppermute | solution.py:19
  57.3 54.0 %collective-permute-start.18 = (f32[2,1,256]{2,1,0:T(1,128)S(1)}, f32[2,1,256]{2,1,0:T(1,128)S(1)}, u32[]{:S(2)}, u32[]{:S(2)}) collective-permute-start(f32[2,1,256]{2,1,0:T(1,128)S(1)} %get-tuple-element.29), channel_id=1, source_target_pairs={{0,4},{4,8},{8,12},{12,16},{16,20},{20,24},{24,28},{1,5},{5,9},{9,... | collective-permute-start | bytes 6152 | tf_op jit(solution)/shard_map/ppermute | solution.py:16
  66.4 44.9 %collective-permute-start.19 = (f32[2,1,256]{2,1,0:T(1,128)S(1)}, f32[2,1,256]{2,1,0:T(1,128)S(1)}, u32[]{:S(2)}, u32[]{:S(2)}) collective-permute-start(f32[2,1,256]{2,1,0:T(1,128)S(1)} %get-tuple-element.28), channel_id=1, source_target_pairs={{4,0},{8,4},{12,8},{16,12},{20,16},{24,20},{28,24},{5,1},{9,5},{13... | collective-permute-start | bytes 6152 | tf_op jit(solution)/shard_map/ppermute | solution.py:19
  68.3 43.0 %collective-permute-start.16 = (f32[2,16,1]{2,1,0:T(8,128)S(1)}, f32[2,16,1]{2,1,0:T(8,128)S(1)}, u32[]{:S(2)}, u32[]{:S(2)}) collective-permute-start(f32[2,16,1]{2,1,0:T(8,128)S(1)} %get-tuple-element.27), channel_id=1, source_target_pairs={{0,1},{1,2},{2,3},{3,0},{4,5},{5,6},{6,7},{7,4},{8,9},{9,10},{10,1... | collective-permute-start | bytes 392 | tf_op jit(solution)/shard_map/ppermute | solution.py:16
  68.4 42.9 %collective-permute-start.17 = (f32[2,16,1]{2,1,0:T(8,128)S(1)}, f32[2,16,1]{2,1,0:T(8,128)S(1)}, u32[]{:S(2)}, u32[]{:S(2)}) collective-permute-start(f32[2,16,1]{2,1,0:T(8,128)S(1)} %get-tuple-element.26), channel_id=1, source_target_pairs={{1,0},{2,1},{3,2},{0,3},{5,4},{6,5},{7,6},{4,7},{9,8},{10,9},{11,1... | collective-permute-start | bytes 392 | tf_op jit(solution)/shard_map/ppermute | solution.py:19
  112.3 56.5 %collective-permute-start.26 = (f32[2,1,256]{2,1,0:T(1,128)S(1)}, f32[2,1,256]{2,1,0:T(1,128)S(1)}, u32[]{:S(2)}, u32[]{:S(2)}) collective-permute-start(f32[2,1,256]{2,1,0:T(1,128)S(1)} %get-tuple-element.25), channel_id=1, source_target_pairs={{0,4},{4,8},{8,12},{12,16},{16,20},{20,24},{24,28},{1,5},{5,9},{9,... | collective-permute-start | bytes 6152 | tf_op jit(solution)/shard_map/ppermute | solution.py:16
  121.1 50.3 %collective-permute-start.27 = (f32[2,1,256]{2,1,0:T(1,128)S(1)}, f32[2,1,256]{2,1,0:T(1,128)S(1)}, u32[]{:S(2)}, u32[]{:S(2)}) collective-permute-start(f32[2,1,256]{2,1,0:T(1,128)S(1)} %get-tuple-element.24), channel_id=1, source_target_pairs={{4,0},{8,4},{12,8},{16,12},{20,16},{24,20},{28,24},{5,1},{9,5},{13... | collective-permute-start | bytes 6152 | tf_op jit(solution)/shard_map/ppermute | solution.py:19
  162.1 4.2 %collective-permute-start.24 = (f32[2,16,1]{2,1,0:T(8,128)S(1)}, f32[2,16,1]{2,1,0:T(8,128)S(1)}, u32[]{:S(2)}, u32[]{:S(2)}) collective-permute-start(f32[2,16,1]{2,1,0:T(8,128)S(1)} %get-tuple-element.23), channel_id=1, source_target_pairs={{0,1},{1,2},{2,3},{3,0},{4,5},{5,6},{6,7},{7,4},{8,9},{9,10},{10,1... | collective-permute-start | bytes 392 | tf_op jit(solution)/shard_map/ppermute | solution.py:16
  162.1 6.6 %collective-permute-start.25 = (f32[2,16,1]{2,1,0:T(8,128)S(1)}, f32[2,16,1]{2,1,0:T(8,128)S(1)}, u32[]{:S(2)}, u32[]{:S(2)}) collective-permute-start(f32[2,16,1]{2,1,0:T(8,128)S(1)} %get-tuple-element.22), channel_id=1, source_target_pairs={{1,0},{2,1},{3,2},{0,3},{5,4},{6,5},{7,6},{4,7},{9,8},{10,9},{11,1... | collective-permute-start | bytes 392 | tf_op jit(solution)/shard_map/ppermute | solution.py:19
  166.2 12.0 %collective-permute-start.3 = (f32[1,16,1,256]{3,2,1,0:T(1,128)S(1)}, f32[1,16,1,256]{3,2,1,0:T(1,128)S(1)}, u32[]{:S(2)}, u32[]{:S(2)}) collective-permute-start(f32[1,16,1,256]{3,2,1,0:T(1,128)S(1)} %get-tuple-element.16), channel_id=1, source_target_pairs={{4,0},{8,4},{12,8},{16,12},{20,16},{24,20},{28,24},{5,1},{9,5},{13... | collective-permute-start | bytes 49160 | tf_op jit(solution)/shard_map/ppermute | solution.py:19
  168.6 6.5 %collective-permute-start = (f32[1,16,16,1]{3,2,1,0:T(8,128)S(1)}, f32[1,16,16,1]{3,2,1,0:T(8,128)S(1)}, u32[]{:S(2)}, u32[]{:S(2)}) collective-permute-start(f32[1,16,16,1]{3,2,1,0:T(8,128)S(1)} %get-tuple-element.15), channel_id=1, source_target_pairs={{0,1},{1,2},{2,3},{3,0},{4,5},{5,6},{6,7},{7,4},{8,9},{9,10},{10,1... | collective-permute-start | bytes 3080 | tf_op jit(solution)/shard_map/ppermute | solution.py:16
  168.7 6.4 %collective-permute-start.1 = (f32[1,16,16,1]{3,2,1,0:T(8,128)S(1)}, f32[1,16,16,1]{3,2,1,0:T(8,128)S(1)}, u32[]{:S(2)}, u32[]{:S(2)}) collective-permute-start(f32[1,16,16,1]{3,2,1,0:T(8,128)S(1)} %get-tuple-element.14), channel_id=1, source_target_pairs={{1,0},{2,1},{3,2},{0,3},{5,4},{6,5},{7,6},{4,7},{9,8},{10,9},{11,1... | collective-permute-start | bytes 3080 | tf_op jit(solution)/shard_map/ppermute | solution.py:19
  178.9 14.8 %collective-permute-start.6 = (f32[1,16,1,256]{3,2,1,0:T(1,128)S(1)}, f32[1,16,1,256]{3,2,1,0:T(1,128)S(1)}, u32[]{:S(2)}, u32[]{:S(2)}) collective-permute-start(f32[1,16,1,256]{3,2,1,0:T(1,128)S(1)} %get-tuple-element.13), channel_id=1, source_target_pairs={{0,4},{4,8},{8,12},{12,16},{16,20},{20,24},{24,28},{1,5},{5,9},{9,... | collective-permute-start | bytes 49160 | tf_op jit(solution)/shard_map/ppermute | solution.py:16
  186.6 7.0 %collective-permute-start.7 = (f32[1,16,1,256]{3,2,1,0:T(1,128)S(1)}, f32[1,16,1,256]{3,2,1,0:T(1,128)S(1)}, u32[]{:S(2)}, u32[]{:S(2)}) collective-permute-start(f32[1,16,1,256]{3,2,1,0:T(1,128)S(1)} %get-tuple-element.12), channel_id=1, source_target_pairs={{4,0},{8,4},{12,8},{16,12},{20,16},{24,20},{28,24},{5,1},{9,5},{13... | collective-permute-start | bytes 49160 | tf_op jit(solution)/shard_map/ppermute | solution.py:19
  188.6 5.1 %collective-permute-start.4 = (f32[1,16,16,1]{3,2,1,0:T(8,128)S(1)}, f32[1,16,16,1]{3,2,1,0:T(8,128)S(1)}, u32[]{:S(2)}, u32[]{:S(2)}) collective-permute-start(f32[1,16,16,1]{3,2,1,0:T(8,128)S(1)} %get-tuple-element.11), channel_id=1, source_target_pairs={{0,1},{1,2},{2,3},{3,0},{4,5},{5,6},{6,7},{7,4},{8,9},{9,10},{10,1... | collective-permute-start | bytes 3080 | tf_op jit(solution)/shard_map/ppermute | solution.py:16
  188.7 5.0 %collective-permute-start.5 = (f32[1,16,16,1]{3,2,1,0:T(8,128)S(1)}, f32[1,16,16,1]{3,2,1,0:T(8,128)S(1)}, u32[]{:S(2)}, u32[]{:S(2)}) collective-permute-start(f32[1,16,16,1]{3,2,1,0:T(8,128)S(1)} %get-tuple-element.10), channel_id=1, source_target_pairs={{1,0},{2,1},{3,2},{0,3},{5,4},{6,5},{7,6},{4,7},{9,8},{10,9},{11,1... | collective-permute-start | bytes 3080 | tf_op jit(solution)/shard_map/ppermute | solution.py:19
  194.4 61.2 %collective-permute-start.14 = (f32[1,16,1,256]{3,2,1,0:T(1,128)S(1)}, f32[1,16,1,256]{3,2,1,0:T(1,128)S(1)}, u32[]{:S(2)}, u32[]{:S(2)}) collective-permute-start(f32[1,16,1,256]{3,2,1,0:T(1,128)S(1)} %get-tuple-element.9), channel_id=1, source_target_pairs={{0,4},{4,8},{8,12},{12,16},{16,20},{20,24},{24,28},{1,5},{5,9},{9,... | collective-permute-start | bytes 49160 | tf_op jit(solution)/shard_map/ppermute | solution.py:16
  199.2 59.0 %collective-permute-start.15 = (f32[1,16,1,256]{3,2,1,0:T(1,128)S(1)}, f32[1,16,1,256]{3,2,1,0:T(1,128)S(1)}, u32[]{:S(2)}, u32[]{:S(2)}) collective-permute-start(f32[1,16,1,256]{3,2,1,0:T(1,128)S(1)} %get-tuple-element.8), channel_id=1, source_target_pairs={{4,0},{8,4},{12,8},{16,12},{20,16},{24,20},{28,24},{5,1},{9,5},{13... | collective-permute-start | bytes 49160 | tf_op jit(solution)/shard_map/ppermute | solution.py:19
  201.1 52.4 %collective-permute-start.12 = (f32[1,16,16,1]{3,2,1,0:T(8,128)S(1)}, f32[1,16,16,1]{3,2,1,0:T(8,128)S(1)}, u32[]{:S(2)}, u32[]{:S(2)}) collective-permute-start(f32[1,16,16,1]{3,2,1,0:T(8,128)S(1)} %get-tuple-element.7), channel_id=1, source_target_pairs={{0,1},{1,2},{2,3},{3,0},{4,5},{5,6},{6,7},{7,4},{8,9},{9,10},{10,1... | collective-permute-start | bytes 3080 | tf_op jit(solution)/shard_map/ppermute | solution.py:16
  202.0 53.4 %collective-permute-start.13 = (f32[1,16,16,1]{3,2,1,0:T(8,128)S(1)}, f32[1,16,16,1]{3,2,1,0:T(8,128)S(1)}, u32[]{:S(2)}, u32[]{:S(2)}) collective-permute-start(f32[1,16,16,1]{3,2,1,0:T(8,128)S(1)} %get-tuple-element.6), channel_id=1, source_target_pairs={{1,0},{2,1},{3,2},{0,3},{5,4},{6,5},{7,6},{4,7},{9,8},{10,9},{11,1... | collective-permute-start | bytes 3080 | tf_op jit(solution)/shard_map/ppermute | solution.py:19
  244.4 20.8 %collective-permute-start.30 = (f32[2,1,256]{2,1,0:T(1,128)S(1)}, f32[2,1,256]{2,1,0:T(1,128)S(1)}, u32[]{:S(2)}, u32[]{:S(2)}) collective-permute-start(f32[2,1,256]{2,1,0:T(1,128)S(1)} %get-tuple-element.21), channel_id=1, source_target_pairs={{0,4},{4,8},{8,12},{12,16},{16,20},{20,24},{24,28},{1,5},{5,9},{9,... | collective-permute-start | bytes 6152 | tf_op jit(solution)/shard_map/ppermute | solution.py:16
  253.5 14.3 %collective-permute-start.31 = (f32[2,1,256]{2,1,0:T(1,128)S(1)}, f32[2,1,256]{2,1,0:T(1,128)S(1)}, u32[]{:S(2)}, u32[]{:S(2)}) collective-permute-start(f32[2,1,256]{2,1,0:T(1,128)S(1)} %get-tuple-element.20), channel_id=1, source_target_pairs={{4,0},{8,4},{12,8},{16,12},{20,16},{24,20},{28,24},{5,1},{9,5},{13... | collective-permute-start | bytes 6152 | tf_op jit(solution)/shard_map/ppermute | solution.py:19
  255.4 7.7 %collective-permute-start.28 = (f32[2,16,1]{2,1,0:T(8,128)S(1)}, f32[2,16,1]{2,1,0:T(8,128)S(1)}, u32[]{:S(2)}, u32[]{:S(2)}) collective-permute-start(f32[2,16,1]{2,1,0:T(8,128)S(1)} %get-tuple-element.19), channel_id=1, source_target_pairs={{0,1},{1,2},{2,3},{3,0},{4,5},{5,6},{6,7},{7,4},{8,9},{9,10},{10,1... | collective-permute-start | bytes 392 | tf_op jit(solution)/shard_map/ppermute | solution.py:16
  255.6 9.5 %collective-permute-start.29 = (f32[2,16,1]{2,1,0:T(8,128)S(1)}, f32[2,16,1]{2,1,0:T(8,128)S(1)}, u32[]{:S(2)}, u32[]{:S(2)}) collective-permute-start(f32[2,16,1]{2,1,0:T(8,128)S(1)} %get-tuple-element.18), channel_id=1, source_target_pairs={{1,0},{2,1},{3,2},{0,3},{5,4},{6,5},{7,6},{4,7},{9,8},{10,9},{11,1... | collective-permute-start | bytes 392 | tf_op jit(solution)/shard_map/ppermute | solution.py:19
  258.9 11.3 %collective-permute-start.22 = (f32[1,16,1,256]{3,2,1,0:T(1,128)S(1)}, f32[1,16,1,256]{3,2,1,0:T(1,128)S(1)}, u32[]{:S(2)}, u32[]{:S(2)}) collective-permute-start(f32[1,16,1,256]{3,2,1,0:T(1,128)S(1)} %get-tuple-element.5), channel_id=1, source_target_pairs={{0,4},{4,8},{8,12},{12,16},{16,20},{20,24},{24,28},{1,5},{5,9},{9,... | collective-permute-start | bytes 49160 | tf_op jit(solution)/shard_map/ppermute | solution.py:16
  263.1 7.1 %collective-permute-start.23 = (f32[1,16,1,256]{3,2,1,0:T(1,128)S(1)}, f32[1,16,1,256]{3,2,1,0:T(1,128)S(1)}, u32[]{:S(2)}, u32[]{:S(2)}) collective-permute-start(f32[1,16,1,256]{3,2,1,0:T(1,128)S(1)} %get-tuple-element.4), channel_id=1, source_target_pairs={{4,0},{8,4},{12,8},{16,12},{20,16},{24,20},{28,24},{5,1},{9,5},{13... | collective-permute-start | bytes 49160 | tf_op jit(solution)/shard_map/ppermute | solution.py:19
  265.1 5.1 %collective-permute-start.20 = (f32[1,16,16,1]{3,2,1,0:T(8,128)S(1)}, f32[1,16,16,1]{3,2,1,0:T(8,128)S(1)}, u32[]{:S(2)}, u32[]{:S(2)}) collective-permute-start(f32[1,16,16,1]{3,2,1,0:T(8,128)S(1)} %get-tuple-element.3), channel_id=1, source_target_pairs={{0,1},{1,2},{2,3},{3,0},{4,5},{5,6},{6,7},{7,4},{8,9},{9,10},{10,1... | collective-permute-start | bytes 3080 | tf_op jit(solution)/shard_map/ppermute | solution.py:16
  265.2 5.0 %collective-permute-start.21 = (f32[1,16,16,1]{3,2,1,0:T(8,128)S(1)}, f32[1,16,16,1]{3,2,1,0:T(8,128)S(1)}, u32[]{:S(2)}, u32[]{:S(2)}) collective-permute-start(f32[1,16,16,1]{3,2,1,0:T(8,128)S(1)} %get-tuple-element.2), channel_id=1, source_target_pairs={{1,0},{2,1},{3,2},{0,3},{5,4},{6,5},{7,6},{4,7},{9,8},{10,9},{11,1... | collective-permute-start | bytes 3080 | tf_op jit(solution)/shard_map/ppermute | solution.py:19
where the time goes:
time: 273 us; the launch traced here: 271 us
  blocking collectives  159 us (58%)
  starting transfers between devices  89.5 us (33%)
  waiting for transfers between devices  12 us (4%)
  other arithmetic  6.54 us (2%)
    all_gather x4, blocking collectives, per_device(): past = lax.all_gather(current, 'ens', axis=0, tiled=True)  159 us
    ppermute x16, starting transfers between devices, extended(): lax.ppermute(lax.slice_in_dim(block, block.shape[dim] - width, None, axis...  53.3 us
    ppermute x16, starting transfers between devices, extended(): lax.ppermute(lax.slice_in_dim(block, 0, width, axis=dim), axis, backward)  36.2 us
    ppermute x16, waiting for transfers between devices, extended(): lax.ppermute(lax.slice_in_dim(block, block.shape[dim] - width, None, axis...  8.94 us
  transfers between devices with their start and end apart: 32, of which 5 were waited for; matrix products, arithmetic and copies ran while one was open for 2% of the time, Pallas kernels for 0%

commit v1 on v0

v1 whole, which is shorter than its diff:
```python
import functools

import jax
import jax.numpy as jnp
from jax import lax
from jax.experimental import pallas as pl
from jax.experimental.pallas import tpu as pltpu
from jax.sharding import PartitionSpec as P

F32 = jnp.float32
I32 = jnp.int32
STEPS = 4
LEV = 16
COEF = 3
NCD = 1 + 3 * COEF
VMEM = pl.BlockSpec(memory_space=pltpu.VMEM)
SMEM = pl.BlockSpec(memory_space=pltpu.SMEM)


def lanes():
    return lax.broadcasted_iota(I32, (8, 128), 1)


def subs():
    return lax.broadcasted_iota(I32, (8, 128), 0)


def rows_at(r):
    return pl.ds(8 * r, 8)


def cols_at(c):
    return pl.ds(128 * c, 128)


def own_tiles(delta_ref, speeds_ref, upwind_ref, a, lev, c):
    if a == 0:
        return [delta_ref[0, lev, rows_at(r), cols_at(c)] for r in range(2)]
    step, kind = divmod(a - 1, 3)
    if kind < 2:
        both = speeds_ref[step, kind, lev, :, cols_at(c)].astype(F32)
        return [both[0:8], both[8:16]]
    return [upwind_ref[step, lev, rows_at(r), cols_at(c)].astype(F32) for r in range(2)]


def pack_columns(delta_ref, speeds_ref, upwind_ref, state_ref, out_ref):
    lane = lanes()
    for a in range(NCD):
        acc = [jnp.zeros((8, 128), F32)] * 2
        for lev in range(LEV):
            left = own_tiles(delta_ref, speeds_ref, upwind_ref, a, lev, 0)
            right = own_tiles(delta_ref, speeds_ref, upwind_ref, a, lev, 1)
            for r in range(2):
                edge = jnp.where(lane < 64, left[r], right[r])
                edge = pltpu.roll(edge, 8 * lev + 4 if 8 * lev + 4 < 128 else 8 * lev + 4 - 128, 1)
                acc[r] = jnp.where(lane // 8 == lev, edge, acc[r])
        for r in range(2):
            out_ref[a, rows_at(r), :] = acc[r]
    first = 2 * lax.axis_index("ens")
    acc = [jnp.zeros((8, 128), F32)] * 2
    for i in range(2):
        for r in range(2):
            edge = jnp.where(
                lane < 64, state_ref[i, rows_at(r), cols_at(0)], state_ref[i, rows_at(r), cols_at(1)]
            )
            edge = pltpu.roll(edge, 8 * (first + i) + 4, 1)
            acc[r] = jnp.where(lane // 8 == first + i, edge, acc[r])
    for r in range(2):
        out_ref[NCD, rows_at(r), :] = acc[r]


def strip_tile(own_ref, west_ref, east_ref, a, r, c):
    half = lanes() % 8 < 4
    own = own_ref[a, rows_at(r), :]
    if c == 0:
        return jnp.where(half, west_ref[a, rows_at(r), :], own)
    return jnp.where(half, own, east_ref[a, rows_at(r), :])


def state_block(state_ref, own_ref, west_ref, east_ref, out_ref):
    out_ref[0:2] = state_ref[...]
    for r in range(2):
        for c in range(2):
            out_ref[2, rows_at(r), cols_at(c)] = strip_tile(own_ref, west_ref, east_ref, NCD, r, c)


def join_pair(own_ref, other_ref, out_ref):
    half = lax.rem(lax.axis_index("ens"), 2)
    out_ref[pl.ds(2 * half, 2)] = own_ref[0:2]
    out_ref[pl.ds(2 - 2 * half, 2)] = other_ref[0:2]
    out_ref[4] = own_ref[2] + other_ref[2]


def merge_rows(pieces):
    sub = subs()
    acc = jnp.zeros((8, 128), F32)
    for tile, shift, first, last in pieces:
        if shift % 8:
            tile = pltpu.roll(tile, shift % 8, 0)
        acc = jnp.where((sub >= first) & (sub <= last), tile, acc)
    return acc


def pack_rows(delta_ref, speeds_ref, upwind_ref, own_ref, west_ref, east_ref, strip_ref, down_ref, up_ref):
    def put(lev, c, tiles):
        for kind in range(3):
            k0, k1, k2 = (tiles[1 + 3 * step + kind] for step in range(3))
            d = tiles[0]
            low = [(k0[0], 0, 0, 2), (k1[0], 3, 3, 4), (k2[0], 5, 5, 5)]
            high = [(k0[1], 0, 5, 7), (k1[1], -3, 3, 4), (k2[1], -5, 2, 2)]
            if kind == 0:
                low.append((d[0], 6, 6, 7))
                high.append((d[1], -4, 0, 1))
            if kind == 1:
                low.append((d[0], 4, 6, 7))
                high.append((d[1], -6, 0, 1))
            down_ref[lev, rows_at(kind), cols_at(c)] = merge_rows(low)
            up_ref[lev, rows_at(kind), cols_at(c)] = merge_rows(high)

    for c in range(2):
        tiles = []
        for a in range(NCD):
            pair = [strip_tile(own_ref, west_ref, east_ref, a, r, c) for r in range(2)]
            for r in range(2):
                strip_ref[a, rows_at(r), cols_at(c)] = pair[r]
            tiles.append(pair)
        put(LEV, c, tiles)

    def body(lev, carry):
        for c in range(2):
            put(lev, c, [own_tiles(delta_ref, speeds_ref, upwind_ref, a, lev, c) for a in range(NCD)])
        return carry

    lax.fori_loop(0, LEV, body, 0)


def full_state(b0_ref, b1_ref, b2_ref, b3_ref, out_ref, down_ref, up_ref):
    mine = lax.axis_index("ens") // 2
    blocks = (b0_ref, b1_ref, b2_ref, b3_ref)
    for ahead in range(4):
        out_ref[pl.ds(4 * lax.rem(mine + ahead, 4), 4)] = blocks[ahead][0:4]
    out_ref[LEV] = (b0_ref[4] + b1_ref[4]) + (b2_ref[4] + b3_ref[4])
    low = subs() < 4
    for p in range(9):
        for c in range(2):
            a0, a1 = out_ref[2 * p, rows_at(0), cols_at(c)], out_ref[2 * p, rows_at(1), cols_at(c)]
            if p < 8:
                b0 = pltpu.roll(out_ref[2 * p + 1, rows_at(0), cols_at(c)], 4, 0)
                b1 = pltpu.roll(out_ref[2 * p + 1, rows_at(1), cols_at(c)], 4, 0)
            else:
                b0, b1 = a0, a1
            down_ref[p, :, cols_at(c)] = jnp.where(low, a0, b0)
            up_ref[p, :, cols_at(c)] = jnp.where(low, b1, a1)


def advance(
    seed_ref, table_ref, visc_ref, rate_ref,
    delta_ref, speeds_ref, upwind_ref, strip_ref, north_ref, south_ref,
    state_ref, snorth_ref, ssouth_ref,
    delta_out, state_out,
    edge_state, edge_delta, finals,
):
    lane, sub = lanes(), subs()
    band = lax.axis_index("lat")
    first = 2 * lax.axis_index("ens")
    seed = seed_ref[0]
    inside = jnp.where(
        sub < 4,
        jnp.where(band < lax.axis_size("lat") - 1, 1.0, 0.0).astype(F32),
        jnp.where(band > 0, 1.0, 0.0).astype(F32),
    )
    keep = [(sub <= 2, sub >= 5), (sub <= 1, sub >= 6), (sub <= 0, sub >= 7)]

    def halo_coef(lev, kind, step, c):
        north = north_ref[lev, rows_at(kind), cols_at(c)]
        south = south_ref[lev, rows_at(kind), cols_at(c)]
        shift = (0, 3, 5)[step]
        if shift:
            north = pltpu.roll(north, 8 - shift, 0)
            south = pltpu.roll(south, shift, 0)
        low, high = keep[step]
        return jnp.where(low, north, jnp.where(high, south, 0.0))

    def halo_delta(lev, c):
        n0 = pltpu.roll(north_ref[lev, rows_at(0), cols_at(c)], 2, 0)
        n1 = pltpu.roll(north_ref[lev, rows_at(1), cols_at(c)], 4, 0)
        s0 = pltpu.roll(south_ref[lev, rows_at(0), cols_at(c)], 4, 0)
        s1 = pltpu.roll(south_ref[lev, rows_at(1), cols_at(c)], 6, 0)
        return jnp.where(sub < 2, n0, jnp.where(sub < 4, n1, jnp.where(sub < 6, s0, s1)))

    def halo_state(p, odd, c):
        north, south = snorth_ref[p, :, cols_at(c)], ssouth_ref[p, :, cols_at(c)]
        if odd:
            return pltpu.roll(jnp.where(sub < 4, south, north), 4, 0)
        return jnp.where(sub < 4, north, south)

    def sides(f, fix_west, fix_east):
        west, east = [], []
        for r, (left, right) in enumerate(f):
            wl, wr = pltpu.roll(left, 1, 1), pltpu.roll(right, 1, 1)
            el, er = pltpu.roll(left, 127, 1), pltpu.roll(right, 127, 1)
            if fix_west is None:
                west.append((wl, wr))
                east.append((el, er))
            else:
                west.append((jnp.where(lane == 0, fix_west[r], wl), jnp.where(lane == 0, wl, wr)))
                east.append((jnp.where(lane == 127, er, el), jnp.where(lane == 127, fix_east[r], er)))
        return west, east

    def ends(f):
        below, above = [], []
        down = [[pltpu.roll(f[r][c], 1, 0) for c in range(2)] for r in range(3)]
        up = [[pltpu.roll(f[r][c], 7, 0) for c in range(2)] for r in range(3)]
        for r in range(3):
            below.append([jnp.where(sub == 0, down[(r + 2) % 3][c], down[r][c]) for c in range(2)])
            above.append([jnp.where(sub == 7, up[(r + 1) % 3][c], up[r][c]) for c in range(2)])
        return below, above

    def run(state, delta, visc, rate, coefs, edges, before):
        for step in range(STEPS):
            before(step, state, delta)
            if step == STEPS - 1 and edges is None:
                return state, delta
            count = 3 if step < STEPS - 1 else 2
            fixes = [None] * 4 if edges is None else edges(step, count)
            ws, es = sides(state[:count], fixes[0], fixes[1])
            wd, ed = sides(delta[:count], fixes[2], fixes[3])
            ss, ns = ends(state)
            sd, nd = ends(delta)
            next_state, next_delta = [], []
            for r in range(count):
                row_s, row_d = [], []
                for c in range(2):
                    s, t, m = coefs(step, r, c)
                    v = visc[c] if r < 2 else visc[c] * inside
                    vs, vt = v + s, v + t
                    eastward, northward = (m & 1) == 1, m >= 2
                    cw, ce = jnp.where(eastward, vs, v), jnp.where(eastward, v, vs)
                    cs, cn = jnp.where(northward, vt, v), jnp.where(northward, v, vt)
                    c0 = ((1.0 - 2.0 * v) - vs) - vt
                    f, d = state[r][c], delta[r][c]
                    loss = rate[c] * (f * f)
                    row_s.append(
                        ((c0 - loss) * f + cw * ws[r][c]) + (ce * es[r][c] + cs * ss[r][c]) + cn * ns[r][c]
                    )
                    row_d.append(
                        ((c0 - 3.0 * loss) * d + cw * wd[r][c]) + (ce * ed[r][c] + cs * sd[r][c]) + cn * nd[r][c]
                    )
                next_state.append(row_s)
                next_delta.append(row_d)
            state, delta = next_state, next_delta
        return state, delta

    visc = rate = amp = jnp.zeros((8, 128), F32)
    for lev in range(LEV):
        here = lane // 8 == lev
        visc = jnp.where(here, visc_ref[lev], visc)
        rate = jnp.where(here, rate_ref[lev], rate)
        amp = jnp.where(here, table_ref[seed, lev], amp)

    def strip_coefs(step, r, c):
        out = []
        for kind in range(3):
            if r < 2:
                out.append(strip_ref[1 + 3 * step + kind, rows_at(r), cols_at(c)])
            else:
                out.append(halo_coef(LEV, kind, step, c))
        return out[0], out[1], out[2].astype(I32)

    def strip_before(step, state, delta):
        for r in range(3):
            for c in range(2):
                edge_state[step, c, rows_at(r), :] = state[r][c]
                edge_delta[step, c, rows_at(r), :] = delta[r][c]

    state = [[state_ref[LEV, rows_at(r), cols_at(c)] for c in range(2)] for r in range(2)]
    state.append([halo_state(8, False, c) for c in range(2)])
    delta = [[strip_ref[0, rows_at(r), cols_at(c)] * amp for c in range(2)] for r in range(2)]
    delta.append([halo_delta(LEV, c) * amp for c in range(2)])
    run(state, delta, [visc] * 2, [rate] * 2, strip_coefs, None, strip_before)

    def one_level(p, odd):
        lev = 2 * p + odd
        visc = [jnp.full((8, 128), visc_ref[lev], F32)] * 2
        rate = [jnp.full((8, 128), rate_ref[lev], F32)] * 2
        amp = table_ref[seed, lev]

        def coefs(step, r, c):
            if r < 2:
                s = speeds_ref[step, 0, lev, :, cols_at(c)].astype(F32)[8 * r : 8 * r + 8]
                t = speeds_ref[step, 1, lev, :, cols_at(c)].astype(F32)[8 * r : 8 * r + 8]
                return s, t, upwind_ref[step, lev, rows_at(r), cols_at(c)]
            s, t, m = (halo_coef(lev, kind, step, c) for kind in range(3))
            return s, t, m.astype(I32)

        def edges(step, count):
            to_first = lax.rem(253 - 8 * lev, 128)
            to_last = lax.rem(251 - 8 * lev, 128)
            out = []
            for ref in (edge_state, edge_delta):
                out.append([pltpu.roll(ref[step, 0, rows_at(r), :], to_first, 1) for r in range(count)])
                out.append([pltpu.roll(ref[step, 1, rows_at(r), :], to_last, 1) for r in range(count)])
            return out

        state = [[state_ref[lev, rows_at(r), cols_at(c)] for c in range(2)] for r in range(2)]
        state.append([halo_state(p, odd, c) for c in range(2)])
        delta = [[delta_ref[0, lev, rows_at(r), cols_at(c)] * amp for c in range(2)] for r in range(2)]
        delta.append([halo_delta(lev, c) * amp for c in range(2)])
        state, delta = run(state, delta, visc, rate, coefs, edges, lambda *unused: None)
        for r in range(2):
            for c in range(2):
                finals[lev, rows_at(r), cols_at(c)] = state[r][c]
                delta_out[0, lev, rows_at(r), cols_at(c)] = delta[r][c]

    def body(p, carry):
        one_level(p, 0)
        one_level(p, 1)
        return carry

    lax.fori_loop(0, LEV // 2, body, 0)
    state_out[...] = finals[pl.ds(first, 2)]


def call(kernel, name, shapes, specs, scratch=(), cost=None):
    out = [jax.ShapeDtypeStruct(shape, F32) for shape in shapes]
    single = len(out) == 1
    return pl.pallas_call(
        kernel,
        name=name,
        out_shape=out[0] if single else out,
        in_specs=specs,
        out_specs=VMEM if single else [VMEM] * len(out),
        scratch_shapes=scratch,
        cost_estimate=pl.CostEstimate(flops=cost or 100000, bytes_accessed=cost or 100000, transcendentals=0),
    )


def per_device(perturbation, seed_ids, amp_table, start_state, speeds, upwind, viscosity, reaction):
    n_lat, n_lon, n_ens = lax.axis_size("lat"), lax.axis_size("lon"), lax.axis_size("ens")
    north = [(i, i + 1) for i in range(n_lat - 1)]
    south = [(j, i) for i, j in north]
    eastward = [(i, (i + 1) % n_lon) for i in range(n_lon)]
    westward = [(j, i) for i, j in eastward]

    columns = call(pack_columns, "pack_columns", [(NCD + 1, 16, 128)], [VMEM] * 4)(
        perturbation, speeds, upwind, start_state
    )
    from_west = lax.ppermute(columns, "lon", eastward)
    from_east = lax.ppermute(columns, "lon", westward)
    block = call(state_block, "state_block", [(3, 16, 256)], [VMEM] * 4)(
        start_state, columns, from_west, from_east
    )
    other = lax.ppermute(block, "ens", [(i, i ^ 1) for i in range(n_ens)])
    strips, down, up = call(
        pack_rows, "pack_rows", [(NCD, 16, 256), (LEV + 1, 24, 256), (LEV + 1, 24, 256)], [VMEM] * 6
    )(perturbation, speeds, upwind, columns, from_west, from_east)
    cd_north = lax.ppermute(down, "lat", south)
    cd_south = lax.ppermute(up, "lat", north)
    quad = call(join_pair, "join_pair", [(5, 16, 256)], [VMEM] * 2)(block, other)
    ahead = [
        lax.ppermute(quad, "ens", [((i + 2 * j) % n_ens, i) for i in range(n_ens)]) for j in (1, 2, 3)
    ]
    states, state_down, state_up = call(
        full_state, "full_state", [(LEV + 1, 16, 256), (9, 8, 256), (9, 8, 256)], [VMEM] * 4
    )(quad, *ahead)
    st_north = lax.ppermute(state_down, "lat", south)
    st_south = lax.ppermute(state_up, "lat", north)
    edge = pltpu.VMEM((STEPS, 2, 24, 128), F32)
    return call(
        advance,
        "advance",
        [(1, LEV, 16, 256), (2, 16, 256)],
        [SMEM] * 4 + [VMEM] * 9,
        scratch=[edge, edge, pltpu.VMEM((LEV, 16, 256), F32)],
        cost=10000000,
    )(
        seed_ids, amp_table, viscosity, reaction,
        perturbation, speeds, upwind, strips, cd_north, cd_south,
        states, st_north, st_south,
    )


def solution(mesh):
    step = jax.shard_map(
        per_device,
        mesh=mesh,
        in_specs=(
            P("ens", None, "lat", "lon"),
            P("ens"),
            P(),
            P("ens", "lat", "lon"),
            P(None, None, None, "lat", "lon"),
            P(None, None, "lat", "lon"),
            P(),
            P(),
        ),
        out_specs=(P("ens", None, "lat", "lon"), P("ens", "lat", "lon")),
        check_vma=False,
    )
    return lambda *args: tuple(step(*args))
```

time: 273 us -> 61.8 us (0.23)
  blocking collectives: 159 us -> 0 us
  starting transfers between devices: 89.5 us -> 26 us
  Pallas kernels: 0 us -> 17.1 us
  other arithmetic: 6.54 us -> 0 us
    all_gather x4 -> x0, blocking collectives: 159 us -> none  [per_device(): past = lax.all_gather(current, 'ens', axis=0, tiled=True)]
    ppermute x32 -> x10, starting transfers between devices: 89.5 us -> 26 us  [the longest x1 5.83 us: per_device(): other = lax.ppermute(block, 'ens', [(i, i ^ 1) for i in range(n_ens)])]
    pallas_call x0 -> x6, Pallas kernels: none -> 17.1 us  [the longest x1 6.75 us: per_device(): call(advance, 'advance', [(1, LEV, 16, 256), (2, 16, 256)], [SMEM] * 4 +...]
    sub x8 -> x0, other arithmetic: 5.48 us -> none  [the longest x4 2.96 us: member_step(): return moved - 3.0 * rates * past * past * delta]
    unnamed x12 -> x20, local copies, waits for them, and re-layouts: 0.03 us -> 3.23 us
    ppermute x32 -> x10, waiting for transfers between devices: 12 us -> 13.7 us  [the longest x3 5.16 us: per_device(): lax.ppermute(quad, 'ens', [((i + 2 * j) % n_ens, i) for i in range(n_ens)])]
  transfers between devices with their start and end apart: 32 -> 10, of which waited for: 5 -> 7; matrix products, arithmetic and copies ran while one was open for 2% -> 0% of each run, Pallas kernels for 0% -> 8%
where the time goes in v1:
time: 61.8 us; the launch traced here: 61.4 us
  starting transfers between devices  26 us (42%)
  Pallas kernels  17.1 us (28%)
  waiting for transfers between devices  13.7 us (22%)
  local copies, waits for them, and re-layouts  3.23 us (5%)
  between operations  1.36 us (2%)
    pallas_call x1, Pallas kernels, per_device(): call(advance, 'advance', [(1, LEV, 16, 256), (2, 16, 256)], [SMEM] * 4 +...  6.75 us
    ppermute x1, starting transfers between devices, per_device(): other = lax.ppermute(block, 'ens', [(i, i ^ 1) for i in range(n_ens)])  5.83 us
    ppermute x1, starting transfers between devices, per_device(): cd_north = lax.ppermute(down, 'lat', south)  5.62 us
    ppermute x3, waiting for transfers between devices, per_device(): lax.ppermute(quad, 'ens', [((i + 2 * j) % n_ens, i) for i in range(n_ens)])  5.16 us
    ppermute x1, waiting for transfers between devices, per_device(): other = lax.ppermute(block, 'ens', [(i, i ^ 1) for i in range(n_ens)])  5.15 us
    ppermute x3, starting transfers between devices, per_device(): lax.ppermute(quad, 'ens', [((i + 2 * j) % n_ens, i) for i in range(n_ens)])  3.77 us
    ppermute x1, starting transfers between devices, per_device(): st_south = lax.ppermute(state_up, 'lat', north)  3.55 us
    unnamed x20, local copies, waits for them, and re-layouts  3.23 us
  transfers between devices with their start and end apart: 10, of which 7 were waited for; matrix products, arithmetic and copies ran while one was open for 0% of the time, Pallas kernels for 8%

profile of v1, /device:TPU:1, one launch (start us, length us, event | category | flops | bytes accessed | tf_op | source)
XLA Modules:
  0.0 61.4 jit_solution(3090151393589861559)
XLA Ops:
  0.6 2.6 %pack_columns.1.own_ref = f32[11,16,128]{2,1,0:T(8,128)} custom-call(f32[1,16,16,256]{3,2,1,0:T(8,128)} %delta_ref.5, bf16[4,2,16,16,256]{4,3,2,1,0:T(8,128)(2,1)} %speeds_ref.5, s32[4,16,16,256]{3,2,1,0:T(8,128)} %upwind_ref.5, f32[2,16,256]{2,1,0:T(8,128)} %state_ref.3), custom_call_target="tpu_custom_call" | custom-call | flops 100000 | bytes 100000 | tf_op jit(solution)/shard_map/pack_columns/pallas_call | solution.py:345
  3.2 2.0 %collective-permute-start = (f32[11,16,128]{2,1,0:T(8,128)}, f32[11,16,128]{2,1,0:T(8,128)S(1)}, u32[]{:S(2)}, u32[]{:S(2)}) collective-permute-start(f32[11,16,128]{2,1,0:T(8,128)} %pack_columns.1.own_ref), channel_id=1, source_target_pairs={{0,1},{1,2},{2,3},{3,0},{4,5},{5,6},{6,7},{7,4},{8,9},{9,10},{10,1... | collective-permute-start | bytes 270344 | tf_op jit(solution)/shard_map/ppermute | solution.py:348
  5.2 1.3 %collective-permute-start.1 = (f32[11,16,128]{2,1,0:T(8,128)}, f32[11,16,128]{2,1,0:T(8,128)S(1)}, u32[]{:S(2)}, u32[]{:S(2)}) collective-permute-start(f32[11,16,128]{2,1,0:T(8,128)} %pack_columns.1.own_ref), channel_id=1, source_target_pairs={{1,0},{2,1},{3,2},{0,3},{5,4},{6,5},{7,6},{4,7},{9,8},{10,9},{11,1... | collective-permute-start | bytes 270344 | tf_op jit(solution)/shard_map/ppermute | solution.py:349
  6.5 2.1 %collective-permute-done.west_ref = f32[11,16,128]{2,1,0:T(8,128)S(1)} collective-permute-done((f32[11,16,128]{2,1,0:T(8,128)}, f32[11,16,128]{2,1,0:T(8,128)S(1)}, u32[]{:S(2)}, u32[]{:S(2)}) %collective-permute-start) | collective-permute-done | bytes 90144 | tf_op jit(solution)/shard_map/ppermute | solution.py:348
  8.6 0.0 copy-start.2
  8.6 0.2 collective-permute-done.1.east_ref
  8.8 0.4 copy-done.2
  9.3 0.0 copy-start.3
  9.3 0.6 %copy-done.3 = f32[11,16,128]{2,1,0:T(8,128)} copy-done((f32[11,16,128]{2,1,0:T(8,128)}, f32[11,16,128]{2,1,0:T(8,128)S(1)}, u32[]{:S(2)}) %copy-start.3) | copy-done | bytes 90136
  9.9 2.9 %pack_rows.1 = (f32[10,16,256]{2,1,0:T(8,128)}, f32[17,24,256]{2,1,0:T(8,128)}, f32[17,24,256]{2,1,0:T(8,128)}) custom-call(f32[1,16,16,256]{3,2,1,0:T(8,128)} %delta_ref.5, bf16[4,2,16,16,256]{4,3,2,1,0:T(8,128)(2,1)} %speeds_ref.5, s32[4,16,16,256]{3,2,1,0:T(8,128)} %upwind_ref.5, f32[11,16,128]{2,1,0:T(8,128)} %pack_columns.1.own_ref, ...), custom_call_target="tpu_custom_call" | custom-call | flops 100000 | bytes 100000 | tf_op jit(solution)/shard_map/pack_rows/pallas_call | solution.py:354
  12.8 5.6 %collective-permute-start.2 = (f32[17,24,256]{2,1,0:T(8,128)}, f32[17,24,256]{2,1,0:T(8,128)S(1)}, u32[]{:S(2)}, u32[]{:S(2)}) collective-permute-start(f32[17,24,256]{2,1,0:T(8,128)} %get-tuple-element.9), channel_id=1, source_target_pairs={{4,0},{8,4},{12,8},{16,12},{20,16},{24,20},{28,24},{5,1},{9,5},{13... | collective-permute-start | bytes 1253384 | tf_op jit(solution)/shard_map/ppermute | solution.py:357
  18.4 1.9 %collective-permute-start.3 = (f32[17,24,256]{2,1,0:T(8,128)}, f32[17,24,256]{2,1,0:T(8,128)S(1)}, u32[]{:S(2)}, u32[]{:S(2)}) collective-permute-start(f32[17,24,256]{2,1,0:T(8,128)} %get-tuple-element.10), channel_id=1, source_target_pairs={{0,4},{4,8},{8,12},{12,16},{16,20},{20,24},{24,28},{1,5},{5,9},{9,... | collective-permute-start | bytes 1253384 | tf_op jit(solution)/shard_map/ppermute | solution.py:358
  20.4 1.6 %state_block.1.own_ref = f32[3,16,256]{2,1,0:T(8,128)} custom-call(f32[2,16,256]{2,1,0:T(8,128)} %state_ref.3, f32[11,16,128]{2,1,0:T(8,128)} %pack_columns.1.own_ref, f32[11,16,128]{2,1,0:T(8,128)} %copy-done.2, f32[11,16,128]{2,1,0:T(8,128)} %copy-done.3), custom_call_target="tpu_custom_call" | custom-call | flops 100000 | bytes 100000 | tf_op jit(solution)/shard_map/state_block/pallas_call | solution.py:350
  22.0 5.8 %collective-permute-start.4 = (f32[3,16,256]{2,1,0:T(8,128)}, f32[3,16,256]{2,1,0:T(8,128)S(1)}, u32[]{:S(2)}, u32[]{:S(2)}) collective-permute-start(f32[3,16,256]{2,1,0:T(8,128)} %state_block.1.own_ref), channel_id=1, source_target_pairs={{0,32},{32,0},{64,96},{96,64},{128,160},{160,128},{192,224},{224,1... | collective-permute-start | bytes 147464 | tf_op jit(solution)/shard_map/ppermute | solution.py:353
  27.8 5.1 %collective-permute-done.4.other_ref = f32[3,16,256]{2,1,0:T(8,128)S(1)} collective-permute-done((f32[3,16,256]{2,1,0:T(8,128)}, f32[3,16,256]{2,1,0:T(8,128)S(1)}, u32[]{:S(2)}, u32[]{:S(2)}) %collective-permute-start.4) | collective-permute-done | bytes 49184 | tf_op jit(solution)/shard_map/ppermute | solution.py:353
  33.0 0.0 copy-start.9
  33.0 0.6 %copy-done.9 = f32[3,16,256]{2,1,0:T(8,128)} copy-done((f32[3,16,256]{2,1,0:T(8,128)}, f32[3,16,256]{2,1,0:T(8,128)S(1)}, u32[]{:S(2)}) %copy-start.9) | copy-done | bytes 49176
  33.6 1.5 %join_pair.1.b0_ref = f32[5,16,256]{2,1,0:T(8,128)} custom-call(f32[3,16,256]{2,1,0:T(8,128)} %state_block.1.own_ref, f32[3,16,256]{2,1,0:T(8,128)} %copy-done.9), custom_call_target="tpu_custom_call" | custom-call | flops 100000 | bytes 100000 | tf_op jit(solution)/shard_map/join_pair/pallas_call | solution.py:359
  35.0 2.7 %collective-permute-start.5 = (f32[5,16,256]{2,1,0:T(8,128)}, f32[5,16,256]{2,1,0:T(8,128)S(1)}, u32[]{:S(2)}, u32[]{:S(2)}) collective-permute-start(f32[5,16,256]{2,1,0:T(8,128)} %join_pair.1.b0_ref), channel_id=1, source_target_pairs={{64,0},{96,32},{128,64},{160,96},{192,128},{224,160},{0,192},{32,2... | collective-permute-start | bytes 245768 | tf_op jit(solution)/shard_map/ppermute | solution.py:361
  37.8 0.3 collective-permute-start.6
  38.1 0.7 %collective-permute-start.7 = (f32[5,16,256]{2,1,0:T(8,128)}, f32[5,16,256]{2,1,0:T(8,128)S(1)}, u32[]{:S(2)}, u32[]{:S(2)}) collective-permute-start(f32[5,16,256]{2,1,0:T(8,128)} %join_pair.1.b0_ref), channel_id=1, source_target_pairs={{192,0},{224,32},{0,64},{32,96},{64,128},{96,160},{128,192},{160,2... | collective-permute-start | bytes 245768 | tf_op jit(solution)/shard_map/ppermute | solution.py:361
  38.8 1.8 %collective-permute-done.5.b1_ref = f32[5,16,256]{2,1,0:T(8,128)S(1)} collective-permute-done((f32[5,16,256]{2,1,0:T(8,128)}, f32[5,16,256]{2,1,0:T(8,128)S(1)}, u32[]{:S(2)}, u32[]{:S(2)}) %collective-permute-start.5) | collective-permute-done | bytes 81952 | tf_op jit(solution)/shard_map/ppermute | solution.py:361
  40.6 0.0 copy-start.4
  40.6 2.5 %collective-permute-done.6.b2_ref = f32[5,16,256]{2,1,0:T(8,128)S(1)} collective-permute-done((f32[5,16,256]{2,1,0:T(8,128)}, f32[5,16,256]{2,1,0:T(8,128)S(1)}, u32[]{:S(2)}, u32[]{:S(2)}) %collective-permute-start.6) | collective-permute-done | bytes 81952 | tf_op jit(solution)/shard_map/ppermute | solution.py:361
  43.1 0.0 copy-start.5
  43.1 0.9 %collective-permute-done.7.b3_ref = f32[5,16,256]{2,1,0:T(8,128)S(1)} collective-permute-done((f32[5,16,256]{2,1,0:T(8,128)}, f32[5,16,256]{2,1,0:T(8,128)S(1)}, u32[]{:S(2)}, u32[]{:S(2)}) %collective-permute-start.7) | collective-permute-done | bytes 81952 | tf_op jit(solution)/shard_map/ppermute | solution.py:361
  44.0 0.0 copy-done.4
  44.0 0.0 copy-done.5
  44.0 0.0 copy-start.6
  44.0 0.6 %copy-done.6 = f32[5,16,256]{2,1,0:T(8,128)} copy-done((f32[5,16,256]{2,1,0:T(8,128)}, f32[5,16,256]{2,1,0:T(8,128)S(1)}, u32[]{:S(2)}) %copy-start.6) | copy-done | bytes 81944
  44.6 1.8 %full_state.1 = (f32[17,16,256]{2,1,0:T(8,128)}, f32[9,8,256]{2,1,0:T(8,128)}, f32[9,8,256]{2,1,0:T(8,128)}) custom-call(f32[5,16,256]{2,1,0:T(8,128)} %join_pair.1.b0_ref, f32[5,16,256]{2,1,0:T(8,128)} %copy-done.4, f32[5,16,256]{2,1,0:T(8,128)} %copy-done.5, f32[5,16,256]{2,1,0:T(8,128)} %copy-done.6), custom_call_target="tpu_custom_call" | custom-call | flops 100000 | bytes 100000 | tf_op jit(solution)/shard_map/full_state/pallas_call | solution.py:363
  46.4 2.0 %collective-permute-start.8 = (f32[9,8,256]{2,1,0:T(8,128)}, f32[9,8,256]{2,1,0:T(8,128)S(1)}, u32[]{:S(2)}, u32[]{:S(2)}) collective-permute-start(f32[9,8,256]{2,1,0:T(8,128)} %get-tuple-element.12), channel_id=1, source_target_pairs={{4,0},{8,4},{12,8},{16,12},{20,16},{24,20},{28,24},{5,1},{9,5},{13... | collective-permute-start | bytes 221192 | tf_op jit(solution)/shard_map/ppermute | solution.py:366
  48.5 3.5 %collective-permute-start.9 = (f32[9,8,256]{2,1,0:T(8,128)}, f32[9,8,256]{2,1,0:T(8,128)S(1)}, u32[]{:S(2)}, u32[]{:S(2)}) collective-permute-start(f32[9,8,256]{2,1,0:T(8,128)} %get-tuple-element.13), channel_id=1, source_target_pairs={{0,4},{4,8},{8,12},{12,16},{16,20},{20,24},{24,28},{1,5},{5,9},{9,... | collective-permute-start | bytes 221192 | tf_op jit(solution)/shard_map/ppermute | solution.py:367
  52.7 0.0 collective-permute-done.8.snorth_ref
  52.7 0.0 copy-start.7
  52.7 1.0 %collective-permute-done.9.ssouth_ref = f32[9,8,256]{2,1,0:T(8,128)S(1)} collective-permute-done((f32[9,8,256]{2,1,0:T(8,128)}, f32[9,8,256]{2,1,0:T(8,128)S(1)}, u32[]{:S(2)}, u32[]{:S(2)}) %collective-permute-start.9) | collective-permute-done | bytes 73760 | tf_op jit(solution)/shard_map/ppermute | solution.py:367
  53.7 0.0 copy-start.8
  53.7 0.0 collective-permute-done.2.north_ref
  53.7 0.0 copy-start
  53.7 0.0 collective-permute-done.3.south_ref
  53.7 0.0 copy-start.1
  53.7 0.0 copy-done.7
  53.7 0.6 copy-done.8
  54.3 0.1 copy-done
  54.5 0.2 copy-done.1
  54.6 6.8 %advance.1 = (f32[1,16,16,256]{3,2,1,0:T(8,128)}, f32[2,16,256]{2,1,0:T(8,128)}) custom-call(s32[1]{0:T(128)S(6)} %copy.10.seed_ref, f32[16,16]{1,0:T(8,128)} %table_ref.1, f32[16]{0:T(128)} %visc_ref.1, f32[16]{0:T(128)} %rate_ref.1, f32[1,16,16,256]{3,2,1,0:T(8,128)} %delta_ref.5, bf16[4,2,16,16,256]{4,3,2,1,0:T(8,128)(2,1)} %speeds_ref.5, ...), custom_call_target="tpu_custom_call" | custom-call | flops 10000000 | bytes 10000000 | tf_op jit(solution)/shard_map/advance/pallas_call | solution.py:369
Async XLA Ops:
  3.2 5.4 %collective-permute-start = (f32[11,16,128]{2,1,0:T(8,128)}, f32[11,16,128]{2,1,0:T(8,128)S(1)}, u32[]{:S(2)}, u32[]{:S(2)}) collective-permute-start(f32[11,16,128]{2,1,0:T(8,128)} %pack_columns.1.own_ref), channel_id=1, source_target_pairs={{0,1},{1,2},{2,3},{3,0},{4,5},{5,6},{6,7},{7,4},{8,9},{9,10},{10,1... | collective-permute-start | bytes 270344 | tf_op jit(solution)/shard_map/ppermute | solution.py:348
  5.2 3.6 %collective-permute-start.1 = (f32[11,16,128]{2,1,0:T(8,128)}, f32[11,16,128]{2,1,0:T(8,128)S(1)}, u32[]{:S(2)}, u32[]{:S(2)}) collective-permute-start(f32[11,16,128]{2,1,0:T(8,128)} %pack_columns.1.own_ref), channel_id=1, source_target_pairs={{1,0},{2,1},{3,2},{0,3},{5,4},{6,5},{7,6},{4,7},{9,8},{10,9},{11,1... | collective-permute-start | bytes 270344 | tf_op jit(solution)/shard_map/ppermute | solution.py:349
  8.6 0.6 %copy-start.2 = (f32[11,16,128]{2,1,0:T(8,128)}, f32[11,16,128]{2,1,0:T(8,128)S(1)}, u32[]{:S(2)}) copy-start(f32[11,16,128]{2,1,0:T(8,128)S(1)} %collective-permute-done.west_ref) | copy-start | bytes 270340
  9.3 0.6 %copy-start.3 = (f32[11,16,128]{2,1,0:T(8,128)}, f32[11,16,128]{2,1,0:T(8,128)S(1)}, u32[]{:S(2)}) copy-start(f32[11,16,128]{2,1,0:T(8,128)S(1)} %collective-permute-done.1.east_ref) | copy-start | bytes 270340
  12.8 40.9 %collective-permute-start.2 = (f32[17,24,256]{2,1,0:T(8,128)}, f32[17,24,256]{2,1,0:T(8,128)S(1)}, u32[]{:S(2)}, u32[]{:S(2)}) collective-permute-start(f32[17,24,256]{2,1,0:T(8,128)} %get-tuple-element.9), channel_id=1, source_target_pairs={{4,0},{8,4},{12,8},{16,12},{20,16},{24,20},{28,24},{5,1},{9,5},{13... | collective-permute-start | bytes 1253384 | tf_op jit(solution)/shard_map/ppermute | solution.py:357
  18.4 35.3 %collective-permute-start.3 = (f32[17,24,256]{2,1,0:T(8,128)}, f32[17,24,256]{2,1,0:T(8,128)S(1)}, u32[]{:S(2)}, u32[]{:S(2)}) collective-permute-start(f32[17,24,256]{2,1,0:T(8,128)} %get-tuple-element.10), channel_id=1, source_target_pairs={{0,4},{4,8},{8,12},{12,16},{16,20},{20,24},{24,28},{1,5},{5,9},{9,... | collective-permute-start | bytes 1253384 | tf_op jit(solution)/shard_map/ppermute | solution.py:358
  22.0 11.0 %collective-permute-start.4 = (f32[3,16,256]{2,1,0:T(8,128)}, f32[3,16,256]{2,1,0:T(8,128)S(1)}, u32[]{:S(2)}, u32[]{:S(2)}) collective-permute-start(f32[3,16,256]{2,1,0:T(8,128)} %state_block.1.own_ref), channel_id=1, source_target_pairs={{0,32},{32,0},{64,96},{96,64},{128,160},{160,128},{192,224},{224,1... | collective-permute-start | bytes 147464 | tf_op jit(solution)/shard_map/ppermute | solution.py:353
  33.0 0.6 %copy-start.9 = (f32[3,16,256]{2,1,0:T(8,128)}, f32[3,16,256]{2,1,0:T(8,128)S(1)}, u32[]{:S(2)}) copy-start(f32[3,16,256]{2,1,0:T(8,128)S(1)} %collective-permute-done.4.other_ref) | copy-start | bytes 147460
  35.0 5.6 %collective-permute-start.5 = (f32[5,16,256]{2,1,0:T(8,128)}, f32[5,16,256]{2,1,0:T(8,128)S(1)}, u32[]{:S(2)}, u32[]{:S(2)}) collective-permute-start(f32[5,16,256]{2,1,0:T(8,128)} %join_pair.1.b0_ref), channel_id=1, source_target_pairs={{64,0},{96,32},{128,64},{160,96},{192,128},{224,160},{0,192},{32,2... | collective-permute-start | bytes 245768 | tf_op jit(solution)/shard_map/ppermute | solution.py:361
  37.8 5.3 %collective-permute-start.6 = (f32[5,16,256]{2,1,0:T(8,128)}, f32[5,16,256]{2,1,0:T(8,128)S(1)}, u32[]{:S(2)}, u32[]{:S(2)}) collective-permute-start(f32[5,16,256]{2,1,0:T(8,128)} %join_pair.1.b0_ref), channel_id=1, source_target_pairs={{128,0},{160,32},{192,64},{224,96},{0,128},{32,160},{64,192},{96,2... | collective-permute-start | bytes 245768 | tf_op jit(solution)/shard_map/ppermute | solution.py:361
  38.1 5.9 %collective-permute-start.7 = (f32[5,16,256]{2,1,0:T(8,128)}, f32[5,16,256]{2,1,0:T(8,128)S(1)}, u32[]{:S(2)}, u32[]{:S(2)}) collective-permute-start(f32[5,16,256]{2,1,0:T(8,128)} %join_pair.1.b0_ref), channel_id=1, source_target_pairs={{192,0},{224,32},{0,64},{32,96},{64,128},{96,160},{128,192},{160,2... | collective-permute-start | bytes 245768 | tf_op jit(solution)/shard_map/ppermute | solution.py:361
  40.6 3.4 %copy-start.4 = (f32[5,16,256]{2,1,0:T(8,128)}, f32[5,16,256]{2,1,0:T(8,128)S(1)}, u32[]{:S(2)}) copy-start(f32[5,16,256]{2,1,0:T(8,128)S(1)} %collective-permute-done.5.b1_ref) | copy-start | bytes 245764
  43.1 0.9 %copy-start.5 = (f32[5,16,256]{2,1,0:T(8,128)}, f32[5,16,256]{2,1,0:T(8,128)S(1)}, u32[]{:S(2)}) copy-start(f32[5,16,256]{2,1,0:T(8,128)S(1)} %collective-permute-done.6.b2_ref) | copy-start | bytes 245764
  44.0 0.6 %copy-start.6 = (f32[5,16,256]{2,1,0:T(8,128)}, f32[5,16,256]{2,1,0:T(8,128)S(1)}, u32[]{:S(2)}) copy-start(f32[5,16,256]{2,1,0:T(8,128)S(1)} %collective-permute-done.7.b3_ref) | copy-start | bytes 245764
  46.4 6.2 %collective-permute-start.8 = (f32[9,8,256]{2,1,0:T(8,128)}, f32[9,8,256]{2,1,0:T(8,128)S(1)}, u32[]{:S(2)}, u32[]{:S(2)}) collective-permute-start(f32[9,8,256]{2,1,0:T(8,128)} %get-tuple-element.12), channel_id=1, source_target_pairs={{4,0},{8,4},{12,8},{16,12},{20,16},{24,20},{28,24},{5,1},{9,5},{13... | collective-permute-start | bytes 221192 | tf_op jit(solution)/shard_map/ppermute | solution.py:366
  48.5 5.3 %collective-permute-start.9 = (f32[9,8,256]{2,1,0:T(8,128)}, f32[9,8,256]{2,1,0:T(8,128)S(1)}, u32[]{:S(2)}, u32[]{:S(2)}) collective-permute-start(f32[9,8,256]{2,1,0:T(8,128)} %get-tuple-element.13), channel_id=1, source_target_pairs={{0,4},{4,8},{8,12},{12,16},{16,20},{20,24},{24,28},{1,5},{5,9},{9,... | collective-permute-start | bytes 221192 | tf_op jit(solution)/shard_map/ppermute | solution.py:367
  52.7 1.1 %copy-start.7 = (f32[9,8,256]{2,1,0:T(8,128)}, f32[9,8,256]{2,1,0:T(8,128)S(1)}, u32[]{:S(2)}) copy-start(f32[9,8,256]{2,1,0:T(8,128)S(1)} %collective-permute-done.8.snorth_ref) | copy-start | bytes 221188
  53.7 0.6 %copy-start.8 = (f32[9,8,256]{2,1,0:T(8,128)}, f32[9,8,256]{2,1,0:T(8,128)S(1)}, u32[]{:S(2)}) copy-start(f32[9,8,256]{2,1,0:T(8,128)S(1)} %collective-permute-done.9.ssouth_ref) | copy-start | bytes 221188
  53.7 0.8 %copy-start = (f32[17,24,256]{2,1,0:T(8,128)}, f32[17,24,256]{2,1,0:T(8,128)S(1)}, u32[]{:S(2)}) copy-start(f32[17,24,256]{2,1,0:T(8,128)S(1)} %collective-permute-done.2.north_ref) | copy-start | bytes 1253380
  53.7 0.9 %copy-start.1 = (f32[17,24,256]{2,1,0:T(8,128)}, f32[17,24,256]{2,1,0:T(8,128)S(1)}, u32[]{:S(2)}) copy-start(f32[17,24,256]{2,1,0:T(8,128)S(1)} %collective-permute-done.3.south_ref) | copy-start | bytes 1253380

commit v2 on v1

--- a/solution.py
+++ b/solution.py
@@ -1,11 +1,10 @@
-import functools
-
 import jax
 import jax.numpy as jnp
 from jax import lax
 from jax.experimental import pallas as pl
 from jax.experimental.pallas import tpu as pltpu
 from jax.sharding import PartitionSpec as P
+
 
 F32 = jnp.float32
 I32 = jnp.int32
@@ -43,30 +42,21 @@
     return [upwind_ref[step, lev, rows_at(r), cols_at(c)].astype(F32) for r in range(2)]
 
 
-def pack_columns(delta_ref, speeds_ref, upwind_ref, state_ref, out_ref):
+def slot(acc, left, right, lev):
     lane = lanes()
+    edge = pltpu.roll(jnp.where(lane < 64, left, right), 8 * lev + 4, 1)
+    return jnp.where(lane // 8 == lev, edge, acc)
+
+
+def pack_columns(delta_ref, speeds_ref, upwind_ref, out_ref):
     for a in range(NCD):
         acc = [jnp.zeros((8, 128), F32)] * 2
         for lev in range(LEV):
             left = own_tiles(delta_ref, speeds_ref, upwind_ref, a, lev, 0)
             right = own_tiles(delta_ref, speeds_ref, upwind_ref, a, lev, 1)
-            for r in range(2):
-                edge = jnp.where(lane < 64, left[r], right[r])
-                edge = pltpu.roll(edge, 8 * lev + 4 if 8 * lev + 4 < 128 else 8 * lev + 4 - 128, 1)
-                acc[r] = jnp.where(lane // 8 == lev, edge, acc[r])
+            acc = [slot(acc[r], left[r], right[r], lev) for r in range(2)]
         for r in range(2):
             out_ref[a, rows_at(r), :] = acc[r]
-    first = 2 * lax.axis_index("ens")
-    acc = [jnp.zeros((8, 128), F32)] * 2
-    for i in range(2):
-        for r in range(2):
-            edge = jnp.where(
-                lane < 64, state_ref[i, rows_at(r), cols_at(0)], state_ref[i, rows_at(r), cols_at(1)]
-            )
-            edge = pltpu.roll(edge, 8 * (first + i) + 4, 1)
-            acc[r] = jnp.where(lane // 8 == first + i, edge, acc[r])
-    for r in range(2):
-        out_ref[NCD, rows_at(r), :] = acc[r]
 
 
 def strip_tile(own_ref, west_ref, east_ref, a, r, c):
@@ -77,18 +67,10 @@
     return jnp.where(half, own, east_ref[a, rows_at(r), :])
 
 
-def state_block(state_ref, own_ref, west_ref, east_ref, out_ref):
-    out_ref[0:2] = state_ref[...]
-    for r in range(2):
-        for c in range(2):
-            out_ref[2, rows_at(r), cols_at(c)] = strip_tile(own_ref, west_ref, east_ref, NCD, r, c)
-
-
 def join_pair(own_ref, other_ref, out_ref):
     half = lax.rem(lax.axis_index("ens"), 2)
-    out_ref[pl.ds(2 * half, 2)] = own_ref[0:2]
-    out_ref[pl.ds(2 - 2 * half, 2)] = other_ref[0:2]
-    out_ref[4] = own_ref[2] + other_ref[2]
+    out_ref[pl.ds(2 * half, 2)] = own_ref[...]
+    out_ref[pl.ds(2 - 2 * half, 2)] = other_ref[...]
 
 
 def merge_rows(pieces):
@@ -134,21 +116,31 @@
     lax.fori_loop(0, LEV, body, 0)
 
 
-def full_state(b0_ref, b1_ref, b2_ref, b3_ref, out_ref, down_ref, up_ref):
+def join_all(b0_ref, b1_ref, b2_ref, b3_ref, out_ref, columns_ref):
     mine = lax.axis_index("ens") // 2
-    blocks = (b0_ref, b1_ref, b2_ref, b3_ref)
-    for ahead in range(4):
-        out_ref[pl.ds(4 * lax.rem(mine + ahead, 4), 4)] = blocks[ahead][0:4]
-    out_ref[LEV] = (b0_ref[4] + b1_ref[4]) + (b2_ref[4] + b3_ref[4])
+    acc = [jnp.zeros((8, 128), F32)] * 2
+    for ahead, ref in enumerate((b0_ref, b1_ref, b2_ref, b3_ref)):
+        base = 4 * lax.rem(mine + ahead, 4)
+        out_ref[pl.ds(base, 4)] = ref[...]
+        for i in range(4):
+            for r in range(2):
+                left, right = (ref[i, rows_at(r), cols_at(c)] for c in range(2))
+                acc[r] = slot(acc[r], left, right, base + i)
+    for r in range(2):
+        columns_ref[0, rows_at(r), :] = acc[r]
+
+
+def state_rows(state_ref, own_ref, west_ref, east_ref, strip_ref, down_ref, up_ref):
     low = subs() < 4
-    for p in range(9):
-        for c in range(2):
-            a0, a1 = out_ref[2 * p, rows_at(0), cols_at(c)], out_ref[2 * p, rows_at(1), cols_at(c)]
-            if p < 8:
-                b0 = pltpu.roll(out_ref[2 * p + 1, rows_at(0), cols_at(c)], 4, 0)
-                b1 = pltpu.roll(out_ref[2 * p + 1, rows_at(1), cols_at(c)], 4, 0)
-            else:
-                b0, b1 = a0, a1
+    for c in range(2):
+        pair = [strip_tile(own_ref, west_ref, east_ref, 0, r, c) for r in range(2)]
+        for r in range(2):
+            strip_ref[rows_at(r), cols_at(c)] = pair[r]
+        down_ref[8, :, cols_at(c)] = pair[0]
+        up_ref[8, :, cols_at(c)] = pair[1]
+        for p in range(8):
+            a0, a1 = (state_ref[2 * p, rows_at(r), cols_at(c)] for r in range(2))
+            b0, b1 = (pltpu.roll(state_ref[2 * p + 1, rows_at(r), cols_at(c)], 4, 0) for r in range(2))
             down_ref[p, :, cols_at(c)] = jnp.where(low, a0, b0)
             up_ref[p, :, cols_at(c)] = jnp.where(low, b1, a1)
 
@@ -156,7 +148,7 @@
 def advance(
     seed_ref, table_ref, visc_ref, rate_ref,
     delta_ref, speeds_ref, upwind_ref, strip_ref, north_ref, south_ref,
-    state_ref, snorth_ref, ssouth_ref,
+    state_ref, state_strip_ref, snorth_ref, ssouth_ref,
     delta_out, state_out,
     edge_state, edge_delta, finals,
 ):
@@ -273,7 +265,7 @@
                 edge_state[step, c, rows_at(r), :] = state[r][c]
                 edge_delta[step, c, rows_at(r), :] = delta[r][c]
 
-    state = [[state_ref[LEV, rows_at(r), cols_at(c)] for c in range(2)] for r in range(2)]
+    state = [[state_strip_ref[rows_at(r), cols_at(c)] for c in range(2)] for r in range(2)]
     state.append([halo_state(8, False, c) for c in range(2)])
     delta = [[strip_ref[0, rows_at(r), cols_at(c)] * amp for c in range(2)] for r in range(2)]
     delta.append([halo_delta(LEV, c) * amp for c in range(2)])
@@ -321,16 +313,16 @@
     state_out[...] = finals[pl.ds(first, 2)]
 
 
-def call(kernel, name, shapes, specs, scratch=(), cost=None):
+def call(kernel, shapes, specs, scratch=(), cost=None):
     out = [jax.ShapeDtypeStruct(shape, F32) for shape in shapes]
     single = len(out) == 1
     return pl.pallas_call(
         kernel,
-        name=name,
         out_shape=out[0] if single else out,
         in_specs=specs,
         out_specs=VMEM if single else [VMEM] * len(out),
         scratch_shapes=scratch,
+        compiler_params=pltpu.CompilerParams(vmem_limit_bytes=12 * 2**20),
         cost_estimate=pl.CostEstimate(flops=cost or 100000, bytes_accessed=cost or 100000, transcendentals=0),
     )
 
@@ -342,41 +334,41 @@
     eastward = [(i, (i + 1) % n_lon) for i in range(n_lon)]
     westward = [(j, i) for i, j in eastward]
 
-    columns = call(pack_columns, "pack_columns", [(NCD + 1, 16, 128)], [VMEM] * 4)(
-        perturbation, speeds, upwind, start_state
-    )
+    def run(kernel, shapes, specs, *args):
+        return call(kernel, shapes, specs)(*args)
+
+    other = lax.ppermute(start_state, "ens", [(i, i ^ 1) for i in range(n_ens)])
+    columns = run(pack_columns, [(NCD, 16, 128)], [VMEM] * 3, perturbation, speeds, upwind)
     from_west = lax.ppermute(columns, "lon", eastward)
     from_east = lax.ppermute(columns, "lon", westward)
-    block = call(state_block, "state_block", [(3, 16, 256)], [VMEM] * 4)(
-        start_state, columns, from_west, from_east
-    )
-    other = lax.ppermute(block, "ens", [(i, i ^ 1) for i in range(n_ens)])
-    strips, down, up = call(
-        pack_rows, "pack_rows", [(NCD, 16, 256), (LEV + 1, 24, 256), (LEV + 1, 24, 256)], [VMEM] * 6
-    )(perturbation, speeds, upwind, columns, from_west, from_east)
+    quad = run(join_pair, [(4, 16, 256)], [VMEM] * 2, start_state, other)
+    ahead = [lax.ppermute(quad, "ens", [((i + 2 * j) % n_ens, i) for i in range(n_ens)]) for j in (1, 2, 3)]
+    strips, down, up = run(
+        pack_rows, [(NCD, 16, 256), (LEV + 1, 24, 256), (LEV + 1, 24, 256)], [VMEM] * 6,
+        perturbation, speeds, upwind, columns, from_west, from_east,
+    )
     cd_north = lax.ppermute(down, "lat", south)
     cd_south = lax.ppermute(up, "lat", north)
-    quad = call(join_pair, "join_pair", [(5, 16, 256)], [VMEM] * 2)(block, other)
-    ahead = [
-        lax.ppermute(quad, "ens", [((i + 2 * j) % n_ens, i) for i in range(n_ens)]) for j in (1, 2, 3)
-    ]
-    states, state_down, state_up = call(
-        full_state, "full_state", [(LEV + 1, 16, 256), (9, 8, 256), (9, 8, 256)], [VMEM] * 4
-    )(quad, *ahead)
+    states, state_columns = run(join_all, [(LEV, 16, 256), (1, 16, 128)], [VMEM] * 4, quad, *ahead)
+    state_west = lax.ppermute(state_columns, "lon", eastward)
+    state_east = lax.ppermute(state_columns, "lon", westward)
+    state_strip, state_down, state_up = run(
+        state_rows, [(16, 256), (9, 8, 256), (9, 8, 256)], [VMEM] * 4,
+        states, state_columns, state_west, state_east,
+    )
     st_north = lax.ppermute(state_down, "lat", south)
     st_south = lax.ppermute(state_up, "lat", north)
     edge = pltpu.VMEM((STEPS, 2, 24, 128), F32)
     return call(
         advance,
-        "advance",
         [(1, LEV, 16, 256), (2, 16, 256)],
-        [SMEM] * 4 + [VMEM] * 9,
+        [SMEM] * 4 + [VMEM] * 10,
         scratch=[edge, edge, pltpu.VMEM((LEV, 16, 256), F32)],
         cost=10000000,
     )(
         seed_ids, amp_table, viscosity, reaction,
         perturbation, speeds, upwind, strips, cd_north, cd_south,
-        states, st_north, st_south,
+        states, state_strip, st_north, st_south,
     )
 
 

time: 61.8 us -> 55.9 us (0.905)
  Pallas kernels: 17.1 us -> 6.15 us
  starting transfers between devices: 26 us -> 29.3 us
  waiting for transfers between devices: 13.7 us -> 14.6 us
  local copies, waits for them, and re-layouts: 3.23 us -> 4.06 us
    pallas_call x6, Pallas kernels: 17.1 us -> 6.15 us  [the longest x1 5.39 us: per_device(): call(advance, [(1, LEV, 16, 256), (2, 16, 256)], [SMEM] * 4 + [VMEM] * 10...]
    ppermute x1 -> x3, starting transfers between devices: 5.83 us -> 8.94 us  [the longest x1 6.1 us: per_device(): other = lax.ppermute(start_state, 'ens', [(i, i ^ 1) for i in range(n_ens)])]
    ppermute x1 -> x3, waiting for transfers between devices: 5.15 us -> 7.66 us  [the longest x1 6.71 us: per_device(): other = lax.ppermute(start_state, 'ens', [(i, i ^ 1) for i in range(n_ens)])]
    ppermute x3, waiting for transfers between devices: 5.16 us -> 4.28 us  [per_device(): lax.ppermute(quad, 'ens', [((i + 2 * j) % n_ens, i) for i in range(n_ens)])]
    unnamed x20 -> x18, local copies, waits for them, and re-layouts: 3.23 us -> 4.06 us
  transfers between devices with their start and end apart: 10 -> 12, of which waited for: 7 -> 8; matrix products, arithmetic and copies ran while one was open for 0% -> 0% of each run, Pallas kernels for 8% -> 0%
where the time goes in v2:
time: 55.9 us; the launch traced here: 55.5 us
  starting transfers between devices  29.3 us (52%)
  waiting for transfers between devices  14.6 us (26%)
  Pallas kernels  6.15 us (11%)
  local copies, waits for them, and re-layouts  4.06 us (7%)
  between operations  1.43 us (3%)
    ppermute x1, waiting for transfers between devices, per_device(): other = lax.ppermute(start_state, 'ens', [(i, i ^ 1) for i in range(n_ens)])  6.71 us
    ppermute x1, starting transfers between devices, per_device(): other = lax.ppermute(start_state, 'ens', [(i, i ^ 1) for i in range(n_ens)])  6.1 us
    ppermute x1, starting transfers between devices, per_device(): cd_north = lax.ppermute(down, 'lat', south)  5.44 us
    pallas_call x1, Pallas kernels, per_device(): call(advance, [(1, LEV, 16, 256), (2, 16, 256)], [SMEM] * 4 + [VMEM] * 10...  5.39 us
    ppermute x3, waiting for transfers between devices, per_device(): lax.ppermute(quad, 'ens', [((i + 2 * j) % n_ens, i) for i in range(n_ens)])  4.28 us
    unnamed x18, local copies, waits for them, and re-layouts  4.06 us
    ppermute x3, starting transfers between devices, per_device(): lax.ppermute(quad, 'ens', [((i + 2 * j) % n_ens, i) for i in range(n_ens)])  3.85 us
    ppermute x1, starting transfers between devices, per_device(): st_south = lax.ppermute(state_up, 'lat', north)  3.64 us
  transfers between devices with their start and end apart: 12, of which 8 were waited for; matrix products, arithmetic and copies ran while one was open for 0% of the time, Pallas kernels for 0%

profile of v2, /device:TPU:1, one launch (start us, length us, event | category | flops | bytes accessed | tf_op | source)
XLA Modules:
  0.0 55.5 jit_solution(17608042896567843968)
XLA Ops:
  0.6 0.0 copy-start
  0.6 1.2 %copy-done = bf16[4,2,16,16,256]{4,3,2,1,0:T(8,128)(2,1)S(1)} copy-done((bf16[4,2,16,16,256]{4,3,2,1,0:T(8,128)(2,1)S(1)}, bf16[4,2,16,16,256]{4,3,2,1,0:T(8,128)(2,1)}, u32[]{:S(2)}) %copy-start) | copy-done | bytes 1048600
  1.9 0.0 copy-start.2
  1.9 1.2 %copy-done.2 = s32[4,16,16,256]{3,2,1,0:T(8,128)S(1)} copy-done((s32[4,16,16,256]{3,2,1,0:T(8,128)S(1)}, s32[4,16,16,256]{3,2,1,0:T(8,128)}, u32[]{:S(2)}) %copy-start.2) | copy-done | bytes 1048600
  3.1 0.0 copy-start.3
  3.1 0.9 %copy-done.3 = f32[1,16,16,256]{3,2,1,0:T(8,128)S(1)} copy-done((f32[1,16,16,256]{3,2,1,0:T(8,128)S(1)}, f32[1,16,16,256]{3,2,1,0:T(8,128)}, u32[]{:S(2)}) %copy-start.3) | copy-done | bytes 262168
  4.0 0.3 shard_map.95.own_ref
  4.3 0.0 copy-start.5
  4.4 0.0 copy-start.1
  4.4 2.1 %collective-permute-start = (f32[10,16,128]{2,1,0:T(8,128)S(1)}, f32[10,16,128]{2,1,0:T(8,128)S(1)}, u32[]{:S(2)}, u32[]{:S(2)}) collective-permute-start(f32[10,16,128]{2,1,0:T(8,128)S(1)} %shard_map.95.own_ref), channel_id=1, source_target_pairs={{0,1},{1,2},{2,3},{3,0},{4,5},{5,6},{6,7},{7,4},{8,9},{9,10},{10,1... | collective-permute-start | bytes 245768 | tf_op jit(solution)/shard_map/ppermute | solution.py:342
  6.5 1.4 %collective-permute-start.1 = (f32[10,16,128]{2,1,0:T(8,128)S(1)}, f32[10,16,128]{2,1,0:T(8,128)S(1)}, u32[]{:S(2)}, u32[]{:S(2)}) collective-permute-start(f32[10,16,128]{2,1,0:T(8,128)S(1)} %shard_map.95.own_ref), channel_id=1, source_target_pairs={{1,0},{2,1},{3,2},{0,3},{5,4},{6,5},{7,6},{4,7},{9,8},{10,9},{11,1... | collective-permute-start | bytes 245768 | tf_op jit(solution)/shard_map/ppermute | solution.py:343
  7.8 1.7 %collective-permute-done.west_ref = f32[10,16,128]{2,1,0:T(8,128)S(1)} collective-permute-done((f32[10,16,128]{2,1,0:T(8,128)S(1)}, f32[10,16,128]{2,1,0:T(8,128)S(1)}, u32[]{:S(2)}, u32[]{:S(2)}) %collective-permute-start) | collective-permute-done | bytes 81952 | tf_op jit(solution)/shard_map/ppermute | solution.py:342
  9.6 0.2 collective-permute-done.1.east_ref
  9.8 0.3 shard_map.96
  10.1 5.4 %collective-permute-start.2 = (f32[17,24,256]{2,1,0:T(8,128)S(1)}, f32[17,24,256]{2,1,0:T(8,128)S(1)}, u32[]{:S(2)}, u32[]{:S(2)}) collective-permute-start(f32[17,24,256]{2,1,0:T(8,128)S(1)} %get-tuple-element.11), channel_id=1, source_target_pairs={{4,0},{8,4},{12,8},{16,12},{20,16},{24,20},{28,24},{5,1},{9,5},{13... | collective-permute-start | bytes 1253384 | tf_op jit(solution)/shard_map/ppermute | solution.py:350
  15.5 2.0 %collective-permute-start.3 = (f32[17,24,256]{2,1,0:T(8,128)S(1)}, f32[17,24,256]{2,1,0:T(8,128)S(1)}, u32[]{:S(2)}, u32[]{:S(2)}) collective-permute-start(f32[17,24,256]{2,1,0:T(8,128)S(1)} %get-tuple-element.12), channel_id=1, source_target_pairs={{0,4},{4,8},{8,12},{12,16},{16,20},{20,24},{24,28},{1,5},{5,9},{9,... | collective-permute-start | bytes 1253384 | tf_op jit(solution)/shard_map/ppermute | solution.py:351
  17.6 0.0 copy-done.5
  17.6 6.1 %collective-permute-start.4 = (f32[2,16,256]{2,1,0:T(8,128)S(1)}, f32[2,16,256]{2,1,0:T(8,128)S(1)}, u32[]{:S(2)}, u32[]{:S(2)}) collective-permute-start(f32[2,16,256]{2,1,0:T(8,128)S(1)} %copy-done.5), channel_id=1, source_target_pairs={{0,32},{32,0},{64,96},{96,64},{128,160},{160,128},{192,224},{224,1... | collective-permute-start | bytes 98312 | tf_op jit(solution)/shard_map/ppermute | solution.py:340
  23.7 6.7 %collective-permute-done.4.other_ref = f32[2,16,256]{2,1,0:T(8,128)S(1)} collective-permute-done((f32[2,16,256]{2,1,0:T(8,128)S(1)}, f32[2,16,256]{2,1,0:T(8,128)S(1)}, u32[]{:S(2)}, u32[]{:S(2)}) %collective-permute-start.4) | collective-permute-done | bytes 32800 | tf_op jit(solution)/shard_map/ppermute | solution.py:340
  30.4 0.0 copy-start.4
  30.4 2.8 %collective-permute-start.5 = (f32[4,16,256]{2,1,0:T(8,128)S(1)}, f32[4,16,256]{2,1,0:T(8,128)S(1)}, u32[]{:S(2)}, u32[]{:S(2)}) collective-permute-start(f32[4,16,256]{2,1,0:T(8,128)S(1)} %shard_map.97.b0_ref), channel_id=1, source_target_pairs={{64,0},{96,32},{128,64},{160,96},{192,128},{224,160},{0,192},{32,2... | collective-permute-start | bytes 196616 | tf_op jit(solution)/shard_map/ppermute | solution.py:345
  33.2 0.3 collective-permute-start.6
  33.6 0.7 %collective-permute-start.7 = (f32[4,16,256]{2,1,0:T(8,128)S(1)}, f32[4,16,256]{2,1,0:T(8,128)S(1)}, u32[]{:S(2)}, u32[]{:S(2)}) collective-permute-start(f32[4,16,256]{2,1,0:T(8,128)S(1)} %shard_map.97.b0_ref), channel_id=1, source_target_pairs={{192,0},{224,32},{0,64},{32,96},{64,128},{96,160},{128,192},{160,2... | collective-permute-start | bytes 196616 | tf_op jit(solution)/shard_map/ppermute | solution.py:345
  34.2 0.3 collective-permute-done.5.b1_ref
  34.5 3.4 %collective-permute-done.6.b2_ref = f32[4,16,256]{2,1,0:T(8,128)S(1)} collective-permute-done((f32[4,16,256]{2,1,0:T(8,128)S(1)}, f32[4,16,256]{2,1,0:T(8,128)S(1)}, u32[]{:S(2)}, u32[]{:S(2)}) %collective-permute-start.6) | collective-permute-done | bytes 65568 | tf_op jit(solution)/shard_map/ppermute | solution.py:345
  37.9 0.6 %collective-permute-done.7.b3_ref = f32[4,16,256]{2,1,0:T(8,128)S(1)} collective-permute-done((f32[4,16,256]{2,1,0:T(8,128)S(1)}, f32[4,16,256]{2,1,0:T(8,128)S(1)}, u32[]{:S(2)}, u32[]{:S(2)}) %collective-permute-start.7) | collective-permute-done | bytes 65568 | tf_op jit(solution)/shard_map/ppermute | solution.py:345
  38.5 0.1 shard_map.98
  38.6 1.3 %collective-permute-start.8 = (f32[1,16,128]{2,1,0:T(8,128)S(1)}, f32[1,16,128]{2,1,0:T(8,128)S(1)}, u32[]{:S(2)}, u32[]{:S(2)}) collective-permute-start(f32[1,16,128]{2,1,0:T(8,128)S(1)} %get-tuple-element.14.own_ref), channel_id=1, source_target_pairs={{0,1},{1,2},{2,3},{3,0},{4,5},{5,6},{6,7},{7,4},{8,9},{9,10},{10,1... | collective-permute-start | bytes 24584 | tf_op jit(solution)/shard_map/ppermute | solution.py:353
  39.9 1.6 %collective-permute-start.9 = (f32[1,16,128]{2,1,0:T(8,128)S(1)}, f32[1,16,128]{2,1,0:T(8,128)S(1)}, u32[]{:S(2)}, u32[]{:S(2)}) collective-permute-start(f32[1,16,128]{2,1,0:T(8,128)S(1)} %get-tuple-element.14.own_ref), channel_id=1, source_target_pairs={{1,0},{2,1},{3,2},{0,3},{5,4},{6,5},{7,6},{4,7},{9,8},{10,9},{11,1... | collective-permute-start | bytes 24584 | tf_op jit(solution)/shard_map/ppermute | solution.py:354
  41.5 0.9 %collective-permute-done.8.west_ref = f32[1,16,128]{2,1,0:T(8,128)S(1)} collective-permute-done((f32[1,16,128]{2,1,0:T(8,128)S(1)}, f32[1,16,128]{2,1,0:T(8,128)S(1)}, u32[]{:S(2)}, u32[]{:S(2)}) %collective-permute-start.8) | collective-permute-done | bytes 8224 | tf_op jit(solution)/shard_map/ppermute | solution.py:353
  42.4 0.0 collective-permute-done.9.east_ref
  42.5 0.0 copy-start.6
  42.5 1.9 %collective-permute-start.10 = (f32[9,8,256]{2,1,0:T(8,128)S(1)}, f32[9,8,256]{2,1,0:T(8,128)S(1)}, u32[]{:S(2)}, u32[]{:S(2)}) collective-permute-start(f32[9,8,256]{2,1,0:T(8,128)S(1)} %get-tuple-element.16), channel_id=1, source_target_pairs={{4,0},{8,4},{12,8},{16,12},{20,16},{24,20},{28,24},{5,1},{9,5},{13... | collective-permute-start | bytes 221192 | tf_op jit(solution)/shard_map/ppermute | solution.py:359
  44.4 3.6 %collective-permute-start.11 = (f32[9,8,256]{2,1,0:T(8,128)S(1)}, f32[9,8,256]{2,1,0:T(8,128)S(1)}, u32[]{:S(2)}, u32[]{:S(2)}) collective-permute-start(f32[9,8,256]{2,1,0:T(8,128)S(1)} %get-tuple-element.17), channel_id=1, source_target_pairs={{0,4},{4,8},{8,12},{12,16},{16,20},{20,24},{24,28},{1,5},{5,9},{9,... | collective-permute-start | bytes 221192 | tf_op jit(solution)/shard_map/ppermute | solution.py:360
  48.7 0.0 collective-permute-done.10.snorth_ref
  48.7 0.7 %collective-permute-done.11.ssouth_ref = f32[9,8,256]{2,1,0:T(8,128)S(1)} collective-permute-done((f32[9,8,256]{2,1,0:T(8,128)S(1)}, f32[9,8,256]{2,1,0:T(8,128)S(1)}, u32[]{:S(2)}, u32[]{:S(2)}) %collective-permute-start.11) | collective-permute-done | bytes 73760 | tf_op jit(solution)/shard_map/ppermute | solution.py:360
  49.5 0.0 collective-permute-done.2.north_ref
  49.5 0.0 collective-permute-done.3.south_ref
  49.5 0.0 copy-start.7
  49.5 0.0 copy-start.8
  49.5 0.0 copy-done.1
  49.5 0.0 copy-done.4
  49.5 0.0 copy-done.6
  49.5 0.6 %copy-done.7 = f32[16]{0:T(128)S(1)} copy-done((f32[16]{0:T(128)S(1)}, f32[16]{0:T(128)}, u32[]{:S(2)}) %copy-start.7) | copy-done | bytes 88
  50.1 0.0 copy-done.8
  50.1 5.4 %shard_map.100 = (f32[1,16,16,256]{3,2,1,0:T(8,128)}, f32[2,16,256]{2,1,0:T(8,128)}) custom-call(s32[1]{0:T(128)S(6)} %copy.10.seed_ref, f32[16,16]{1,0:T(8,128)S(1)} %copy-done.6, f32[16]{0:T(128)S(1)} %copy-done.7, f32[16]{0:T(128)S(1)} %copy-done.8, f32[1,16,16,256]{3,2,1,0:T(8,128)S(1)} %copy-done.4, bf16[4,2,16,16,256]{4,3,2,1,0:T(8,128)(2,1)S(1)} %copy-done.1, ...), custom_call_target="tpu_custom_call" | custom-call | flops 10000000 | bytes 10000000 | tf_op jit(solution)/shard_map/pallas_call | solution.py:362
  (2 shorter events, 0.0 us)
Async XLA Ops:
  0.6 1.2 %copy-start = (bf16[4,2,16,16,256]{4,3,2,1,0:T(8,128)(2,1)S(1)}, bf16[4,2,16,16,256]{4,3,2,1,0:T(8,128)(2,1)}, u32[]{:S(2)}) copy-start(bf16[4,2,16,16,256]{4,3,2,1,0:T(8,128)(2,1)} %speeds_ref.5) | copy-start | bytes 3145732
  1.9 1.2 %copy-start.2 = (s32[4,16,16,256]{3,2,1,0:T(8,128)S(1)}, s32[4,16,16,256]{3,2,1,0:T(8,128)}, u32[]{:S(2)}) copy-start(s32[4,16,16,256]{3,2,1,0:T(8,128)} %upwind_ref.5) | copy-start | bytes 3145732
  3.1 0.9 %copy-start.3 = (f32[1,16,16,256]{3,2,1,0:T(8,128)S(1)}, f32[1,16,16,256]{3,2,1,0:T(8,128)}, u32[]{:S(2)}) copy-start(f32[1,16,16,256]{3,2,1,0:T(8,128)} %delta_ref.5) | copy-start | bytes 786436
  4.3 13.2 %copy-start.5 = (f32[2,16,256]{2,1,0:T(8,128)S(1)}, f32[2,16,256]{2,1,0:T(8,128)}, u32[]{:S(2)}) copy-start(f32[2,16,256]{2,1,0:T(8,128)} %own_ref.1) | copy-start | bytes 98308
  4.4 45.1 %copy-start.1 = (bf16[4,2,16,16,256]{4,3,2,1,0:T(8,128)(2,1)S(1)}, bf16[4,2,16,16,256]{4,3,2,1,0:T(8,128)(2,1)}, u32[]{:S(2)}) copy-start(bf16[4,2,16,16,256]{4,3,2,1,0:T(8,128)(2,1)} %speeds_ref.5) | copy-start | bytes 3145732
  4.4 5.2 %collective-permute-start = (f32[10,16,128]{2,1,0:T(8,128)S(1)}, f32[10,16,128]{2,1,0:T(8,128)S(1)}, u32[]{:S(2)}, u32[]{:S(2)}) collective-permute-start(f32[10,16,128]{2,1,0:T(8,128)S(1)} %shard_map.95.own_ref), channel_id=1, source_target_pairs={{0,1},{1,2},{2,3},{3,0},{4,5},{5,6},{6,7},{7,4},{8,9},{9,10},{10,1... | collective-permute-start | bytes 245768 | tf_op jit(solution)/shard_map/ppermute | solution.py:342
  6.5 3.3 %collective-permute-start.1 = (f32[10,16,128]{2,1,0:T(8,128)S(1)}, f32[10,16,128]{2,1,0:T(8,128)S(1)}, u32[]{:S(2)}, u32[]{:S(2)}) collective-permute-start(f32[10,16,128]{2,1,0:T(8,128)S(1)} %shard_map.95.own_ref), channel_id=1, source_target_pairs={{1,0},{2,1},{3,2},{0,3},{5,4},{6,5},{7,6},{4,7},{9,8},{10,9},{11,1... | collective-permute-start | bytes 245768 | tf_op jit(solution)/shard_map/ppermute | solution.py:343
  10.1 39.4 %collective-permute-start.2 = (f32[17,24,256]{2,1,0:T(8,128)S(1)}, f32[17,24,256]{2,1,0:T(8,128)S(1)}, u32[]{:S(2)}, u32[]{:S(2)}) collective-permute-start(f32[17,24,256]{2,1,0:T(8,128)S(1)} %get-tuple-element.11), channel_id=1, source_target_pairs={{4,0},{8,4},{12,8},{16,12},{20,16},{24,20},{28,24},{5,1},{9,5},{13... | collective-permute-start | bytes 1253384 | tf_op jit(solution)/shard_map/ppermute | solution.py:350
  15.5 33.9 %collective-permute-start.3 = (f32[17,24,256]{2,1,0:T(8,128)S(1)}, f32[17,24,256]{2,1,0:T(8,128)S(1)}, u32[]{:S(2)}, u32[]{:S(2)}) collective-permute-start(f32[17,24,256]{2,1,0:T(8,128)S(1)} %get-tuple-element.12), channel_id=1, source_target_pairs={{0,4},{4,8},{8,12},{12,16},{16,20},{20,24},{24,28},{1,5},{5,9},{9,... | collective-permute-start | bytes 1253384 | tf_op jit(solution)/shard_map/ppermute | solution.py:351
  17.6 12.8 %collective-permute-start.4 = (f32[2,16,256]{2,1,0:T(8,128)S(1)}, f32[2,16,256]{2,1,0:T(8,128)S(1)}, u32[]{:S(2)}, u32[]{:S(2)}) collective-permute-start(f32[2,16,256]{2,1,0:T(8,128)S(1)} %copy-done.5), channel_id=1, source_target_pairs={{0,32},{32,0},{64,96},{96,64},{128,160},{160,128},{192,224},{224,1... | collective-permute-start | bytes 98312 | tf_op jit(solution)/shard_map/ppermute | solution.py:340
  30.4 19.1 %copy-start.4 = (f32[1,16,16,256]{3,2,1,0:T(8,128)S(1)}, f32[1,16,16,256]{3,2,1,0:T(8,128)}, u32[]{:S(2)}) copy-start(f32[1,16,16,256]{3,2,1,0:T(8,128)} %delta_ref.5) | copy-start | bytes 786436
  30.4 4.1 %collective-permute-start.5 = (f32[4,16,256]{2,1,0:T(8,128)S(1)}, f32[4,16,256]{2,1,0:T(8,128)S(1)}, u32[]{:S(2)}, u32[]{:S(2)}) collective-permute-start(f32[4,16,256]{2,1,0:T(8,128)S(1)} %shard_map.97.b0_ref), channel_id=1, source_target_pairs={{64,0},{96,32},{128,64},{160,96},{192,128},{224,160},{0,192},{32,2... | collective-permute-start | bytes 196616 | tf_op jit(solution)/shard_map/ppermute | solution.py:345
  33.2 4.7 %collective-permute-start.6 = (f32[4,16,256]{2,1,0:T(8,128)S(1)}, f32[4,16,256]{2,1,0:T(8,128)S(1)}, u32[]{:S(2)}, u32[]{:S(2)}) collective-permute-start(f32[4,16,256]{2,1,0:T(8,128)S(1)} %shard_map.97.b0_ref), channel_id=1, source_target_pairs={{128,0},{160,32},{192,64},{224,96},{0,128},{32,160},{64,192},{96,2... | collective-permute-start | bytes 196616 | tf_op jit(solution)/shard_map/ppermute | solution.py:345
  33.6 5.0 %collective-permute-start.7 = (f32[4,16,256]{2,1,0:T(8,128)S(1)}, f32[4,16,256]{2,1,0:T(8,128)S(1)}, u32[]{:S(2)}, u32[]{:S(2)}) collective-permute-start(f32[4,16,256]{2,1,0:T(8,128)S(1)} %shard_map.97.b0_ref), channel_id=1, source_target_pairs={{192,0},{224,32},{0,64},{32,96},{64,128},{96,160},{128,192},{160,2... | collective-permute-start | bytes 196616 | tf_op jit(solution)/shard_map/ppermute | solution.py:345
  38.6 3.8 %collective-permute-start.8 = (f32[1,16,128]{2,1,0:T(8,128)S(1)}, f32[1,16,128]{2,1,0:T(8,128)S(1)}, u32[]{:S(2)}, u32[]{:S(2)}) collective-permute-start(f32[1,16,128]{2,1,0:T(8,128)S(1)} %get-tuple-element.14.own_ref), channel_id=1, source_target_pairs={{0,1},{1,2},{2,3},{3,0},{4,5},{5,6},{6,7},{7,4},{8,9},{9,10},{10,1... | collective-permute-start | bytes 24584 | tf_op jit(solution)/shard_map/ppermute | solution.py:353
  39.9 2.5 %collective-permute-start.9 = (f32[1,16,128]{2,1,0:T(8,128)S(1)}, f32[1,16,128]{2,1,0:T(8,128)S(1)}, u32[]{:S(2)}, u32[]{:S(2)}) collective-permute-start(f32[1,16,128]{2,1,0:T(8,128)S(1)} %get-tuple-element.14.own_ref), channel_id=1, source_target_pairs={{1,0},{2,1},{3,2},{0,3},{5,4},{6,5},{7,6},{4,7},{9,8},{10,9},{11,1... | collective-permute-start | bytes 24584 | tf_op jit(solution)/shard_map/ppermute | solution.py:354
  42.5 7.0 %copy-start.6 = (f32[16,16]{1,0:T(8,128)S(1)}, f32[16,16]{1,0:T(8,128)}, u32[]{:S(2)}) copy-start(f32[16,16]{1,0:T(8,128)} %table_ref.1) | copy-start | bytes 3076
  42.5 6.2 %collective-permute-start.10 = (f32[9,8,256]{2,1,0:T(8,128)S(1)}, f32[9,8,256]{2,1,0:T(8,128)S(1)}, u32[]{:S(2)}, u32[]{:S(2)}) collective-permute-start(f32[9,8,256]{2,1,0:T(8,128)S(1)} %get-tuple-element.16), channel_id=1, source_target_pairs={{4,0},{8,4},{12,8},{16,12},{20,16},{24,20},{28,24},{5,1},{9,5},{13... | collective-permute-start | bytes 221192 | tf_op jit(solution)/shard_map/ppermute | solution.py:359
  44.4 5.0 %collective-permute-start.11 = (f32[9,8,256]{2,1,0:T(8,128)S(1)}, f32[9,8,256]{2,1,0:T(8,128)S(1)}, u32[]{:S(2)}, u32[]{:S(2)}) collective-permute-start(f32[9,8,256]{2,1,0:T(8,128)S(1)} %get-tuple-element.17), channel_id=1, source_target_pairs={{0,4},{4,8},{8,12},{12,16},{16,20},{20,24},{24,28},{1,5},{5,9},{9,... | collective-permute-start | bytes 221192 | tf_op jit(solution)/shard_map/ppermute | solution.py:360
  49.5 0.7 %copy-start.7 = (f32[16]{0:T(128)S(1)}, f32[16]{0:T(128)}, u32[]{:S(2)}) copy-start(f32[16]{0:T(128)} %visc_ref.1) | copy-start | bytes 196
  49.5 0.7 %copy-start.8 = (f32[16]{0:T(128)S(1)}, f32[16]{0:T(128)}, u32[]{:S(2)}) copy-start(f32[16]{0:T(128)} %rate_ref.1) | copy-start | bytes 196

commit v3 on v2

v3 whole, which is shorter than its diff:
```python
import jax
import jax.numpy as jnp
from jax import lax
from jax.experimental import pallas as pl
from jax.experimental.pallas import tpu as pltpu
from jax.sharding import PartitionSpec as P


F32 = jnp.float32
I32 = jnp.int32
STEPS = 4
LEV = 16
COEF = 3
NCD = 1 + 3 * COEF
VMEM = pl.BlockSpec(memory_space=pltpu.VMEM)
SMEM = pl.BlockSpec(memory_space=pltpu.SMEM)
HBM = pl.BlockSpec(memory_space=pltpu.HBM)
LIMIT = 8 * 2**20


def lanes():
    return lax.broadcasted_iota(I32, (8, 128), 1)


def subs():
    return lax.broadcasted_iota(I32, (8, 128), 0)


def rows_at(r):
    return pl.ds(8 * r, 8)


def cols_at(c):
    return pl.ds(128 * c, 128)


def is_odd(axis):
    return jnp.full((8, 128), lax.rem(lax.axis_index(axis), 2), I32) == 1


def own_tiles(delta_ref, speeds_ref, upwind_ref, a, lev, c):
    if a == 0:
        return [delta_ref[0, lev, rows_at(r), cols_at(c)] for r in range(2)]
    step, kind = divmod(a - 1, 3)
    if kind < 2:
        both = speeds_ref[step, kind, lev, :, cols_at(c)].astype(F32)
        return [both[0:8], both[8:16]]
    return [upwind_ref[step, lev, rows_at(r), cols_at(c)].astype(F32) for r in range(2)]


def slot(acc, left, right, lev):
    lane = lanes()
    edge = pltpu.roll(jnp.where(lane < 64, left, right), 8 * lev + 4, 1)
    return jnp.where(lane // 8 == lev, edge, acc)


def pack_columns(
    seed_hbm, table_hbm, visc_hbm, rate_hbm, state_hbm, delta_hbm, speeds_hbm, upwind_hbm,
    out_ref, state_ref, delta_ref, speeds_ref, upwind_ref, const_ref,
    seed_ref, table_ref, visc_ref, rate_ref, small_sems, sems, last_sems,
):
    small = [
        pltpu.make_async_copy(src, dst, small_sems.at[n])
        for n, (src, dst) in enumerate(
            ((seed_hbm, seed_ref), (table_hbm, table_ref), (visc_hbm, visc_ref), (rate_hbm, rate_ref))
        )
    ]
    groups = [[pltpu.make_async_copy(delta_hbm, delta_ref, sems.at[0])]]
    last = [pltpu.make_async_copy(state_hbm, state_ref, last_sems.at[0])]
    for step in range(STEPS):
        pair = []
        for n, (src, dst) in enumerate(((speeds_hbm, speeds_ref), (upwind_hbm, upwind_ref))):
            sem = sems.at[1 + 2 * step + n] if step < COEF else last_sems.at[1 + n]
            pair.append(pltpu.make_async_copy(src.at[step], dst.at[step], sem))
        if step < COEF:
            groups.append(pair)
        else:
            last += pair
    for copy in small + [c for group in groups for c in group] + last:
        copy.start()
    for copy in small:
        copy.wait()
    lane = lanes()
    seed = seed_ref[0]
    spread = [jnp.zeros((8, 128), F32)] * 3
    for lev in range(LEV):
        here = (visc_ref[lev], rate_ref[lev], table_ref[seed, lev])
        for q in range(3):
            tile = jnp.full((8, 128), here[q], F32)
            const_ref[lev, q] = tile
            spread[q] = jnp.where(lane // 8 == lev, tile, spread[q])
    for q in range(3):
        const_ref[LEV, q] = spread[q]
    for a in range(NCD):
        if a % 3 < 2 and (a == 0 or a % 3 == 1):
            for copy in groups[(a + 2) // 3]:
                copy.wait()
        acc = [jnp.zeros((8, 128), F32)] * 2
        for lev in range(LEV):
            left = own_tiles(delta_ref, speeds_ref, upwind_ref, a, lev, 0)
            right = own_tiles(delta_ref, speeds_ref, upwind_ref, a, lev, 1)
            acc = [slot(acc[r], left[r], right[r], lev) for r in range(2)]
        for r in range(2):
            out_ref[a, rows_at(r), :] = acc[r]
    for copy in last:
        copy.wait()


def strip_tile(own_ref, inner_ref, outer_ref, a, r, c):
    half, odd = lanes() % 8 < 4, is_odd("lon")
    own = own_ref[a, rows_at(r), :]
    inner, outer = inner_ref[a, rows_at(r), :], outer_ref[a, rows_at(r), :]
    if c == 0:
        return jnp.where(half, jnp.where(odd, inner, outer), own)
    return jnp.where(half, own, jnp.where(odd, outer, inner))


def join_pair(own_ref, other_ref, out_ref):
    half = lax.rem(lax.axis_index("ens"), 2)
    out_ref[pl.ds(2 * half, 2)] = own_ref[...]
    out_ref[pl.ds(2 - 2 * half, 2)] = other_ref[...]


def merge_rows(pieces):
    sub = subs()
    acc = jnp.zeros((8, 128), F32)
    for tile, shift, first, last in pieces:
        if shift % 8:
            tile = pltpu.roll(tile, shift % 8, 0)
        acc = jnp.where((sub >= first) & (sub <= last), tile, acc)
    return acc


def pack_rows(delta_ref, speeds_ref, upwind_ref, own_ref, near_ref, far_ref, strip_ref, inner_ref, outer_ref):
    odd = is_odd("lat")

    def put(lev, c, tiles):
        for kind in range(3):
            k0, k1, k2 = (tiles[1 + 3 * step + kind] for step in range(3))
            d = tiles[0]
            low = [(k0[0], 0, 0, 2), (k1[0], 3, 3, 4), (k2[0], 5, 5, 5)]
            high = [(k0[1], 0, 5, 7), (k1[1], -3, 3, 4), (k2[1], -5, 2, 2)]
            if kind == 0:
                low.append((d[0], 6, 6, 7))
                high.append((d[1], -4, 0, 1))
            if kind == 1:
                low.append((d[0], 4, 6, 7))
                high.append((d[1], -6, 0, 1))
            down, up = merge_rows(low), merge_rows(high)
            inner_ref[lev, rows_at(kind), cols_at(c)] = jnp.where(odd, down, up)
            outer_ref[lev, rows_at(kind), cols_at(c)] = jnp.where(odd, up, down)

    for c in range(2):
        tiles = []
        for a in range(NCD):
            pair = [strip_tile(own_ref, near_ref, far_ref, a, r, c) for r in range(2)]
            for r in range(2):
                strip_ref[a, rows_at(r), cols_at(c)] = pair[r]
            tiles.append(pair)
        put(LEV, c, tiles)

    def body(lev, carry):
        for c in range(2):
            put(lev, c, [own_tiles(delta_ref, speeds_ref, upwind_ref, a, lev, c) for a in range(NCD)])
        return carry

    lax.fori_loop(0, LEV, body, 0)


def join_all(b0_ref, b1_ref, b2_ref, b3_ref, out_ref, columns_ref):
    mine = lax.axis_index("ens") // 2
    acc = [jnp.zeros((8, 128), F32)] * 2
    for ahead, ref in enumerate((b0_ref, b1_ref, b2_ref, b3_ref)):
        base = 4 * (mine ^ ahead)
        out_ref[pl.ds(base, 4)] = ref[...]
        for i in range(4):
            for r in range(2):
                left, right = (ref[i, rows_at(r), cols_at(c)] for c in range(2))
                acc[r] = slot(acc[r], left, right, base + i)
    for r in range(2):
        columns_ref[0, rows_at(r), :] = acc[r]


def state_rows(state_ref, own_ref, near_ref, far_ref, strip_ref, inner_ref, outer_ref):
    low, odd = subs() < 4, is_odd("lat")
    for c in range(2):
        pair = [strip_tile(own_ref, near_ref, far_ref, 0, r, c) for r in range(2)]
        for r in range(2):
            strip_ref[rows_at(r), cols_at(c)] = pair[r]
        inner_ref[8, :, cols_at(c)] = jnp.where(odd, pair[0], pair[1])
        outer_ref[8, :, cols_at(c)] = jnp.where(odd, pair[1], pair[0])
        for p in range(8):
            a0, a1 = (state_ref[2 * p, rows_at(r), cols_at(c)] for r in range(2))
            b0, b1 = (pltpu.roll(state_ref[2 * p + 1, rows_at(r), cols_at(c)], 4, 0) for r in range(2))
            down, up = jnp.where(low, a0, b0), jnp.where(low, b1, a1)
            inner_ref[p, :, cols_at(c)] = jnp.where(odd, down, up)
            outer_ref[p, :, cols_at(c)] = jnp.where(odd, up, down)


def weights(s, t, m, v):
    vs, vt = v + s, v + t
    eastward, northward = (m & 1) == 1, m >= 2
    return (
        ((1.0 - 2.0 * v) - vs) - vt,
        jnp.where(eastward, vs, v),
        jnp.where(eastward, v, vs),
        jnp.where(northward, vt, v),
        jnp.where(northward, v, vt),
    )


def own_weights(speeds_ref, upwind_ref, strip_ref, const_ref, out_ref):
    def put(lev, step, r, c, tiles):
        for q, tile in enumerate(tiles):
            out_ref[lev, ((step * 2 + r) * 2 + c) * 5 + q] = tile

    for step in range(COEF):
        for r in range(2):
            for c in range(2):
                s, t, m = (strip_ref[1 + 3 * step + kind, rows_at(r), cols_at(c)] for kind in range(3))
                put(LEV, step, r, c, weights(s, t, m.astype(I32), const_ref[LEV, 0]))

    def body(lev, carry):
        v = const_ref[lev, 0]
        for step in range(STEPS):
            for c in range(2):
                s = speeds_ref[step, 0, lev, :, cols_at(c)].astype(F32)
                t = speeds_ref[step, 1, lev, :, cols_at(c)].astype(F32)
                for r in range(2):
                    m = upwind_ref[step, lev, rows_at(r), cols_at(c)]
                    put(lev, step, r, c, weights(s[8 * r : 8 * r + 8], t[8 * r : 8 * r + 8], m, v))
        return carry

    lax.fori_loop(0, LEV, body, 0)


def halo_weights(inner_ref, outer_ref, const_ref, out_ref, delta_ref):
    sub, odd = subs(), is_odd("lat")
    band = lax.axis_index("lat")
    inside = jnp.where(
        sub < 4,
        jnp.where(band < lax.axis_size("lat") - 1, 1.0, 0.0).astype(F32),
        jnp.where(band > 0, 1.0, 0.0).astype(F32),
    )
    keep = [(sub <= 2, sub >= 5), (sub <= 1, sub >= 6), (sub <= 0, sub >= 7)]

    def body(lev, carry):
        v, amp = const_ref[lev, 0] * inside, const_ref[lev, 2]
        for c in range(2):
            inner = [inner_ref[lev, rows_at(kind), cols_at(c)] for kind in range(3)]
            outer = [outer_ref[lev, rows_at(kind), cols_at(c)] for kind in range(3)]
            north = [jnp.where(odd, outer[kind], inner[kind]) for kind in range(3)]
            south = [jnp.where(odd, inner[kind], outer[kind]) for kind in range(3)]
            for step, shift in enumerate((0, 3, 5)):
                low, high = keep[step]
                stm = []
                for kind in range(3):
                    n, s = north[kind], south[kind]
                    if shift:
                        n, s = pltpu.roll(n, 8 - shift, 0), pltpu.roll(s, shift, 0)
                    stm.append(jnp.where(low, n, jnp.where(high, s, 0.0)))
                for q, tile in enumerate(weights(stm[0], stm[1], stm[2].astype(I32), v)):
                    out_ref[lev, (step * 2 + c) * 5 + q] = tile
            n0, n1 = pltpu.roll(north[0], 2, 0), pltpu.roll(north[1], 4, 0)
            s0, s1 = pltpu.roll(south[0], 4, 0), pltpu.roll(south[1], 6, 0)
            tile = jnp.where(sub < 2, n0, jnp.where(sub < 4, n1, jnp.where(sub < 6, s0, s1)))
            delta_ref[lev, :, cols_at(c)] = tile * amp
        return carry

    lax.fori_loop(0, LEV + 1, body, 0)


def advance(
    const_ref, delta_ref, strip_ref, own_ref, halo_ref, delta_halo_ref,
    state_ref, state_strip_ref, inner_ref, outer_ref,
    delta_out, state_out,
    edge_state, edge_delta, finals, work,
):
    lane = lanes()
    first = 2 * lax.axis_index("ens")
    outer_first = (subs() // 4 == 0) == is_odd("lat")

    def halo_state(p, odd, c):
        inner, outer = inner_ref[p, :, cols_at(c)], outer_ref[p, :, cols_at(c)]
        if odd:
            return pltpu.roll(jnp.where(outer_first, inner, outer), 4, 0)
        return jnp.where(outer_first, outer, inner)

    def sides(f, fix_west, fix_east):
        west, east = [], []
        for r, (left, right) in enumerate(f):
            wl, wr = pltpu.roll(left, 1, 1), pltpu.roll(right, 1, 1)
            el, er = pltpu.roll(left, 127, 1), pltpu.roll(right, 127, 1)
            if fix_west is None:
                west.append((wl, wr))
                east.append((el, er))
            else:
                west.append((jnp.where(lane == 0, fix_west[r], wl), jnp.where(lane == 0, wl, wr)))
                east.append((jnp.where(lane == 127, er, el), jnp.where(lane == 127, fix_east[r], er)))
        return west, east

    def ends(f, buf, count):
        for c in range(2):
            for r in range(3):
                buf[c, pl.ds(8 + 8 * r, 8), :] = f[r][c]
            buf[c, pl.ds(0, 8), :] = f[2][c]
            if count == 3:
                buf[c, pl.ds(32, 8), :] = f[0][c]
        below = [[buf[c, pl.ds(8 * r + 7, 8), :] for c in range(2)] for r in range(count)]
        above = [[buf[c, pl.ds(8 * r + 9, 8), :] for c in range(2)] for r in range(count)]
        return below, above

    def run(lev, odd, state, delta, edges, before):
        rate = const_ref[lev, 1]
        for step in range(STEPS):
            before(step, state, delta)
            if step == STEPS - 1 and edges is None:
                return state, delta
            count = 3 if step < STEPS - 1 else 2
            fixes = [None] * 4 if edges is None else edges(step, count)
            ws, es = sides(state[:count], fixes[0], fixes[1])
            wd, ed = sides(delta[:count], fixes[2], fixes[3])
            ss, ns = ends(state, work.at[odd, step % 2, 0], count)
            sd, nd = ends(delta, work.at[odd, step % 2, 1], count)
            next_state, next_delta = [], []
            for r in range(count):
                row_s, row_d = [], []
                for c in range(2):
                    if r < 2:
                        at = [own_ref[lev, ((step * 2 + r) * 2 + c) * 5 + q] for q in range(5)]
                    else:
                        at = [halo_ref[lev, (step * 2 + c) * 5 + q] for q in range(5)]
                    c0, cw, ce, cs, cn = at
                    f, d = state[r][c], delta[r][c]
                    loss = rate * (f * f)
                    row_s.append(
                        ((c0 - loss) * f + cw * ws[r][c]) + (ce * es[r][c] + cs * ss[r][c]) + cn * ns[r][c]
                    )
                    row_d.append(
                        ((c0 - 3.0 * loss) * d + cw * wd[r][c]) + (ce * ed[r][c] + cs * sd[r][c]) + cn * nd[r][c]
                    )
                next_state.append(row_s)
                next_delta.append(row_d)
            state, delta = next_state, next_delta
        return state, delta

    def strip_before(step, state, delta):
        for r in range(3):
            for c in range(2):
                edge_state[step, c, rows_at(r), :] = state[r][c]
                edge_delta[step, c, rows_at(r), :] = delta[r][c]

    amp = const_ref[LEV, 2]
    state = [[state_strip_ref[rows_at(r), cols_at(c)] for c in range(2)] for r in range(2)]
    state.append([halo_state(8, 0, c) for c in range(2)])
    delta = [[strip_ref[0, rows_at(r), cols_at(c)] * amp for c in range(2)] for r in range(2)]
    delta.append([delta_halo_ref[LEV, :, cols_at(c)] for c in range(2)])
    run(LEV, 0, state, delta, None, strip_before)

    def one_level(p, odd):
        lev = 2 * p + odd
        amp = const_ref[lev, 2]

        def edges(step, count):
            to_first = lax.rem(253 - 8 * lev, 128)
            to_last = lax.rem(251 - 8 * lev, 128)
            out = []
            for ref in (edge_state, edge_delta):
                out.append([pltpu.roll(ref[step, 0, rows_at(r), :], to_first, 1) for r in range(count)])
                out.append([pltpu.roll(ref[step, 1, rows_at(r), :], to_last, 1) for r in range(count)])
            return out

        state = [[state_ref[lev, rows_at(r), cols_at(c)] for c in range(2)] for r in range(2)]
        state.append([halo_state(p, odd, c) for c in range(2)])
        delta = [[delta_ref[0, lev, rows_at(r), cols_at(c)] * amp for c in range(2)] for r in range(2)]
        delta.append([delta_halo_ref[lev, :, cols_at(c)] for c in range(2)])
        state, delta = run(lev, odd, state, delta, edges, lambda *unused: None)
        for r in range(2):
            for c in range(2):
                finals[lev, rows_at(r), cols_at(c)] = state[r][c]
                delta_out[0, lev, rows_at(r), cols_at(c)] = delta[r][c]

    def body(p, carry):
        one_level(p, 0)
        one_level(p, 1)
        return carry

    lax.fori_loop(0, LEV // 2, body, 0)
    state_out[...] = finals[pl.ds(first, 2)]


def call(kernel, shapes, specs, scratch=(), cost=100000):
    out = [jax.ShapeDtypeStruct(shape, dtype) for shape, dtype in ((*e, F32)[:2] for e in shapes)]
    single = len(out) == 1
    return pl.pallas_call(
        kernel,
        out_shape=out[0] if single else out,
        in_specs=specs,
        out_specs=VMEM if single else [VMEM] * len(out),
        scratch_shapes=scratch,
        compiler_params=pltpu.CompilerParams(vmem_limit_bytes=LIMIT),
        cost_estimate=pl.CostEstimate(flops=cost, bytes_accessed=cost, transcendentals=0),
    )


def per_device(perturbation, seed_ids, amp_table, start_state, speeds, upwind, viscosity, reaction):
    n_lat, n_lon, n_ens = lax.axis_size("lat"), lax.axis_size("lon"), lax.axis_size("ens")
    lat_inner = [(i, i ^ 1) for i in range(n_lat)]
    lat_outer = [(i, ((i + 1) ^ 1) - 1) for i in range(1, n_lat - 1)]
    lon_inner = [(i, i ^ 1) for i in range(n_lon)]
    lon_outer = [(i, (((i + 1) ^ 1) - 1) % n_lon) for i in range(n_lon)]

    def run(kernel, shapes, specs, *args, **more):
        return call(kernel, [(shape,) if isinstance(shape[0], int) else shape for shape in shapes], specs, **more)(*args)

    other = lax.ppermute(start_state, "ens", [(i, i ^ 1) for i in range(n_ens)])
    columns, state, delta, fast, wind, consts = run(
        pack_columns,
        [
            (NCD, 16, 128), start_state.shape, perturbation.shape, (speeds.shape, speeds.dtype), (upwind.shape, upwind.dtype),
            (LEV + 1, 3, 8, 128),
        ],
        [HBM] * 8,
        seed_ids,
        *(
            pltpu.with_memory_space_constraint(x, pltpu.HBM)
            for x in (amp_table, viscosity, reaction, start_state, perturbation, speeds, upwind)
        ),
        scratch=[
            pltpu.SMEM(seed_ids.shape, I32), pltpu.SMEM(amp_table.shape, F32),
            pltpu.SMEM(viscosity.shape, F32), pltpu.SMEM(reaction.shape, F32),
            pltpu.SemaphoreType.DMA((4,)), pltpu.SemaphoreType.DMA((1 + 2 * COEF,)),
            pltpu.SemaphoreType.DMA((3,)),
        ],
    )
    near = lax.ppermute(columns, "lon", lon_inner)
    far = lax.ppermute(columns, "lon", lon_outer)
    quad = run(join_pair, [(4, 16, 256)], [VMEM] * 2, state, other)
    ahead = [lax.ppermute(quad, "ens", [(i, i ^ (2 * j)) for i in range(n_ens)]) for j in (1, 2, 3)]
    strips, down, up = run(
        pack_rows, [(NCD, 16, 256), (LEV + 1, 24, 256), (LEV + 1, 24, 256)], [VMEM] * 6,
        delta, fast, wind, columns, near, far,
    )
    cd_north = lax.ppermute(down, "lat", lat_inner)
    cd_south = lax.ppermute(up, "lat", lat_outer)
    states, state_columns = run(join_all, [(LEV, 16, 256), (1, 16, 128)], [VMEM] * 4, quad, *ahead)
    state_west = lax.ppermute(state_columns, "lon", lon_inner)
    state_east = lax.ppermute(state_columns, "lon", lon_outer)
    own = run(own_weights, [(LEV + 1, 20 * STEPS, 8, 128)], [VMEM] * 4, fast, wind, strips, consts)
    state_strip, state_down, state_up = run(
        state_rows, [(16, 256), (9, 8, 256), (9, 8, 256)], [VMEM] * 4,
        states, state_columns, state_west, state_east,
    )
    st_north = lax.ppermute(state_down, "lat", lat_inner)
    st_south = lax.ppermute(state_up, "lat", lat_outer)
    halo, delta_halo = run(
        halo_weights, [(LEV + 1, 10 * COEF, 8, 128), (LEV + 1, 8, 256)], [VMEM] * 3,
        cd_north, cd_south, consts,
    )
    edge = pltpu.VMEM((STEPS, 2, 24, 128), F32)
    return run(
        advance, [(1, LEV, 16, 256), (2, 16, 256)], [VMEM] * 10,
        consts, delta, strips, own, halo, delta_halo, states, state_strip, st_north, st_south,
        scratch=[edge, edge, pltpu.VMEM((LEV, 16, 256), F32), pltpu.VMEM((2, 2, 2, 2, 40, 128), F32)],
        cost=10000000,
    )


def solution(mesh):
    step = jax.shard_map(
        per_device,
        mesh=mesh,
        in_specs=(
            P("ens", None, "lat", "lon"),
            P("ens"),
            P(),
            P("ens", "lat", "lon"),
            P(None, None, None, "lat", "lon"),
            P(None, None, "lat", "lon"),
            P(),
            P(),
        ),
        out_specs=(P("ens", None, "lat", "lon"), P("ens", "lat", "lon")),
        check_vma=False,
    )
    return lambda *args: tuple(step(*args))
```

time: 55.9 us -> 54.1 us (0.968)
  local copies, waits for them, and re-layouts: 4.06 us -> 0 us
  Pallas kernels: 6.15 us -> 8.02 us
  waiting for transfers between devices: 14.6 us -> 15.5 us
    unnamed x18 -> x0, local copies, waits for them, and re-layouts: 4.06 us -> none
    ppermute x11, waiting for transfers between devices: 7.9 us -> 9.85 us  [the longest x3 4.32 us: per_device(): lax.ppermute(quad, 'ens', [(i, i ^ 2 * j) for i in range(n_ens)])]
    pallas_call x6 -> x8, Pallas kernels: 6.15 us -> 8.02 us  [run(): call(kernel, [(shape,) if isinstance(shape[0], int) else shape for shape...]
    ppermute x1, waiting for transfers between devices: 6.71 us -> 5.68 us  [per_device(): other = lax.ppermute(start_state, 'ens', [(i, i ^ 1) for i in range(n_ens)])]
  transfers between devices with their start and end apart: 12 -> 12, of which waited for: 8 -> 7; matrix products, arithmetic and copies ran while one was open for 0% -> 0% of each run, Pallas kernels for 0% -> 2%
where the time goes in v3:
time: 54.1 us; the launch traced here: 54 us
  starting transfers between devices  29 us (54%)
  waiting for transfers between devices  15.5 us (29%)
  Pallas kernels  8.02 us (15%)
  between operations  1.38 us (3%)
    pallas_call x8, Pallas kernels, run(): call(kernel, [(shape,) if isinstance(shape[0], int) else shape for shape...  8.02 us
    ppermute x1, starting transfers between devices, per_device(): st_south = lax.ppermute(state_up, 'lat', lat_outer)  7.29 us
    ppermute x1, starting transfers between devices, per_device(): other = lax.ppermute(start_state, 'ens', [(i, i ^ 1) for i in range(n_ens)])  6.1 us
    ppermute x1, waiting for transfers between devices, per_device(): other = lax.ppermute(start_state, 'ens', [(i, i ^ 1) for i in range(n_ens)])  5.68 us
    ppermute x3, waiting for transfers between devices, per_device(): lax.ppermute(quad, 'ens', [(i, i ^ 2 * j) for i in range(n_ens)])  4.32 us
    ppermute x3, starting transfers between devices, per_device(): lax.ppermute(quad, 'ens', [(i, i ^ 2 * j) for i in range(n_ens)])  4.01 us
    ppermute x1, starting transfers between devices, per_device(): cd_south = lax.ppermute(up, 'lat', lat_outer)  3.13 us
    ppermute x1, waiting for transfers between devices, per_device(): far = lax.ppermute(columns, 'lon', lon_outer)  2.67 us
  transfers between devices with their start and end apart: 12, of which 7 were waited for; matrix products, arithmetic and copies ran while one was open for 0% of the time, Pallas kernels for 2%

profile of v3, /device:TPU:1, one launch (start us, length us, event | category | flops | bytes accessed | tf_op | source)
XLA Modules:
  0.0 54.0 jit_solution(4379825647173250674)
XLA Ops:
  1.3 1.7 %shard_map.95 = (f32[10,16,128]{2,1,0:T(8,128)S(1)}, f32[2,16,256]{2,1,0:T(8,128)S(1)}, f32[1,16,16,256]{3,2,1,0:T(8,128)S(1)}, bf16[4,2,16,16,256]{4,3,2,1,0:T(...) custom-call(s32[1]{0:T(128)S(6)} %copy.10.seed_hbm, f32[16,16]{1,0:T(8,128)} %table_hbm.1, ...), custom_call_target="tpu_custom_call" | custom-call | flops 100000 | bytes 100000 | tf_op jit(solution)/shard_map/pallas_call | solution.py:414
  3.0 2.1 %collective-permute-start = (f32[10,16,128]{2,1,0:T(8,128)S(1)}, f32[10,16,128]{2,1,0:T(8,128)S(1)}, u32[]{:S(2)}, u32[]{:S(2)}) collective-permute-start(f32[10,16,128]{2,1,0:T(8,128)S(1)} %get-tuple-element.22.own_ref), channel_id=1, source_target_pairs={{0,1},{1,0},{2,3},{3,2},{4,5},{5,4},{6,7},{7,6},{8,9},{9,8},{10,11... | collective-permute-start | bytes 245768 | tf_op jit(solution)/shard_map/ppermute | solution.py:436
  5.1 1.8 %collective-permute-start.1 = (f32[10,16,128]{2,1,0:T(8,128)S(1)}, f32[10,16,128]{2,1,0:T(8,128)S(1)}, u32[]{:S(2)}, u32[]{:S(2)}) collective-permute-start(f32[10,16,128]{2,1,0:T(8,128)S(1)} %get-tuple-element.22.own_ref), channel_id=1, source_target_pairs={{0,3},{1,2},{2,1},{3,0},{4,7},{5,6},{6,5},{7,4},{8,11},{9,10},{10,... | collective-permute-start | bytes 245768 | tf_op jit(solution)/shard_map/ppermute | solution.py:437
  6.9 0.0 collective-permute-done.near_ref
  7.0 2.7 %collective-permute-done.1.far_ref = f32[10,16,128]{2,1,0:T(8,128)S(1)} collective-permute-done((f32[10,16,128]{2,1,0:T(8,128)S(1)}, f32[10,16,128]{2,1,0:T(8,128)S(1)}, u32[]{:S(2)}, u32[]{:S(2)}) %collective-permute-start.1) | collective-permute-done | bytes 81952 | tf_op jit(solution)/shard_map/ppermute | solution.py:437
  9.6 0.4 shard_map.96
  10.0 2.5 %collective-permute-start.2 = (f32[17,24,256]{2,1,0:T(8,128)S(1)}, f32[17,24,256]{2,1,0:T(8,128)S(1)}, u32[]{:S(2)}, u32[]{:S(2)}) collective-permute-start(f32[17,24,256]{2,1,0:T(8,128)S(1)} %get-tuple-element.24), channel_id=1, source_target_pairs={{0,4},{4,0},{8,12},{12,8},{16,20},{20,16},{24,28},{28,24},{1,5},{5... | collective-permute-start | bytes 1253384 | tf_op jit(solution)/shard_map/ppermute | solution.py:444
  12.5 3.1 %collective-permute-start.3 = (f32[17,24,256]{2,1,0:T(8,128)S(1)}, f32[17,24,256]{2,1,0:T(8,128)S(1)}, u32[]{:S(2)}, u32[]{:S(2)}) collective-permute-start(f32[17,24,256]{2,1,0:T(8,128)S(1)} %get-tuple-element.25), channel_id=1, source_target_pairs={{4,8},{8,4},{12,16},{16,12},{20,24},{24,20},{5,9},{9,5},{13,17},{1... | collective-permute-start | bytes 1253384 | tf_op jit(solution)/shard_map/ppermute | solution.py:445
  15.6 6.1 %collective-permute-start.4 = (f32[2,16,256]{2,1,0:T(8,128)}, f32[2,16,256]{2,1,0:T(8,128)S(1)}, u32[]{:S(2)}, u32[]{:S(2)}) collective-permute-start(f32[2,16,256]{2,1,0:T(8,128)} %state_hbm.1), channel_id=1, source_target_pairs={{0,32},{32,0},{64,96},{96,64},{128,160},{160,128},{192,224},{224,1... | collective-permute-start | bytes 98312 | tf_op jit(solution)/shard_map/ppermute | solution.py:416
  21.7 5.7 %collective-permute-done.4.other_ref = f32[2,16,256]{2,1,0:T(8,128)S(1)} collective-permute-done((f32[2,16,256]{2,1,0:T(8,128)}, f32[2,16,256]{2,1,0:T(8,128)S(1)}, u32[]{:S(2)}, u32[]{:S(2)}) %collective-permute-start.4) | collective-permute-done | bytes 32800 | tf_op jit(solution)/shard_map/ppermute | solution.py:416
  27.4 1.4 %collective-permute-start.5 = (f32[4,16,256]{2,1,0:T(8,128)S(1)}, f32[4,16,256]{2,1,0:T(8,128)S(1)}, u32[]{:S(2)}, u32[]{:S(2)}) collective-permute-start(f32[4,16,256]{2,1,0:T(8,128)S(1)} %shard_map.99.b0_ref), channel_id=1, source_target_pairs={{0,64},{32,96},{64,0},{96,32},{128,192},{160,224},{192,128},{224,1... | collective-permute-start | bytes 196616 | tf_op jit(solution)/shard_map/ppermute | solution.py:439
  28.8 2.6 %collective-permute-start.6 = (f32[4,16,256]{2,1,0:T(8,128)S(1)}, f32[4,16,256]{2,1,0:T(8,128)S(1)}, u32[]{:S(2)}, u32[]{:S(2)}) collective-permute-start(f32[4,16,256]{2,1,0:T(8,128)S(1)} %shard_map.99.b0_ref), channel_id=1, source_target_pairs={{0,128},{32,160},{64,192},{96,224},{128,0},{160,32},{192,64},{224,... | collective-permute-start | bytes 196616 | tf_op jit(solution)/shard_map/ppermute | solution.py:439
  31.4 0.0 collective-permute-start.7
  31.4 0.0 collective-permute-done.5.b1_ref
  31.4 2.3 %collective-permute-done.6.b2_ref = f32[4,16,256]{2,1,0:T(8,128)S(1)} collective-permute-done((f32[4,16,256]{2,1,0:T(8,128)S(1)}, f32[4,16,256]{2,1,0:T(8,128)S(1)}, u32[]{:S(2)}, u32[]{:S(2)}) %collective-permute-start.6) | collective-permute-done | bytes 65568 | tf_op jit(solution)/shard_map/ppermute | solution.py:439
  33.8 2.0 %collective-permute-done.7.b3_ref = f32[4,16,256]{2,1,0:T(8,128)S(1)} collective-permute-done((f32[4,16,256]{2,1,0:T(8,128)S(1)}, f32[4,16,256]{2,1,0:T(8,128)S(1)}, u32[]{:S(2)}, u32[]{:S(2)}) %collective-permute-start.7) | collective-permute-done | bytes 65568 | tf_op jit(solution)/shard_map/ppermute | solution.py:439
  35.8 0.1 shard_map.100
  35.9 0.1 collective-permute-start.8
  36.0 1.9 %collective-permute-start.9 = (f32[1,16,128]{2,1,0:T(8,128)S(1)}, f32[1,16,128]{2,1,0:T(8,128)S(1)}, u32[]{:S(2)}, u32[]{:S(2)}) collective-permute-start(f32[1,16,128]{2,1,0:T(8,128)S(1)} %get-tuple-element.30.own_ref), channel_id=1, source_target_pairs={{0,3},{1,2},{2,1},{3,0},{4,7},{5,6},{6,5},{7,4},{8,11},{9,10},{10,... | collective-permute-start | bytes 24584 | tf_op jit(solution)/shard_map/ppermute | solution.py:448
  37.9 0.6 %collective-permute-done.8.near_ref = f32[1,16,128]{2,1,0:T(8,128)S(1)} collective-permute-done((f32[1,16,128]{2,1,0:T(8,128)S(1)}, f32[1,16,128]{2,1,0:T(8,128)S(1)}, u32[]{:S(2)}, u32[]{:S(2)}) %collective-permute-start.8) | collective-permute-done | bytes 8224 | tf_op jit(solution)/shard_map/ppermute | solution.py:447
  38.5 1.3 %collective-permute-done.9.far_ref = f32[1,16,128]{2,1,0:T(8,128)S(1)} collective-permute-done((f32[1,16,128]{2,1,0:T(8,128)S(1)}, f32[1,16,128]{2,1,0:T(8,128)S(1)}, u32[]{:S(2)}, u32[]{:S(2)}) %collective-permute-start.9) | collective-permute-done | bytes 8224 | tf_op jit(solution)/shard_map/ppermute | solution.py:448
  39.8 0.1 collective-permute-start.10
  39.9 7.3 %collective-permute-start.11 = (f32[9,8,256]{2,1,0:T(8,128)S(1)}, f32[9,8,256]{2,1,0:T(8,128)S(1)}, u32[]{:S(2)}, u32[]{:S(2)}) collective-permute-start(f32[9,8,256]{2,1,0:T(8,128)S(1)} %get-tuple-element.33), channel_id=1, source_target_pairs={{4,8},{8,4},{12,16},{16,12},{20,24},{24,20},{5,9},{9,5},{13,17},{1... | collective-permute-start | bytes 221192 | tf_op jit(solution)/shard_map/ppermute | solution.py:455
  47.2 0.5 shard_map.97.own_ref
  47.7 0.0 collective-permute-done.2.inner_ref
  47.8 0.0 collective-permute-done.3.outer_ref
  47.8 0.5 shard_map.98
  48.3 0.0 collective-permute-done.10.inner_ref
  48.3 0.9 %collective-permute-done.11.outer_ref = f32[9,8,256]{2,1,0:T(8,128)S(1)} collective-permute-done((f32[9,8,256]{2,1,0:T(8,128)S(1)}, f32[9,8,256]{2,1,0:T(8,128)S(1)}, u32[]{:S(2)}, u32[]{:S(2)}) %collective-permute-start.11) | collective-permute-done | bytes 73760 | tf_op jit(solution)/shard_map/ppermute | solution.py:455
  49.2 4.8 %shard_map.102 = (f32[1,16,16,256]{3,2,1,0:T(8,128)}, f32[2,16,256]{2,1,0:T(8,128)}) custom-call(f32[17,3,8,128]{3,2,1,0:T(8,128)S(1)} %get-tuple-element.18.const_ref, f32[1,16,16,256]{3,2,1,0:T(8,128)S(1)} %get-tuple-element.19.delta_ref, f32[10,16,256]{2,1,0:T(8,128)S(1)} %get-tuple-element.23.strip_ref, f32[17,80,8,128]{3,2,1,0:T(8,128)S(1)} %shard_map.97.own_ref, ...), custom_call_target="tpu_custom_call" | custom-call | flops 10000000 | bytes 10000000 | tf_op jit(solution)/shard_map/pallas_call | solution.py:414
  (2 shorter events, 0.0 us)
Async XLA Ops:
  3.0 3.9 %collective-permute-start = (f32[10,16,128]{2,1,0:T(8,128)S(1)}, f32[10,16,128]{2,1,0:T(8,128)S(1)}, u32[]{:S(2)}, u32[]{:S(2)}) collective-permute-start(f32[10,16,128]{2,1,0:T(8,128)S(1)} %get-tuple-element.22.own_ref), channel_id=1, source_target_pairs={{0,1},{1,0},{2,3},{3,2},{4,5},{5,4},{6,7},{7,6},{8,9},{9,8},{10,11... | collective-permute-start | bytes 245768 | tf_op jit(solution)/shard_map/ppermute | solution.py:436
  5.1 4.5 %collective-permute-start.1 = (f32[10,16,128]{2,1,0:T(8,128)S(1)}, f32[10,16,128]{2,1,0:T(8,128)S(1)}, u32[]{:S(2)}, u32[]{:S(2)}) collective-permute-start(f32[10,16,128]{2,1,0:T(8,128)S(1)} %get-tuple-element.22.own_ref), channel_id=1, source_target_pairs={{0,3},{1,2},{2,1},{3,0},{4,7},{5,6},{6,5},{7,4},{8,11},{9,10},{10,... | collective-permute-start | bytes 245768 | tf_op jit(solution)/shard_map/ppermute | solution.py:437
  10.0 37.7 %collective-permute-start.2 = (f32[17,24,256]{2,1,0:T(8,128)S(1)}, f32[17,24,256]{2,1,0:T(8,128)S(1)}, u32[]{:S(2)}, u32[]{:S(2)}) collective-permute-start(f32[17,24,256]{2,1,0:T(8,128)S(1)} %get-tuple-element.24), channel_id=1, source_target_pairs={{0,4},{4,0},{8,12},{12,8},{16,20},{20,16},{24,28},{28,24},{1,5},{5... | collective-permute-start | bytes 1253384 | tf_op jit(solution)/shard_map/ppermute | solution.py:444
  12.5 35.3 %collective-permute-start.3 = (f32[17,24,256]{2,1,0:T(8,128)S(1)}, f32[17,24,256]{2,1,0:T(8,128)S(1)}, u32[]{:S(2)}, u32[]{:S(2)}) collective-permute-start(f32[17,24,256]{2,1,0:T(8,128)S(1)} %get-tuple-element.25), channel_id=1, source_target_pairs={{4,8},{8,4},{12,16},{16,12},{20,24},{24,20},{5,9},{9,5},{13,17},{1... | collective-permute-start | bytes 1253384 | tf_op jit(solution)/shard_map/ppermute | solution.py:445
  15.6 11.8 %collective-permute-start.4 = (f32[2,16,256]{2,1,0:T(8,128)}, f32[2,16,256]{2,1,0:T(8,128)S(1)}, u32[]{:S(2)}, u32[]{:S(2)}) collective-permute-start(f32[2,16,256]{2,1,0:T(8,128)} %state_hbm.1), channel_id=1, source_target_pairs={{0,32},{32,0},{64,96},{96,64},{128,160},{160,128},{192,224},{224,1... | collective-permute-start | bytes 98312 | tf_op jit(solution)/shard_map/ppermute | solution.py:416
  27.4 4.0 %collective-permute-start.5 = (f32[4,16,256]{2,1,0:T(8,128)S(1)}, f32[4,16,256]{2,1,0:T(8,128)S(1)}, u32[]{:S(2)}, u32[]{:S(2)}) collective-permute-start(f32[4,16,256]{2,1,0:T(8,128)S(1)} %shard_map.99.b0_ref), channel_id=1, source_target_pairs={{0,64},{32,96},{64,0},{96,32},{128,192},{160,224},{192,128},{224,1... | collective-permute-start | bytes 196616 | tf_op jit(solution)/shard_map/ppermute | solution.py:439
  28.8 5.0 %collective-permute-start.6 = (f32[4,16,256]{2,1,0:T(8,128)S(1)}, f32[4,16,256]{2,1,0:T(8,128)S(1)}, u32[]{:S(2)}, u32[]{:S(2)}) collective-permute-start(f32[4,16,256]{2,1,0:T(8,128)S(1)} %shard_map.99.b0_ref), channel_id=1, source_target_pairs={{0,128},{32,160},{64,192},{96,224},{128,0},{160,32},{192,64},{224,... | collective-permute-start | bytes 196616 | tf_op jit(solution)/shard_map/ppermute | solution.py:439
  31.4 4.3 %collective-permute-start.7 = (f32[4,16,256]{2,1,0:T(8,128)S(1)}, f32[4,16,256]{2,1,0:T(8,128)S(1)}, u32[]{:S(2)}, u32[]{:S(2)}) collective-permute-start(f32[4,16,256]{2,1,0:T(8,128)S(1)} %shard_map.99.b0_ref), channel_id=1, source_target_pairs={{0,192},{32,224},{64,128},{96,160},{128,64},{160,96},{192,0},{224,... | collective-permute-start | bytes 196616 | tf_op jit(solution)/shard_map/ppermute | solution.py:439
  35.9 2.6 %collective-permute-start.8 = (f32[1,16,128]{2,1,0:T(8,128)S(1)}, f32[1,16,128]{2,1,0:T(8,128)S(1)}, u32[]{:S(2)}, u32[]{:S(2)}) collective-permute-start(f32[1,16,128]{2,1,0:T(8,128)S(1)} %get-tuple-element.30.own_ref), channel_id=1, source_target_pairs={{0,1},{1,0},{2,3},{3,2},{4,5},{5,4},{6,7},{7,6},{8,9},{9,8},{10,11... | collective-permute-start | bytes 24584 | tf_op jit(solution)/shard_map/ppermute | solution.py:447
  36.0 3.8 %collective-permute-start.9 = (f32[1,16,128]{2,1,0:T(8,128)S(1)}, f32[1,16,128]{2,1,0:T(8,128)S(1)}, u32[]{:S(2)}, u32[]{:S(2)}) collective-permute-start(f32[1,16,128]{2,1,0:T(8,128)S(1)} %get-tuple-element.30.own_ref), channel_id=1, source_target_pairs={{0,3},{1,2},{2,1},{3,0},{4,7},{5,6},{6,5},{7,4},{8,11},{9,10},{10,... | collective-permute-start | bytes 24584 | tf_op jit(solution)/shard_map/ppermute | solution.py:448
  39.8 8.5 %collective-permute-start.10 = (f32[9,8,256]{2,1,0:T(8,128)S(1)}, f32[9,8,256]{2,1,0:T(8,128)S(1)}, u32[]{:S(2)}, u32[]{:S(2)}) collective-permute-start(f32[9,8,256]{2,1,0:T(8,128)S(1)} %get-tuple-element.32), channel_id=1, source_target_pairs={{0,4},{4,0},{8,12},{12,8},{16,20},{20,16},{24,28},{28,24},{1,5},{5... | collective-permute-start | bytes 221192 | tf_op jit(solution)/shard_map/ppermute | solution.py:454
  39.9 9.3 %collective-permute-start.11 = (f32[9,8,256]{2,1,0:T(8,128)S(1)}, f32[9,8,256]{2,1,0:T(8,128)S(1)}, u32[]{:S(2)}, u32[]{:S(2)}) collective-permute-start(f32[9,8,256]{2,1,0:T(8,128)S(1)} %get-tuple-element.33), channel_id=1, source_target_pairs={{4,8},{8,4},{12,16},{16,12},{20,24},{24,20},{5,9},{9,5},{13,17},{1... | collective-permute-start | bytes 221192 | tf_op jit(solution)/shard_map/ppermute | solution.py:455

commit v4 on v3

--- a/solution.py
+++ b/solution.py
@@ -1,3 +1,5 @@
+import itertools
+
 import jax
 import jax.numpy as jnp
 from jax import lax
@@ -16,6 +18,7 @@
 SMEM = pl.BlockSpec(memory_space=pltpu.SMEM)
 HBM = pl.BlockSpec(memory_space=pltpu.HBM)
 LIMIT = 8 * 2**20
+GROUP = 2
 
 
 def lanes():
@@ -55,41 +58,33 @@
 
 
 def pack_columns(
-    seed_hbm, table_hbm, visc_hbm, rate_hbm, state_hbm, delta_hbm, speeds_hbm, upwind_hbm,
+    visc_hbm, rate_hbm, state_hbm, delta_hbm, speeds_hbm, upwind_hbm,
     out_ref, state_ref, delta_ref, speeds_ref, upwind_ref, const_ref,
-    seed_ref, table_ref, visc_ref, rate_ref, small_sems, sems, last_sems,
+    visc_ref, rate_ref, small_sems, sems, last_sems,
 ):
     small = [
         pltpu.make_async_copy(src, dst, small_sems.at[n])
-        for n, (src, dst) in enumerate(
-            ((seed_hbm, seed_ref), (table_hbm, table_ref), (visc_hbm, visc_ref), (rate_hbm, rate_ref))
-        )
+        for n, (src, dst) in enumerate(((visc_hbm, visc_ref), (rate_hbm, rate_ref)))
     ]
     groups = [[pltpu.make_async_copy(delta_hbm, delta_ref, sems.at[0])]]
     last = [pltpu.make_async_copy(state_hbm, state_ref, last_sems.at[0])]
-    for step in range(STEPS):
-        pair = []
+    for step in range(COEF):
+        groups.append([])
         for n, (src, dst) in enumerate(((speeds_hbm, speeds_ref), (upwind_hbm, upwind_ref))):
-            sem = sems.at[1 + 2 * step + n] if step < COEF else last_sems.at[1 + n]
-            pair.append(pltpu.make_async_copy(src.at[step], dst.at[step], sem))
-        if step < COEF:
-            groups.append(pair)
-        else:
-            last += pair
+            groups[-1].append(pltpu.make_async_copy(src.at[step], dst.at[step], sems.at[1 + 2 * step + n]))
     for copy in small + [c for group in groups for c in group] + last:
         copy.start()
     for copy in small:
         copy.wait()
     lane = lanes()
-    seed = seed_ref[0]
-    spread = [jnp.zeros((8, 128), F32)] * 3
+    spread = [jnp.zeros((8, 128), F32)] * 2
     for lev in range(LEV):
-        here = (visc_ref[lev], rate_ref[lev], table_ref[seed, lev])
-        for q in range(3):
+        here = (visc_ref[lev], rate_ref[lev])
+        for q in range(2):
             tile = jnp.full((8, 128), here[q], F32)
             const_ref[lev, q] = tile
             spread[q] = jnp.where(lane // 8 == lev, tile, spread[q])
-    for q in range(3):
+    for q in range(2):
         const_ref[LEV, q] = spread[q]
     for a in range(NCD):
         if a % 3 < 2 and (a == 0 or a % 3 == 1):
@@ -209,7 +204,16 @@
     )
 
 
-def own_weights(speeds_ref, upwind_ref, strip_ref, const_ref, out_ref):
+def own_weights(
+    speeds_hbm, upwind_hbm, early_speeds, early_upwind, strip_ref, const_ref, out_ref, late_speeds, late_upwind, sems
+):
+    copies = [
+        pltpu.make_async_copy(speeds_hbm.at[COEF], late_speeds, sems.at[0]),
+        pltpu.make_async_copy(upwind_hbm.at[COEF], late_upwind, sems.at[1]),
+    ]
+    for copy in copies:
+        copy.start()
+
     def put(lev, step, r, c, tiles):
         for q, tile in enumerate(tiles):
             out_ref[lev, ((step * 2 + r) * 2 + c) * 5 + q] = tile
@@ -220,21 +224,39 @@
                 s, t, m = (strip_ref[1 + 3 * step + kind, rows_at(r), cols_at(c)] for kind in range(3))
                 put(LEV, step, r, c, weights(s, t, m.astype(I32), const_ref[LEV, 0]))
 
-    def body(lev, carry):
+    def level(lev, steps):
         v = const_ref[lev, 0]
-        for step in range(STEPS):
+        for step in steps:
+            speeds_ref, upwind_ref = late_speeds, late_upwind
+            if step < COEF:
+                speeds_ref, upwind_ref = early_speeds.at[step], early_upwind.at[step]
             for c in range(2):
-                s = speeds_ref[step, 0, lev, :, cols_at(c)].astype(F32)
-                t = speeds_ref[step, 1, lev, :, cols_at(c)].astype(F32)
+                s = speeds_ref[0, lev, :, cols_at(c)].astype(F32)
+                t = speeds_ref[1, lev, :, cols_at(c)].astype(F32)
                 for r in range(2):
-                    m = upwind_ref[step, lev, rows_at(r), cols_at(c)]
+                    m = upwind_ref[lev, rows_at(r), cols_at(c)]
                     put(lev, step, r, c, weights(s[8 * r : 8 * r + 8], t[8 * r : 8 * r + 8], m, v))
+
+    def early(lev, carry):
+        level(lev, range(COEF))
         return carry
 
-    lax.fori_loop(0, LEV, body, 0)
-
-
-def halo_weights(inner_ref, outer_ref, const_ref, out_ref, delta_ref):
+    def late(lev, carry):
+        level(lev, (COEF,))
+        return carry
+
+    lax.fori_loop(0, LEV, early, 0)
+    for copy in copies:
+        copy.wait()
+    lax.fori_loop(0, LEV, late, 0)
+
+
+def halo_weights(
+    seed_ref, table_hbm, inner_ref, outer_ref, const_ref, out_ref, delta_ref, amp_ref, table_ref, sem
+):
+    copy = pltpu.make_async_copy(table_hbm, table_ref, sem)
+    copy.start()
+    lane = lanes()
     sub, odd = subs(), is_odd("lat")
     band = lax.axis_index("lat")
     inside = jnp.where(
@@ -245,7 +267,7 @@
     keep = [(sub <= 2, sub >= 5), (sub <= 1, sub >= 6), (sub <= 0, sub >= 7)]
 
     def body(lev, carry):
-        v, amp = const_ref[lev, 0] * inside, const_ref[lev, 2]
+        v = const_ref[lev, 0] * inside
         for c in range(2):
             inner = [inner_ref[lev, rows_at(kind), cols_at(c)] for kind in range(3)]
             outer = [outer_ref[lev, rows_at(kind), cols_at(c)] for kind in range(3)]
@@ -264,14 +286,22 @@
             n0, n1 = pltpu.roll(north[0], 2, 0), pltpu.roll(north[1], 4, 0)
             s0, s1 = pltpu.roll(south[0], 4, 0), pltpu.roll(south[1], 6, 0)
             tile = jnp.where(sub < 2, n0, jnp.where(sub < 4, n1, jnp.where(sub < 6, s0, s1)))
-            delta_ref[lev, :, cols_at(c)] = tile * amp
+            delta_ref[lev, :, cols_at(c)] = tile
         return carry
 
     lax.fori_loop(0, LEV + 1, body, 0)
+    copy.wait()
+    seed = seed_ref[0]
+    spread = jnp.zeros((8, 128), F32)
+    for lev in range(LEV):
+        tile = jnp.full((8, 128), table_ref[seed, lev], F32)
+        amp_ref[lev] = tile
+        spread = jnp.where(lane // 8 == lev, tile, spread)
+    amp_ref[LEV] = spread
 
 
 def advance(
-    const_ref, delta_ref, strip_ref, own_ref, halo_ref, delta_halo_ref,
+    const_ref, amp_ref, delta_ref, strip_ref, own_ref, halo_ref, delta_halo_ref,
     state_ref, state_strip_ref, inner_ref, outer_ref,
     delta_out, state_out,
     edge_state, edge_delta, finals, work,
@@ -286,17 +316,17 @@
             return pltpu.roll(jnp.where(outer_first, inner, outer), 4, 0)
         return jnp.where(outer_first, outer, inner)
 
-    def sides(f, fix_west, fix_east):
+    def sides(f, fix):
         west, east = [], []
         for r, (left, right) in enumerate(f):
             wl, wr = pltpu.roll(left, 1, 1), pltpu.roll(right, 1, 1)
             el, er = pltpu.roll(left, 127, 1), pltpu.roll(right, 127, 1)
-            if fix_west is None:
+            if fix is None:
                 west.append((wl, wr))
                 east.append((el, er))
             else:
-                west.append((jnp.where(lane == 0, fix_west[r], wl), jnp.where(lane == 0, wl, wr)))
-                east.append((jnp.where(lane == 127, er, el), jnp.where(lane == 127, fix_east[r], er)))
+                west.append((jnp.where(lane == 0, fix[r], wl), jnp.where(lane == 0, wl, wr)))
+                east.append((jnp.where(lane == 127, er, el), jnp.where(lane == 127, fix[r], er)))
         return west, east
 
     def ends(f, buf, count):
@@ -310,18 +340,22 @@
         above = [[buf[c, pl.ds(8 * r + 9, 8), :] for c in range(2)] for r in range(count)]
         return below, above
 
-    def run(lev, odd, state, delta, edges, before):
+    def run(lev, place, state, delta, edges):
         rate = const_ref[lev, 1]
         for step in range(STEPS):
-            before(step, state, delta)
-            if step == STEPS - 1 and edges is None:
-                return state, delta
+            yield
             count = 3 if step < STEPS - 1 else 2
-            fixes = [None] * 4 if edges is None else edges(step, count)
-            ws, es = sides(state[:count], fixes[0], fixes[1])
-            wd, ed = sides(delta[:count], fixes[2], fixes[3])
-            ss, ns = ends(state, work.at[odd, step % 2, 0], count)
-            sd, nd = ends(delta, work.at[odd, step % 2, 1], count)
+            fixes = (None, None) if edges is None else edges(step, count)
+            ws, es = sides(state[:count], fixes[0])
+            wd, ed = sides(delta[:count], fixes[1])
+            if edges is None:
+                for ref, west, east in ((edge_state, ws, es), (edge_delta, wd, ed)):
+                    for r in range(count):
+                        ref[step, rows_at(r), :] = jnp.where(lane % 8 == 4, west[r][0], east[r][1])
+                if step == STEPS - 1:
+                    return
+            ss, ns = ends(state, work.at[place, step % 2, 0], count)
+            sd, nd = ends(delta, work.at[place, step % 2, 1], count)
             next_state, next_delta = [], []
             for r in range(count):
                 row_s, row_d = [], []
@@ -342,50 +376,43 @@
                 next_state.append(row_s)
                 next_delta.append(row_d)
             state, delta = next_state, next_delta
-        return state, delta
-
-    def strip_before(step, state, delta):
-        for r in range(3):
-            for c in range(2):
-                edge_state[step, c, rows_at(r), :] = state[r][c]
-                edge_delta[step, c, rows_at(r), :] = delta[r][c]
-
-    amp = const_ref[LEV, 2]
-    state = [[state_strip_ref[rows_at(r), cols_at(c)] for c in range(2)] for r in range(2)]
-    state.append([halo_state(8, 0, c) for c in range(2)])
-    delta = [[strip_ref[0, rows_at(r), cols_at(c)] * amp for c in range(2)] for r in range(2)]
-    delta.append([delta_halo_ref[LEV, :, cols_at(c)] for c in range(2)])
-    run(LEV, 0, state, delta, None, strip_before)
-
-    def one_level(p, odd):
-        lev = 2 * p + odd
-        amp = const_ref[lev, 2]
-
-        def edges(step, count):
-            to_first = lax.rem(253 - 8 * lev, 128)
-            to_last = lax.rem(251 - 8 * lev, 128)
-            out = []
-            for ref in (edge_state, edge_delta):
-                out.append([pltpu.roll(ref[step, 0, rows_at(r), :], to_first, 1) for r in range(count)])
-                out.append([pltpu.roll(ref[step, 1, rows_at(r), :], to_last, 1) for r in range(count)])
-            return out
-
-        state = [[state_ref[lev, rows_at(r), cols_at(c)] for c in range(2)] for r in range(2)]
-        state.append([halo_state(p, odd, c) for c in range(2)])
-        delta = [[delta_ref[0, lev, rows_at(r), cols_at(c)] * amp for c in range(2)] for r in range(2)]
-        delta.append([delta_halo_ref[lev, :, cols_at(c)] for c in range(2)])
-        state, delta = run(lev, odd, state, delta, edges, lambda *unused: None)
         for r in range(2):
             for c in range(2):
                 finals[lev, rows_at(r), cols_at(c)] = state[r][c]
                 delta_out[0, lev, rows_at(r), cols_at(c)] = delta[r][c]
 
+    amp = amp_ref[LEV]
+    state = [[state_strip_ref[rows_at(r), cols_at(c)] for c in range(2)] for r in range(2)]
+    state.append([halo_state(8, 0, c) for c in range(2)])
+    delta = [[strip_ref[0, rows_at(r), cols_at(c)] * amp for c in range(2)] for r in range(2)]
+    delta.append([delta_halo_ref[LEV, :, cols_at(c)] * amp for c in range(2)])
+    for _ in run(LEV, 0, state, delta, None):
+        pass
+
+    def one_level(p, place):
+        odd = place % 2
+        p = GROUP // 2 * p + place // 2
+        lev = 2 * p + odd
+        amp = amp_ref[lev]
+
+        def edges(step, count):
+            return [
+                [pltpu.roll(ref[step, rows_at(r), :], 124 - 8 * lev, 1) for r in range(count)]
+                for ref in (edge_state, edge_delta)
+            ]
+
+        state = [[state_ref[lev, rows_at(r), cols_at(c)] for c in range(2)] for r in range(2)]
+        state.append([halo_state(p, odd, c) for c in range(2)])
+        delta = [[delta_ref[0, lev, rows_at(r), cols_at(c)] * amp for c in range(2)] for r in range(2)]
+        delta.append([delta_halo_ref[lev, :, cols_at(c)] * amp for c in range(2)])
+        return run(lev, place, state, delta, edges)
+
     def body(p, carry):
-        one_level(p, 0)
-        one_level(p, 1)
+        for _ in itertools.zip_longest(*(one_level(p, place) for place in range(GROUP))):
+            pass
         return carry
 
-    lax.fori_loop(0, LEV // 2, body, 0)
+    lax.fori_loop(0, LEV // GROUP, body, 0)
     state_out[...] = finals[pl.ds(first, 2)]
 
 
@@ -417,20 +444,18 @@
     columns, state, delta, fast, wind, consts = run(
         pack_columns,
         [
-            (NCD, 16, 128), start_state.shape, perturbation.shape, (speeds.shape, speeds.dtype), (upwind.shape, upwind.dtype),
-            (LEV + 1, 3, 8, 128),
+            (NCD, 16, 128), start_state.shape, perturbation.shape, ((COEF, *speeds.shape[1:]), speeds.dtype), ((COEF, *upwind.shape[1:]), upwind.dtype),
+            (LEV + 1, 2, 8, 128),
         ],
-        [HBM] * 8,
-        seed_ids,
+        [HBM] * 6,
         *(
             pltpu.with_memory_space_constraint(x, pltpu.HBM)
-            for x in (amp_table, viscosity, reaction, start_state, perturbation, speeds, upwind)
+            for x in (viscosity, reaction, start_state, perturbation, speeds, upwind)
         ),
         scratch=[
-            pltpu.SMEM(seed_ids.shape, I32), pltpu.SMEM(amp_table.shape, F32),
             pltpu.SMEM(viscosity.shape, F32), pltpu.SMEM(reaction.shape, F32),
-            pltpu.SemaphoreType.DMA((4,)), pltpu.SemaphoreType.DMA((1 + 2 * COEF,)),
-            pltpu.SemaphoreType.DMA((3,)),
+            pltpu.SemaphoreType.DMA((2,)), pltpu.SemaphoreType.DMA((1 + 2 * COEF,)),
+            pltpu.SemaphoreType.DMA((1,)),
         ],
     )
     near = lax.ppermute(columns, "lon", lon_inner)
@@ -446,22 +471,31 @@
     states, state_columns = run(join_all, [(LEV, 16, 256), (1, 16, 128)], [VMEM] * 4, quad, *ahead)
     state_west = lax.ppermute(state_columns, "lon", lon_inner)
     state_east = lax.ppermute(state_columns, "lon", lon_outer)
-    own = run(own_weights, [(LEV + 1, 20 * STEPS, 8, 128)], [VMEM] * 4, fast, wind, strips, consts)
+    own = run(
+        own_weights, [(LEV + 1, 20 * STEPS, 8, 128)], [HBM] * 2 + [VMEM] * 4,
+        *(pltpu.with_memory_space_constraint(x, pltpu.HBM) for x in (speeds, upwind)), fast, wind, strips, consts,
+        scratch=[
+            pltpu.VMEM(speeds.shape[1:], speeds.dtype), pltpu.VMEM(upwind.shape[1:], upwind.dtype),
+            pltpu.SemaphoreType.DMA((2,)),
+        ],
+    )
     state_strip, state_down, state_up = run(
         state_rows, [(16, 256), (9, 8, 256), (9, 8, 256)], [VMEM] * 4,
         states, state_columns, state_west, state_east,
     )
     st_north = lax.ppermute(state_down, "lat", lat_inner)
     st_south = lax.ppermute(state_up, "lat", lat_outer)
-    halo, delta_halo = run(
-        halo_weights, [(LEV + 1, 10 * COEF, 8, 128), (LEV + 1, 8, 256)], [VMEM] * 3,
-        cd_north, cd_south, consts,
-    )
-    edge = pltpu.VMEM((STEPS, 2, 24, 128), F32)
+    halo, delta_halo, amp = run(
+        halo_weights, [(LEV + 1, 10 * COEF, 8, 128), (LEV + 1, 8, 256), (LEV + 1, 8, 128)],
+        [SMEM, HBM] + [VMEM] * 3,
+        seed_ids, pltpu.with_memory_space_constraint(amp_table, pltpu.HBM), cd_north, cd_south, consts,
+        scratch=[pltpu.SMEM(amp_table.shape, F32), pltpu.SemaphoreType.DMA],
+    )
+    edge = pltpu.VMEM((STEPS, 24, 128), F32)
     return run(
-        advance, [(1, LEV, 16, 256), (2, 16, 256)], [VMEM] * 10,
-        consts, delta, strips, own, halo, delta_halo, states, state_strip, st_north, st_south,
-        scratch=[edge, edge, pltpu.VMEM((LEV, 16, 256), F32), pltpu.VMEM((2, 2, 2, 2, 40, 128), F32)],
+        advance, [(1, LEV, 16, 256), (2, 16, 256)], [VMEM] * 11,
+        consts, amp, delta, strips, own, halo, delta_halo, states, state_strip, st_north, st_south,
+        scratch=[edge, edge, pltpu.VMEM((LEV, 16, 256), F32), pltpu.VMEM((GROUP, 2, 2, 2, 40, 128), F32)],
         cost=10000000,
     )
 

time: 54.1 us -> 53.4 us (0.987)
  waiting for transfers between devices: 15.5 us -> 14.6 us
    ppermute x1, waiting for transfers between devices: 0.94 us -> 0.01 us  [per_device(): st_south = lax.ppermute(state_up, 'lat', lat_outer)]
  transfers between devices with their start and end apart: 12 -> 12, of which waited for: 7 -> 6; matrix products, arithmetic and copies ran while one was open for 0% -> 0% of each run, Pallas kernels for 2% -> 4%
where the time goes in v4:
time: 53.4 us; the launch traced here: 53.2 us
  starting transfers between devices  29 us (54%)
  waiting for transfers between devices  14.6 us (27%)
  Pallas kernels  8.16 us (15%)
  between operations  1.39 us (3%)
    pallas_call x8, Pallas kernels, run(): call(kernel, [(shape,) if isinstance(shape[0], int) else shape for shape...  8.16 us
    ppermute x1, starting transfers between devices, per_device(): st_south = lax.ppermute(state_up, 'lat', lat_outer)  7.29 us
    ppermute x1, starting transfers between devices, per_device(): other = lax.ppermute(start_state, 'ens', [(i, i ^ 1) for i in range(n_ens)])  6.1 us
    ppermute x1, waiting for transfers between devices, per_device(): other = lax.ppermute(start_state, 'ens', [(i, i ^ 1) for i in range(n_ens)])  5.68 us
    ppermute x3, waiting for transfers between devices, per_device(): lax.ppermute(quad, 'ens', [(i, i ^ 2 * j) for i in range(n_ens)])  4.32 us
    ppermute x3, starting transfers between devices, per_device(): lax.ppermute(quad, 'ens', [(i, i ^ 2 * j) for i in range(n_ens)])  4.01 us
    ppermute x1, starting transfers between devices, per_device(): cd_south = lax.ppermute(up, 'lat', lat_outer)  3.13 us
    ppermute x1, waiting for transfers between devices, per_device(): far = lax.ppermute(columns, 'lon', lon_outer)  2.67 us
  transfers between devices with their start and end apart: 12, of which 6 were waited for; matrix products, arithmetic and copies ran while one was open for 0% of the time, Pallas kernels for 4%

profile of v4, /device:TPU:1, one launch (start us, length us, event | category | flops | bytes accessed | tf_op | source)
XLA Modules:
  0.0 53.2 jit_solution(8116994610939752738)
XLA Ops:
  0.6 1.7 %shard_map.95 = (f32[10,16,128]{2,1,0:T(8,128)S(1)}, f32[2,16,256]{2,1,0:T(8,128)S(1)}, f32[1,16,16,256]{3,2,1,0:T(8,128)S(1)}, bf16[3,2,16,16,256]{4,3,2,1,0:T(...) custom-call(f32[16]{0:T(128)} %visc_hbm.1, f32[16]{0:T(128)} %rate_hbm.1, ...), custom_call_target="tpu_custom_call" | custom-call | flops 100000 | bytes 100000 | tf_op jit(solution)/shard_map/pallas_call | solution.py:441
  2.3 2.1 %collective-permute-start = (f32[10,16,128]{2,1,0:T(8,128)S(1)}, f32[10,16,128]{2,1,0:T(8,128)S(1)}, u32[]{:S(2)}, u32[]{:S(2)}) collective-permute-start(f32[10,16,128]{2,1,0:T(8,128)S(1)} %get-tuple-element.23.own_ref), channel_id=1, source_target_pairs={{0,1},{1,0},{2,3},{3,2},{4,5},{5,4},{6,7},{7,6},{8,9},{9,8},{10,11... | collective-permute-start | bytes 245768 | tf_op jit(solution)/shard_map/ppermute | solution.py:461
  4.4 1.8 %collective-permute-start.1 = (f32[10,16,128]{2,1,0:T(8,128)S(1)}, f32[10,16,128]{2,1,0:T(8,128)S(1)}, u32[]{:S(2)}, u32[]{:S(2)}) collective-permute-start(f32[10,16,128]{2,1,0:T(8,128)S(1)} %get-tuple-element.23.own_ref), channel_id=1, source_target_pairs={{0,3},{1,2},{2,1},{3,0},{4,7},{5,6},{6,5},{7,4},{8,11},{9,10},{10,... | collective-permute-start | bytes 245768 | tf_op jit(solution)/shard_map/ppermute | solution.py:462
  6.2 0.0 collective-permute-done.near_ref
  6.2 2.7 %collective-permute-done.1.far_ref = f32[10,16,128]{2,1,0:T(8,128)S(1)} collective-permute-done((f32[10,16,128]{2,1,0:T(8,128)S(1)}, f32[10,16,128]{2,1,0:T(8,128)S(1)}, u32[]{:S(2)}, u32[]{:S(2)}) %collective-permute-start.1) | collective-permute-done | bytes 81952 | tf_op jit(solution)/shard_map/ppermute | solution.py:462
  8.9 0.4 shard_map.96
  9.3 2.5 %collective-permute-start.2 = (f32[17,24,256]{2,1,0:T(8,128)S(1)}, f32[17,24,256]{2,1,0:T(8,128)S(1)}, u32[]{:S(2)}, u32[]{:S(2)}) collective-permute-start(f32[17,24,256]{2,1,0:T(8,128)S(1)} %get-tuple-element.24), channel_id=1, source_target_pairs={{0,4},{4,0},{8,12},{12,8},{16,20},{20,16},{24,28},{28,24},{1,5},{5... | collective-permute-start | bytes 1253384 | tf_op jit(solution)/shard_map/ppermute | solution.py:469
  11.8 3.1 %collective-permute-start.3 = (f32[17,24,256]{2,1,0:T(8,128)S(1)}, f32[17,24,256]{2,1,0:T(8,128)S(1)}, u32[]{:S(2)}, u32[]{:S(2)}) collective-permute-start(f32[17,24,256]{2,1,0:T(8,128)S(1)} %get-tuple-element.25), channel_id=1, source_target_pairs={{4,8},{8,4},{12,16},{16,12},{20,24},{24,20},{5,9},{9,5},{13,17},{1... | collective-permute-start | bytes 1253384 | tf_op jit(solution)/shard_map/ppermute | solution.py:470
  14.9 6.1 %collective-permute-start.4 = (f32[2,16,256]{2,1,0:T(8,128)}, f32[2,16,256]{2,1,0:T(8,128)S(1)}, u32[]{:S(2)}, u32[]{:S(2)}) collective-permute-start(f32[2,16,256]{2,1,0:T(8,128)} %state_hbm.1), channel_id=1, source_target_pairs={{0,32},{32,0},{64,96},{96,64},{128,160},{160,128},{192,224},{224,1... | collective-permute-start | bytes 98312 | tf_op jit(solution)/shard_map/ppermute | solution.py:443
  21.0 5.7 %collective-permute-done.4.other_ref = f32[2,16,256]{2,1,0:T(8,128)S(1)} collective-permute-done((f32[2,16,256]{2,1,0:T(8,128)}, f32[2,16,256]{2,1,0:T(8,128)S(1)}, u32[]{:S(2)}, u32[]{:S(2)}) %collective-permute-start.4) | collective-permute-done | bytes 32800 | tf_op jit(solution)/shard_map/ppermute | solution.py:443
  26.7 1.4 %collective-permute-start.5 = (f32[4,16,256]{2,1,0:T(8,128)S(1)}, f32[4,16,256]{2,1,0:T(8,128)S(1)}, u32[]{:S(2)}, u32[]{:S(2)}) collective-permute-start(f32[4,16,256]{2,1,0:T(8,128)S(1)} %shard_map.99.b0_ref), channel_id=1, source_target_pairs={{0,64},{32,96},{64,0},{96,32},{128,192},{160,224},{192,128},{224,1... | collective-permute-start | bytes 196616 | tf_op jit(solution)/shard_map/ppermute | solution.py:464
  28.1 2.6 %collective-permute-start.6 = (f32[4,16,256]{2,1,0:T(8,128)S(1)}, f32[4,16,256]{2,1,0:T(8,128)S(1)}, u32[]{:S(2)}, u32[]{:S(2)}) collective-permute-start(f32[4,16,256]{2,1,0:T(8,128)S(1)} %shard_map.99.b0_ref), channel_id=1, source_target_pairs={{0,128},{32,160},{64,192},{96,224},{128,0},{160,32},{192,64},{224,... | collective-permute-start | bytes 196616 | tf_op jit(solution)/shard_map/ppermute | solution.py:464
  30.7 0.0 collective-permute-start.7
  30.7 0.0 collective-permute-done.5.b1_ref
  30.7 2.3 %collective-permute-done.6.b2_ref = f32[4,16,256]{2,1,0:T(8,128)S(1)} collective-permute-done((f32[4,16,256]{2,1,0:T(8,128)S(1)}, f32[4,16,256]{2,1,0:T(8,128)S(1)}, u32[]{:S(2)}, u32[]{:S(2)}) %collective-permute-start.6) | collective-permute-done | bytes 65568 | tf_op jit(solution)/shard_map/ppermute | solution.py:464
  33.1 2.0 %collective-permute-done.7.b3_ref = f32[4,16,256]{2,1,0:T(8,128)S(1)} collective-permute-done((f32[4,16,256]{2,1,0:T(8,128)S(1)}, f32[4,16,256]{2,1,0:T(8,128)S(1)}, u32[]{:S(2)}, u32[]{:S(2)}) %collective-permute-start.7) | collective-permute-done | bytes 65568 | tf_op jit(solution)/shard_map/ppermute | solution.py:464
  35.0 0.1 shard_map.100
  35.2 0.1 collective-permute-start.8
  35.3 1.9 %collective-permute-start.9 = (f32[1,16,128]{2,1,0:T(8,128)S(1)}, f32[1,16,128]{2,1,0:T(8,128)S(1)}, u32[]{:S(2)}, u32[]{:S(2)}) collective-permute-start(f32[1,16,128]{2,1,0:T(8,128)S(1)} %get-tuple-element.32.own_ref), channel_id=1, source_target_pairs={{0,3},{1,2},{2,1},{3,0},{4,7},{5,6},{6,5},{7,4},{8,11},{9,10},{10,... | collective-permute-start | bytes 24584 | tf_op jit(solution)/shard_map/ppermute | solution.py:473
  37.2 0.6 %collective-permute-done.8.near_ref = f32[1,16,128]{2,1,0:T(8,128)S(1)} collective-permute-done((f32[1,16,128]{2,1,0:T(8,128)S(1)}, f32[1,16,128]{2,1,0:T(8,128)S(1)}, u32[]{:S(2)}, u32[]{:S(2)}) %collective-permute-start.8) | collective-permute-done | bytes 8224 | tf_op jit(solution)/shard_map/ppermute | solution.py:472
  37.7 1.3 %collective-permute-done.9.far_ref = f32[1,16,128]{2,1,0:T(8,128)S(1)} collective-permute-done((f32[1,16,128]{2,1,0:T(8,128)S(1)}, f32[1,16,128]{2,1,0:T(8,128)S(1)}, u32[]{:S(2)}, u32[]{:S(2)}) %collective-permute-start.9) | collective-permute-done | bytes 8224 | tf_op jit(solution)/shard_map/ppermute | solution.py:473
  39.1 0.1 collective-permute-start.10
  39.2 7.3 %collective-permute-start.11 = (f32[9,8,256]{2,1,0:T(8,128)S(1)}, f32[9,8,256]{2,1,0:T(8,128)S(1)}, u32[]{:S(2)}, u32[]{:S(2)}) collective-permute-start(f32[9,8,256]{2,1,0:T(8,128)S(1)} %get-tuple-element.35), channel_id=1, source_target_pairs={{4,8},{8,4},{12,16},{16,12},{20,24},{24,20},{5,9},{9,5},{13,17},{1... | collective-permute-start | bytes 221192 | tf_op jit(solution)/shard_map/ppermute | solution.py:487
  47.1 1.2 %shard_map.98.own_ref = f32[17,80,8,128]{3,2,1,0:T(8,128)S(1)} custom-call(bf16[4,2,16,16,256]{4,3,2,1,0:T(8,128)(2,1)} %speeds_hbm.3, s32[4,16,16,256]{3,2,1,0:T(8,128)} %upwind_hbm.3, bf16[3,2,16,16,256]{4,3,2,1,0:T(8,128)(2,1)S(1)} %get-tuple-element.21.speeds_ref.early_speeds, s32[3,16,16,256]{3,2,1,0:T(8,128)S(1)} %get-tuple-element.22.upwind_ref.early_upwind, ...), custom_call_target="tpu_custom_call" | custom-call | flops 100000 | bytes 100000 | tf_op jit(solution)/shard_map/pallas_call | solution.py:441
  48.4 0.0 collective-permute-done.2.inner_ref
  48.4 0.0 collective-permute-done.3.outer_ref
  48.4 0.8 %shard_map.97 = (f32[17,30,8,128]{3,2,1,0:T(8,128)S(1)}, f32[17,8,256]{2,1,0:T(8,128)S(1)}, f32[17,8,128]{2,1,0:T(8,128)S(1)}) custom-call(s32[1]{0:T(128)S(6)} %copy.10.seed_ref, f32[16,16]{1,0:T(8,128)} %table_hbm.1, f32[17,24,256]{2,1,0:T(8,128)S(1)} %collective-permute-done.2.inner_ref, f32[17,24,256]{2,1,0:T(8,128)S(1)} %collective-permute-done.3.outer_ref, ...), custom_call_target="tpu_custom_call" | custom-call | flops 100000 | bytes 100000 | tf_op jit(solution)/shard_map/pallas_call | solution.py:441
  49.2 0.0 collective-permute-done.10.inner_ref
  49.2 0.0 collective-permute-done.11.outer_ref
  49.2 4.0 %shard_map.102 = (f32[1,16,16,256]{3,2,1,0:T(8,128)}, f32[2,16,256]{2,1,0:T(8,128)}) custom-call(f32[17,2,8,128]{3,2,1,0:T(8,128)S(1)} %get-tuple-element.19.const_ref, f32[17,8,128]{2,1,0:T(8,128)S(1)} %get-tuple-element.26.amp_ref, f32[1,16,16,256]{3,2,1,0:T(8,128)S(1)} %get-tuple-element.20.delta_ref, f32[10,16,256]{2,1,0:T(8,128)S(1)} %get-tuple-element.27.strip_ref, ...), custom_call_target="tpu_custom_call" | custom-call | flops 10000000 | bytes 10000000 | tf_op jit(solution)/shard_map/pallas_call | solution.py:441
  (2 shorter events, 0.0 us)
Async XLA Ops:
  2.3 3.9 %collective-permute-start = (f32[10,16,128]{2,1,0:T(8,128)S(1)}, f32[10,16,128]{2,1,0:T(8,128)S(1)}, u32[]{:S(2)}, u32[]{:S(2)}) collective-permute-start(f32[10,16,128]{2,1,0:T(8,128)S(1)} %get-tuple-element.23.own_ref), channel_id=1, source_target_pairs={{0,1},{1,0},{2,3},{3,2},{4,5},{5,4},{6,7},{7,6},{8,9},{9,8},{10,11... | collective-permute-start | bytes 245768 | tf_op jit(solution)/shard_map/ppermute | solution.py:461
  4.4 4.5 %collective-permute-start.1 = (f32[10,16,128]{2,1,0:T(8,128)S(1)}, f32[10,16,128]{2,1,0:T(8,128)S(1)}, u32[]{:S(2)}, u32[]{:S(2)}) collective-permute-start(f32[10,16,128]{2,1,0:T(8,128)S(1)} %get-tuple-element.23.own_ref), channel_id=1, source_target_pairs={{0,3},{1,2},{2,1},{3,0},{4,7},{5,6},{6,5},{7,4},{8,11},{9,10},{10,... | collective-permute-start | bytes 245768 | tf_op jit(solution)/shard_map/ppermute | solution.py:462
  9.3 39.1 %collective-permute-start.2 = (f32[17,24,256]{2,1,0:T(8,128)S(1)}, f32[17,24,256]{2,1,0:T(8,128)S(1)}, u32[]{:S(2)}, u32[]{:S(2)}) collective-permute-start(f32[17,24,256]{2,1,0:T(8,128)S(1)} %get-tuple-element.24), channel_id=1, source_target_pairs={{0,4},{4,0},{8,12},{12,8},{16,20},{20,16},{24,28},{28,24},{1,5},{5... | collective-permute-start | bytes 1253384 | tf_op jit(solution)/shard_map/ppermute | solution.py:469
  11.8 36.6 %collective-permute-start.3 = (f32[17,24,256]{2,1,0:T(8,128)S(1)}, f32[17,24,256]{2,1,0:T(8,128)S(1)}, u32[]{:S(2)}, u32[]{:S(2)}) collective-permute-start(f32[17,24,256]{2,1,0:T(8,128)S(1)} %get-tuple-element.25), channel_id=1, source_target_pairs={{4,8},{8,4},{12,16},{16,12},{20,24},{24,20},{5,9},{9,5},{13,17},{1... | collective-permute-start | bytes 1253384 | tf_op jit(solution)/shard_map/ppermute | solution.py:470
  14.9 11.8 %collective-permute-start.4 = (f32[2,16,256]{2,1,0:T(8,128)}, f32[2,16,256]{2,1,0:T(8,128)S(1)}, u32[]{:S(2)}, u32[]{:S(2)}) collective-permute-start(f32[2,16,256]{2,1,0:T(8,128)} %state_hbm.1), channel_id=1, source_target_pairs={{0,32},{32,0},{64,96},{96,64},{128,160},{160,128},{192,224},{224,1... | collective-permute-start | bytes 98312 | tf_op jit(solution)/shard_map/ppermute | solution.py:443
  26.7 4.0 %collective-permute-start.5 = (f32[4,16,256]{2,1,0:T(8,128)S(1)}, f32[4,16,256]{2,1,0:T(8,128)S(1)}, u32[]{:S(2)}, u32[]{:S(2)}) collective-permute-start(f32[4,16,256]{2,1,0:T(8,128)S(1)} %shard_map.99.b0_ref), channel_id=1, source_target_pairs={{0,64},{32,96},{64,0},{96,32},{128,192},{160,224},{192,128},{224,1... | collective-permute-start | bytes 196616 | tf_op jit(solution)/shard_map/ppermute | solution.py:464
  28.1 5.0 %collective-permute-start.6 = (f32[4,16,256]{2,1,0:T(8,128)S(1)}, f32[4,16,256]{2,1,0:T(8,128)S(1)}, u32[]{:S(2)}, u32[]{:S(2)}) collective-permute-start(f32[4,16,256]{2,1,0:T(8,128)S(1)} %shard_map.99.b0_ref), channel_id=1, source_target_pairs={{0,128},{32,160},{64,192},{96,224},{128,0},{160,32},{192,64},{224,... | collective-permute-start | bytes 196616 | tf_op jit(solution)/shard_map/ppermute | solution.py:464
  30.7 4.3 %collective-permute-start.7 = (f32[4,16,256]{2,1,0:T(8,128)S(1)}, f32[4,16,256]{2,1,0:T(8,128)S(1)}, u32[]{:S(2)}, u32[]{:S(2)}) collective-permute-start(f32[4,16,256]{2,1,0:T(8,128)S(1)} %shard_map.99.b0_ref), channel_id=1, source_target_pairs={{0,192},{32,224},{64,128},{96,160},{128,64},{160,96},{192,0},{224,... | collective-permute-start | bytes 196616 | tf_op jit(solution)/shard_map/ppermute | solution.py:464
  35.2 2.6 %collective-permute-start.8 = (f32[1,16,128]{2,1,0:T(8,128)S(1)}, f32[1,16,128]{2,1,0:T(8,128)S(1)}, u32[]{:S(2)}, u32[]{:S(2)}) collective-permute-start(f32[1,16,128]{2,1,0:T(8,128)S(1)} %get-tuple-element.32.own_ref), channel_id=1, source_target_pairs={{0,1},{1,0},{2,3},{3,2},{4,5},{5,4},{6,7},{7,6},{8,9},{9,8},{10,11... | collective-permute-start | bytes 24584 | tf_op jit(solution)/shard_map/ppermute | solution.py:472
  35.3 3.8 %collective-permute-start.9 = (f32[1,16,128]{2,1,0:T(8,128)S(1)}, f32[1,16,128]{2,1,0:T(8,128)S(1)}, u32[]{:S(2)}, u32[]{:S(2)}) collective-permute-start(f32[1,16,128]{2,1,0:T(8,128)S(1)} %get-tuple-element.32.own_ref), channel_id=1, source_target_pairs={{0,3},{1,2},{2,1},{3,0},{4,7},{5,6},{6,5},{7,4},{8,11},{9,10},{10,... | collective-permute-start | bytes 24584 | tf_op jit(solution)/shard_map/ppermute | solution.py:473
  39.1 10.1 %collective-permute-start.10 = (f32[9,8,256]{2,1,0:T(8,128)S(1)}, f32[9,8,256]{2,1,0:T(8,128)S(1)}, u32[]{:S(2)}, u32[]{:S(2)}) collective-permute-start(f32[9,8,256]{2,1,0:T(8,128)S(1)} %get-tuple-element.34), channel_id=1, source_target_pairs={{0,4},{4,0},{8,12},{12,8},{16,20},{20,16},{24,28},{28,24},{1,5},{5... | collective-permute-start | bytes 221192 | tf_op jit(solution)/shard_map/ppermute | solution.py:486
  39.2 10.0 %collective-permute-start.11 = (f32[9,8,256]{2,1,0:T(8,128)S(1)}, f32[9,8,256]{2,1,0:T(8,128)S(1)}, u32[]{:S(2)}, u32[]{:S(2)}) collective-permute-start(f32[9,8,256]{2,1,0:T(8,128)S(1)} %get-tuple-element.35), channel_id=1, source_target_pairs={{4,8},{8,4},{12,16},{16,12},{20,24},{24,20},{5,9},{9,5},{13,17},{1... | collective-permute-start | bytes 221192 | tf_op jit(solution)/shard_map/ppermute | solution.py:487
